TPU v7x, 32 devices: a whole 2x2x4 slice. The times are simulated.
32 devices in a mesh: section: 2 (over x), seq: 16 (over z, y, core).
Axes of the slice: x: 2, y: 2, z: 4, core: 2. Of those that a mesh axis runs over, the one named last changes fastest.
Arguments:
- prev_out: bfloat16 [2, 2048, 1792], P('section', 'seq'), may hold values from -6 to 6
- prev_grad: bfloat16 [2, 2048, 1792], P('section', 'seq'), may hold values from -6 to 6
- saved_in: bfloat16 [2, 2048, 1792], P('section', 'seq'), may hold values from -6 to 6
- seq_mix: bfloat16 [2, 128, 128], P('section'), may hold values from -0.5 to 0.5
- coeffs: float32 [2, 4, 4, 1792], P('section'), may hold values from -1 to 1
- mixer: bfloat16 [2, 1792, 448], P('section'), may hold values from -0.25 to 0.25
Outputs:
- out_fwd: bfloat16 [2, 2048, 1792], P('section', 'seq')
- out_dh: bfloat16 [2, 2048, 1792], P('section', 'seq')
- grad_w: float32 [2, 1792, 448], P('section', 'seq')
- grad_b: float32 [2, 128, 128], P('section')
All inputs are finite; a program needn't handle non-finite values.
Results may differ from a plain program's by a relative error of at most 0.01.
Values may be sent and summed in bfloat16 or wider, within the bound.
No kernel may reach another device: no remote copies, remote signals or barrier semaphores. Data moves between devices by JAX's collectives and lax.ppermute only.
A program may use at most 64 MiB of HBM per device.

v0:
```python
import jax
import jax.numpy as jnp
from jax import lax
from jax.sharding import PartitionSpec as P


def swapped(block, axis, stride):
    count = lax.axis_size(axis)
    route = []
    for low in range(count):
        high = low | 1 << stride
        if high != low and high < count:
            route += [(low, high), (high, low)]
    return lax.ppermute(block, axis, route)


def from_behind(block, axis, distance):
    devices = range(lax.axis_size(axis))
    route = [((i - distance) % len(devices), i) for i in devices]
    return lax.ppermute(block, axis, route)


def mix_forward(state, factors):
    position = lax.axis_index("seq")
    number = lax.axis_size("seq").bit_length() - 1
    for bit_level in range(number):
        partner = swapped(state, "seq", bit_level)
        upper_side = jnp.bitwise_and(jnp.right_shift(position, bit_level), 1) == 1
        own_vals = state.astype(jnp.float32)
        partner_vals = partner.astype(jnp.float32)
        as_lower = factors[bit_level, 0] * own_vals + factors[bit_level, 1] * partner_vals
        as_upper = factors[bit_level, 2] * partner_vals + factors[bit_level, 3] * own_vals
        state = jnp.where(upper_side, as_upper, as_lower).astype(jnp.bfloat16)
    return state


def mix_adjoint(state, factors):
    position = lax.axis_index("seq")
    number = lax.axis_size("seq").bit_length() - 1
    for bit_level in reversed(range(number)):
        partner = swapped(state, "seq", bit_level)
        upper_side = jnp.bitwise_and(jnp.right_shift(position, bit_level), 1) == 1
        own_vals = state.astype(jnp.float32)
        partner_vals = partner.astype(jnp.float32)
        as_lower = factors[bit_level, 0] * own_vals + factors[bit_level, 2] * partner_vals
        as_upper = factors[bit_level, 1] * partner_vals + factors[bit_level, 3] * own_vals
        state = jnp.where(upper_side, as_upper, as_lower).astype(jnp.bfloat16)
    return state


def block_apply(rows, blocks):
    block_len = blocks.shape[0]
    shaped = rows.reshape(-1, block_len, rows.shape[1])
    mixed = jnp.einsum("ij,bjd->bid", blocks, shaped, preferred_element_type=jnp.float32)
    return mixed.reshape(rows.shape).astype(jnp.bfloat16)


def layer_forward(rows, blocks, factors, weights):
    width = rows.shape[1]
    block_width = weights.shape[1]
    nblocks = width // block_width
    blocked = block_apply(rows, blocks)
    state = mix_forward(blocked, factors)
    act = (rows.astype(jnp.float32) + state.astype(jnp.float32)).astype(jnp.bfloat16)
    act3 = act.reshape(-1, nblocks, block_width)
    weight3 = weights.reshape(nblocks, block_width, block_width)
    pre = jnp.einsum("tbi,bio->tbo", act3, weight3, preferred_element_type=jnp.float32)
    return (act3, pre)


def on_device(prev_out, prev_grad, saved_in, seq_mix, coeffs, mixer):
    incoming = from_behind(prev_out, "section", 1)[0]
    upstream = from_behind(prev_grad, "section", -1)[0]
    blocks = seq_mix[0]
    factors = coeffs[0]
    weights = mixer[0]
    rows_dev, width = incoming.shape
    block_width = weights.shape[1]
    nblocks = width // block_width
    block_len = blocks.shape[0]
    act3, pre = layer_forward(incoming, blocks, factors, weights)
    result = (
        (act3.astype(jnp.float32) + jax.nn.silu(pre)).reshape(rows_dev, width).astype(jnp.bfloat16)
    )
    stored = saved_in[0]
    act_two, pre_two = layer_forward(stored, blocks, factors, weights)
    sigma = jax.nn.sigmoid(pre_two)
    gz = (
        upstream.astype(jnp.float32).reshape(-1, nblocks, block_width)
        * (sigma * (1.0 + pre_two * (1.0 - sigma)))
    ).astype(jnp.bfloat16)
    weight3 = weights.reshape(nblocks, block_width, block_width)
    back = jnp.einsum("tbo,bio->tbi", gz, weight3, preferred_element_type=jnp.float32)
    d_act = (upstream.astype(jnp.float32) + back.reshape(rows_dev, width)).astype(jnp.bfloat16)
    weight_term = jnp.einsum(
        "tbi,tbo->bio", act_two, gz, preferred_element_type=jnp.float32
    ).reshape(width, block_width)
    grad_weight = lax.psum_scatter(weight_term, "seq", scatter_dimension=0, tiled=True)
    dblocked = mix_adjoint(d_act, factors)
    dblk = dblocked.reshape(-1, block_len, width)
    stored_blk = stored.reshape(-1, block_len, width)
    block_term = jnp.einsum("bid,bjd->ij", dblk, stored_blk, preferred_element_type=jnp.float32)
    grad_block = lax.psum(block_term, "seq")
    through = jnp.einsum("ij,bid->bjd", blocks, dblk, preferred_element_type=jnp.float32).reshape(
        rows_dev, width
    )
    in_grad = (d_act.astype(jnp.float32) + through).astype(jnp.bfloat16)
    return (result[None], in_grad[None], grad_weight[None], grad_block[None])


def solution(mesh):
    placed = (
        P("section", "seq", None),
        P("section", "seq", None),
        P("section", "seq", None),
        P("section", None, None),
        P("section", None, None, None),
        P("section", None, None),
    )
    return jax.shard_map(
        on_device,
        mesh=mesh,
        in_specs=placed,
        out_specs=(
            P("section", "seq", None),
            P("section", "seq", None),
            P("section", "seq", None),
            P("section", None, None),
        ),
        check_vma=False,
    )
```

profile of v0, /device:TPU:0, one launch (start us, length us, event | category | flops | bytes accessed | tf_op | source)
XLA Modules:
  0.0 301.7 jit_solution(15228928650524788524)
XLA Ops:
  12.6 3.0 collective-permute-start.7
  15.5 10.8 %collective-permute-done.7 = bf16[128,1792]{0,1:T(8,128)(2,1)S(1)} collective-permute-done((bf16[128,1792]{0,1:T(8,128)(2,1)S(1)}, bf16[128,1792]{0,1:T(8,128)(2,1)S(1)}, u32[]{:S(2)}, u32[]{:S(2)}) %collective-permute-start.7) | collective-permute-done | bytes 458784 | tf_op jit(solution)/shard_map/ppermute | solution.py:14
  27.7 1.9 collective-permute-start.8
  29.6 10.3 %collective-permute-done.8 = bf16[128,1792]{0,1:T(8,128)(2,1)S(1)} collective-permute-done((bf16[128,1792]{0,1:T(8,128)(2,1)S(1)}, bf16[128,1792]{0,1:T(8,128)(2,1)S(1)}, u32[]{:S(2)}, u32[]{:S(2)}) %collective-permute-start.8) | collective-permute-done | bytes 458784 | tf_op jit(solution)/shard_map/ppermute | solution.py:14
  41.2 2.6 collective-permute-start.9
  47.2 2.8 copy.18
  50.0 13.3 %collective-permute-done.9 = bf16[128,1792]{0,1:T(8,128)(2,1)} collective-permute-done((bf16[128,1792]{0,1:T(8,128)(2,1)S(1)}, bf16[128,1792]{0,1:T(8,128)(2,1)}, u32[]{:S(2)}, u32[]{:S(2)}) %collective-permute-start.9) | collective-permute-done | bytes 458784 | tf_op jit(solution)/shard_map/ppermute | solution.py:14
  63.2 3.0 add_convert_fusion.1
  69.1 22.5 %collective-permute-done.10 = bf16[128,1792]{0,1:T(8,128)(2,1)S(1)} collective-permute-done((bf16[128,1792]{0,1:T(8,128)(2,1)S(1)}, bf16[128,1792]{0,1:T(8,128)(2,1)S(1)}, u32[]{:S(2)}, u32[]{:S(2)}) %collective-permute-start.10) | collective-permute-done | bytes 458784 | tf_op jit(solution)/shard_map/ppermute | solution.py:14
  91.6 2.2 fusion.36
  93.8 2.0 copy.10
  96.4 9.0 %collective-permute-done.11 = bf16[128,1792]{0,1:T(8,128)(2,1)} collective-permute-done((bf16[128,1792]{0,1:T(8,128)(2,1)}, bf16[128,1792]{0,1:T(8,128)(2,1)}, u32[]{:S(2)}, u32[]{:S(2)}) %collective-permute-start.11) | collective-permute-done | bytes 458784 | tf_op jit(solution)/shard_map/ppermute | solution.py:14
  105.5 2.9 fusion.40
  108.8 10.0 %collective-permute-done.12 = bf16[128,1792]{0,1:T(8,128)(2,1)S(1)} collective-permute-done((bf16[128,1792]{0,1:T(8,128)(2,1)S(1)}, bf16[128,1792]{0,1:T(8,128)(2,1)S(1)}, u32[]{:S(2)}, u32[]{:S(2)}) %collective-permute-start.12) | collective-permute-done | bytes 458784 | tf_op jit(solution)/shard_map/ppermute | solution.py:14
  122.0 2.2 fusion.48
  126.3 3.7 %fusion.58 = f32[4,448,448]{2,1,0:T(8,128)} fusion(bf16[128,4,448]{0,2,1:T(8,128)(2,1)S(1)} %bitcast.83, f32[128,4,448]{0,2,1:T(8,128)} %copy-done.6, bf16[128,4,448]{0,2,1:T(8,128)(2,1)S(1)} %bitcast.81), kind=kOutput, calls=%fused_computation.135 | convolution fusion | flops 207814656 | bytes 5046272 | tf_op jit(solution)/shard_map/tbi,tbo->bio/dot_general | solution.py:95
  131.3 12.5 %collective-permute-done.2 = bf16[128,1792]{0,1:T(8,128)(2,1)S(1)} collective-permute-done((bf16[128,1792]{0,1:T(8,128)(2,1)S(1)}, bf16[128,1792]{0,1:T(8,128)(2,1)S(1)}, u32[]{:S(2)}, u32[]{:S(2)}) %collective-permute-start.2) | collective-permute-done | bytes 458784 | tf_op jit(solution)/shard_map/ppermute | solution.py:14
  146.0 11.1 %collective-permute-done.3 = bf16[128,1792]{0,1:T(8,128)(2,1)S(1)} collective-permute-done((bf16[128,1792]{0,1:T(8,128)(2,1)S(1)}, bf16[128,1792]{0,1:T(8,128)(2,1)S(1)}, u32[]{:S(2)}, u32[]{:S(2)}) %collective-permute-start.3) | collective-permute-done | bytes 458784 | tf_op jit(solution)/shard_map/ppermute | solution.py:14
  157.1 2.2 fusion.12
  159.3 2.6 collective-permute-start.4
  163.1 18.6 %collective-permute-done.4 = bf16[128,1792]{0,1:T(8,128)(2,1)} collective-permute-done((bf16[128,1792]{0,1:T(8,128)(2,1)}, bf16[128,1792]{0,1:T(8,128)(2,1)}, u32[]{:S(2)}, u32[]{:S(2)}) %collective-permute-start.4) | collective-permute-done | bytes 458784 | tf_op jit(solution)/shard_map/ppermute | solution.py:14
  181.7 2.9 add_convert_fusion.3
  186.4 31.9 %all-reduce.2.cloned.1.call-done = f32[1,128,128]{2,1,0:T(8,128)} async-done(((f32[1,128,128]{2,1,0:T(8,128)}), f32[1,128,128]{2,1,0:T(8,128)}) %all-reduce.2.cloned.1.call-update) | async-done | bytes 65552 | tf_op jit(solution)/shard_map/psum | solution.py:103
  218.3 75.1 %reduce-scatter.2.cloned.1.call-done = f32[112,448]{1,0:T(8,128)} async-done(((f32[1792,448]{1,0:T(8,128)}), f32[112,448]{1,0:T(8,128)}) %reduce-scatter.2.cloned.1.call-update) | async-done | bytes 200720 | tf_op jit(solution)/shard_map/reduce_scatter | solution.py:98
  (63 shorter events, 28.5 us)
Async XLA Ops:
  7.2 211.1 %all-reduce.2.cloned.1.call-start = ((), (), s32[]{:S(2)}) async-start(), calls=%async_computation.2 | async-start | bytes 131072 | tf_op jit(solution)/shard_map/psum | solution.py:103
  9.3 2.0 collective-permute-start.6
  11.2 32.5 %copy-start.11 = (bf16[1,128,1792]{2,1,0:T(8,128)(2,1)S(1)}, bf16[1,128,1792]{2,1,0:T(8,128)(2,1)}, u32[]{:S(2)}) copy-start(bf16[1,128,1792]{2,1,0:T(8,128)(2,1)} %param.7) | copy-start | bytes 1376260
  12.6 13.8 %collective-permute-start.7 = (bf16[128,1792]{0,1:T(8,128)(2,1)S(1)}, bf16[128,1792]{0,1:T(8,128)(2,1)S(1)}, u32[]{:S(2)}, u32[]{:S(2)}) collective-permute-start(bf16[128,1792]{0,1:T(8,128)(2,1)S(1)} %fusion.20), channel_id=1, source_target_pairs={{0,2},{2,0},{1,3},{3,1},{4,6},{6,4},{5,7},{7,5},{8,10},{10,8},{9,1... | collective-permute-start | bytes 1376264 | tf_op jit(solution)/shard_map/ppermute | solution.py:14
  26.3 19.9 %copy-start.1 = (bf16[1,128,1792]{2,1,0:T(8,128)(2,1)S(1)}, bf16[1,128,1792]{2,1,0:T(8,128)(2,1)}, u32[]{:S(2)}) copy-start(bf16[1,128,1792]{2,1,0:T(8,128)(2,1)} %param.8) | copy-start | bytes 1376260
  27.7 12.1 %collective-permute-start.8 = (bf16[128,1792]{0,1:T(8,128)(2,1)S(1)}, bf16[128,1792]{0,1:T(8,128)(2,1)S(1)}, u32[]{:S(2)}, u32[]{:S(2)}) collective-permute-start(bf16[128,1792]{0,1:T(8,128)(2,1)S(1)} %fusion.24), channel_id=1, source_target_pairs={{0,4},{4,0},{1,5},{5,1},{2,6},{6,2},{3,7},{7,3},{8,12},{12,8},{9,1... | collective-permute-start | bytes 1376264 | tf_op jit(solution)/shard_map/ppermute | solution.py:14
  41.2 8.8 %copy-start.10 = (bf16[128,1792]{0,1:T(8,128)(2,1)}, bf16[128,1792]{0,1:T(8,128)(2,1)S(1)}, u32[]{:S(2)}) copy-start(bf16[128,1792]{0,1:T(8,128)(2,1)S(1)} %fusion.28) | copy-start | bytes 1376260
  41.2 22.1 %collective-permute-start.9 = (bf16[128,1792]{0,1:T(8,128)(2,1)S(1)}, bf16[128,1792]{0,1:T(8,128)(2,1)}, u32[]{:S(2)}, u32[]{:S(2)}) collective-permute-start(bf16[128,1792]{0,1:T(8,128)(2,1)S(1)} %fusion.28), channel_id=1, source_target_pairs={{0,8},{8,0},{1,9},{9,1},{2,10},{10,2},{3,11},{11,3},{4,12},{12,4},... | collective-permute-start | bytes 1376264 | tf_op jit(solution)/shard_map/ppermute | solution.py:14
  44.7 22.4 %collective-permute-start.5 = (bf16[1,128,1792]{1,2,0:T(8,128)(2,1)}, bf16[1,128,1792]{1,2,0:T(8,128)(2,1)S(1)}, u32[]{:S(2)}, u32[]{:S(2)}) collective-permute-start(bf16[1,128,1792]{1,2,0:T(8,128)(2,1)} %copy.12), channel_id=1, source_target_pairs={{16,0},{0,16},{17,1},{1,17},{18,2},{2,18},{19,3},{3,19},{20,4},{4,... | collective-permute-start | bytes 1376264 | tf_op jit(solution)/shard_map/ppermute | solution.py:20
  69.0 22.6 %collective-permute-start.10 = (bf16[128,1792]{0,1:T(8,128)(2,1)S(1)}, bf16[128,1792]{0,1:T(8,128)(2,1)S(1)}, u32[]{:S(2)}, u32[]{:S(2)}) collective-permute-start(bf16[128,1792]{0,1:T(8,128)(2,1)S(1)} %fusion.50), channel_id=1, source_target_pairs={{0,8},{8,0},{1,9},{9,1},{2,10},{10,2},{3,11},{11,3},{4,12},{12,4},... | collective-permute-start | bytes 1376264 | tf_op jit(solution)/shard_map/ppermute | solution.py:14
  93.8 11.6 %collective-permute-start.11 = (bf16[128,1792]{0,1:T(8,128)(2,1)}, bf16[128,1792]{0,1:T(8,128)(2,1)}, u32[]{:S(2)}, u32[]{:S(2)}) collective-permute-start(bf16[128,1792]{0,1:T(8,128)(2,1)} %fusion.36), channel_id=1, source_target_pairs={{0,4},{4,0},{1,5},{5,1},{2,6},{6,2},{3,7},{7,3},{8,12},{12,8},{9,1... | collective-permute-start | bytes 1376264 | tf_op jit(solution)/shard_map/ppermute | solution.py:14
  95.8 12.6 %collective-permute-start = (bf16[1,128,1792]{1,2,0:T(8,128)(2,1)}, bf16[1,128,1792]{1,2,0:T(8,128)(2,1)S(1)}, u32[]{:S(2)}, u32[]{:S(2)}) collective-permute-start(bf16[1,128,1792]{1,2,0:T(8,128)(2,1)} %copy.10), channel_id=1, source_target_pairs={{16,0},{0,16},{17,1},{1,17},{18,2},{2,18},{19,3},{3,19},{20,4},{4,... | collective-permute-start | bytes 1376264 | tf_op jit(solution)/shard_map/ppermute | solution.py:20
  108.3 10.5 %collective-permute-start.12 = (bf16[128,1792]{0,1:T(8,128)(2,1)S(1)}, bf16[128,1792]{0,1:T(8,128)(2,1)S(1)}, u32[]{:S(2)}, u32[]{:S(2)}) collective-permute-start(bf16[128,1792]{0,1:T(8,128)(2,1)S(1)} %fusion.40), channel_id=1, source_target_pairs={{0,2},{2,0},{1,3},{3,1},{4,6},{6,4},{5,7},{7,5},{8,10},{10,8},{9,1... | collective-permute-start | bytes 1376264 | tf_op jit(solution)/shard_map/ppermute | solution.py:14
  108.4 11.8 %copy-start.7 = (bf16[1,128,1792]{1,2,0:T(8,128)(2,1)}, bf16[1,128,1792]{1,2,0:T(8,128)(2,1)S(1)}, u32[]{:S(2)}) copy-start(bf16[1,128,1792]{1,2,0:T(8,128)(2,1)S(1)} %collective-permute-done) | copy-start | bytes 1376260
  108.7 11.5 %collective-permute-start.1 = (bf16[128,1792]{0,1:T(8,128)(2,1)S(1)}, bf16[128,1792]{0,1:T(8,128)(2,1)S(1)}, u32[]{:S(2)}, u32[]{:S(2)}) collective-permute-start(bf16[128,1792]{0,1:T(8,128)(2,1)S(1)} %fusion), channel_id=1, source_target_pairs={{0,1},{1,0},{2,3},{3,2},{4,5},{5,4},{6,7},{7,6},{8,9},{9,8},{10,11... | collective-permute-start | bytes 1376264 | tf_op jit(solution)/shard_map/ppermute | solution.py:14
  120.2 1.9 collective-permute-start.13
  126.0 167.3 %reduce-scatter.2.cloned.1.call-start = ((), (), s32[]{:S(2)}) async-start(), calls=%async_computation.1 | async-start | bytes 3899392 | tf_op jit(solution)/shard_map/reduce_scatter | solution.py:98
  129.9 1.0 copy-start.9
  129.9 15.8 %copy-start.3 = (bf16[128,1792]{0,1:T(8,128)(2,1)S(1)}, bf16[128,1792]{0,1:T(8,128)(2,1)}, u32[]{:S(2)}) copy-start(bf16[128,1792]{0,1:T(8,128)(2,1)} %copy-done.2) | copy-start | bytes 1376260
  131.0 31.0 %copy-start.5 = (f32[4,128,448]{1,2,0:T(8,128)S(1)}, f32[4,128,448]{1,2,0:T(8,128)}, u32[]{:S(2)}) copy-start(f32[4,128,448]{1,2,0:T(8,128)} %copy-done.4) | copy-start | bytes 2752516
  131.0 12.8 %collective-permute-start.2 = (bf16[128,1792]{0,1:T(8,128)(2,1)S(1)}, bf16[128,1792]{0,1:T(8,128)(2,1)S(1)}, u32[]{:S(2)}, u32[]{:S(2)}) collective-permute-start(bf16[128,1792]{0,1:T(8,128)(2,1)S(1)} %copy-done.9), channel_id=1, source_target_pairs={{0,2},{2,0},{1,3},{3,1},{4,6},{6,4},{5,7},{7,5},{8,10},{10,8},{9,1... | collective-permute-start | bytes 1376264 | tf_op jit(solution)/shard_map/ppermute | solution.py:14
  145.1 12.0 %collective-permute-start.3 = (bf16[128,1792]{0,1:T(8,128)(2,1)S(1)}, bf16[128,1792]{0,1:T(8,128)(2,1)S(1)}, u32[]{:S(2)}, u32[]{:S(2)}) collective-permute-start(bf16[128,1792]{0,1:T(8,128)(2,1)S(1)} %fusion.8), channel_id=1, source_target_pairs={{0,4},{4,0},{1,5},{5,1},{2,6},{6,2},{3,7},{7,3},{8,12},{12,8},{9,1... | collective-permute-start | bytes 1376264 | tf_op jit(solution)/shard_map/ppermute | solution.py:14
  159.3 22.3 %collective-permute-start.4 = (bf16[128,1792]{0,1:T(8,128)(2,1)}, bf16[128,1792]{0,1:T(8,128)(2,1)}, u32[]{:S(2)}, u32[]{:S(2)}) collective-permute-start(bf16[128,1792]{0,1:T(8,128)(2,1)} %fusion.12), channel_id=1, source_target_pairs={{0,8},{8,0},{1,9},{9,1},{2,10},{10,2},{3,11},{11,3},{4,12},{12,4},... | collective-permute-start | bytes 1376264 | tf_op jit(solution)/shard_map/ppermute | solution.py:14
  161.9 19.7 %copy-start.8 = (bf16[1,128,1792]{1,2,0:T(8,128)(2,1)S(1)}, bf16[1,128,1792]{1,2,0:T(8,128)(2,1)}, u32[]{:S(2)}) copy-start(bf16[1,128,1792]{1,2,0:T(8,128)(2,1)} %copy-done.7) | copy-start | bytes 1376260
  (4 other events, 3.4 us)
Sparse Core Ops, SparseCore 0:
  126.2 92.0 all-reduce.1
  223.2 70.1 reduce-scatter.1
where the time goes:
time: 302 us
  waiting for transfers between devices  227 us (75%)
  other arithmetic  22.3 us (7%)
  local copies, waits for them, and re-layouts  15.1 us (5%)
  between operations  14.3 us (5%)
  starting transfers between devices  14.1 us (5%)
  matrix products  8.92 us (3%)
    ppermute x12, waiting for transfers between devices, swapped(): return lax.ppermute(block, axis, route)  120 us
    reduce_scatter x1, waiting for transfers between devices, on_device(): lax.psum_scatter(weight_term, 'seq', scatter_dimension=0, tiled=True)  75.1 us
    psum x1, waiting for transfers between devices, on_device(): grad_block = lax.psum(block_term, 'seq')  31.9 us
    ppermute x12, starting transfers between devices, swapped(): return lax.ppermute(block, axis, route)  11.7 us
    unnamed x30, local copies, waits for them, and re-layouts  11 us
    convert_element_type x4, other arithmetic, mix_adjoint(): state = jnp.where(upper_side, as_upper, as_lower).astype(jnp.bfloat16)  8.65 us
    convert_element_type x5, other arithmetic, mix_forward(): state = jnp.where(upper_side, as_upper, as_lower).astype(jnp.bfloat16)  7.57 us
  transfers between devices with their start and end apart: 16, of which 13 were waited for; matrix products, arithmetic and copies ran while one was open for 10% of the time, Pallas kernels for 0%

commit v1 on v0

v1 whole, which is shorter than its diff:
```python
import functools

import jax
import jax.numpy as jnp
from jax import lax
from jax.experimental import pallas as pl
from jax.experimental.pallas import tpu as pltpu
from jax.sharding import PartitionSpec as P

F32 = jnp.float32
BF16 = jnp.bfloat16
VMEM = pl.BlockSpec(memory_space=pltpu.VMEM)
SMEM = pl.BlockSpec(memory_space=pltpu.SMEM)


def dot(a, b, ca, cb):
    return lax.dot_general(a, b, (((ca,), (cb,)), ((), ())), preferred_element_type=F32)


def call(body, outs, ins, scratch=(), name=None):
    return pl.pallas_call(
        body,
        out_shape=outs,
        in_specs=[SMEM if a.dtype == jnp.int32 else VMEM for a in ins],
        out_specs=jax.tree.map(lambda _: VMEM, outs),
        scratch_shapes=scratch,
        name=name,
    )(*ins)


def pack_body(nb, z_ref, x_ref, *refs):
    outs, buf = refs[:nb], refs[nb]
    rows, width = x_ref.shape
    bw = width // nb
    for j in range(width // 128):
        buf[j * 128 : (j + 1) * 128, :] = x_ref[:, j * 128 : (j + 1) * 128].T
    z = z_ref[0]
    for k in range(nb):
        start = pl.multiple_of(jnp.bitwise_xor(z, k) * bw, 16)
        outs[k][...] = buf[pl.ds(start, bw), :]


def pack(z, x, nb, name):
    rows, width = x.shape
    bw = width // nb
    return call(
        functools.partial(pack_body, nb),
        [jax.ShapeDtypeStruct((bw, rows), x.dtype)] * nb,
        [z, x],
        [pltpu.VMEM((width, rows), x.dtype)],
        name,
    )


def unpack_body(nb, z_ref, *refs):
    ins, out, buf = refs[:nb], refs[nb], refs[nb + 1]
    rows, width = out.shape
    bw = width // nb
    z = z_ref[0]
    for k in range(nb):
        start = pl.multiple_of(jnp.bitwise_xor(z, k) * bw, 16)
        buf[pl.ds(start, bw), :] = ins[k][...]
    for j in range(width // 128):
        out[:, j * 128 : (j + 1) * 128] = buf[j * 128 : (j + 1) * 128, :].T


def unpack(z, pieces, name):
    nb = len(pieces)
    bw, rows = pieces[0].shape
    return call(
        functools.partial(unpack_body, nb),
        jax.ShapeDtypeStruct((rows, nb * bw), pieces[0].dtype),
        [z, *pieces],
        [pltpu.VMEM((nb * bw, rows), pieces[0].dtype)],
        name,
    )


def local_levels(vals, coef, first):
    vals = list(vals)
    nb = len(vals)
    for j in range(nb.bit_length() - 1):
        c = [coef[:, first + 4 * j + i : first + 4 * j + i + 1] for i in range(4)]
        for k in range(nb):
            if not k >> j & 1:
                m = k | 1 << j
                a, b = vals[k], vals[m]
                vals[k] = c[0] * a + c[1] * b
                vals[m] = c[2] * b + c[3] * a
    return vals


CH = 64


def local_body(nb, first, coef_ref, *refs):
    ins, out = refs[:nb], refs[nb]
    for s in range(0, out.shape[1], CH):
        vals = [r[s : s + CH, :].astype(F32) for r in ins]
        vals = local_levels(vals, coef_ref[s : s + CH, :], first)
        for k in range(nb):
            out[k, s : s + CH, :] = vals[k].astype(BF16)


def combine_body(first, coef_ref, own_ref, other_ref, out_ref):
    for s in range(0, out_ref.shape[1], CH):
        c0 = coef_ref[s : s + CH, first : first + 1]
        c1 = coef_ref[s : s + CH, first + 1 : first + 2]
        for k in range(out_ref.shape[0]):
            out_ref[k, s : s + CH, :] = (
                c0 * own_ref[k, s : s + CH, :].astype(F32) + c1 * other_ref[k, s : s + CH, :].astype(F32)
            ).astype(BF16)


def combine(coef, first, own, other, name):
    return call(
        functools.partial(combine_body, first),
        jax.ShapeDtypeStruct(own.shape, BF16),
        [coef, own, other],
        (),
        name,
    )


def forward_body(nb, first, coef_ref, b_ref, wt_ref, own_ref, other_ref, *refs):
    ins, outs = refs[:nb], refs[nb : 2 * nb]
    c0 = coef_ref[:, first : first + 1]
    c1 = coef_ref[:, first + 1 : first + 2]
    for k in range(nb):
        u = (c0 * own_ref[k].astype(F32) + c1 * other_ref[k].astype(F32)).astype(BF16)
        act = (ins[k][...].astype(F32) + dot(u, b_ref[...], 1, 1)).astype(BF16)
        pre = dot(wt_ref[...], act, 1, 0)
        outs[k][...] = (act.astype(F32) + pre * jax.nn.sigmoid(pre)).astype(BF16)


def backward_body(nb, first, first_adj, coef_ref, b_ref, w_ref, wt_ref, own_ref, other_ref, *refs):
    ins, ups = refs[:nb], refs[nb : 2 * nb]
    v_ref, d_ref, act_ref, gz_ref, u_ref = refs[2 * nb :]
    c0 = coef_ref[:, first : first + 1]
    c1 = coef_ref[:, first + 1 : first + 2]
    vs = []
    for k in range(nb):
        u = (c0 * own_ref[k].astype(F32) + c1 * other_ref[k].astype(F32)).astype(BF16)
        u_ref[k] = u
        act = (ins[k][...].astype(F32) + dot(u, b_ref[...], 1, 1)).astype(BF16)
        act_ref[k] = act
        pre = dot(wt_ref[...], act, 1, 0)
        sig = jax.nn.sigmoid(pre)
        up = ups[k][...].astype(F32)
        gz = (up * (sig * (1.0 + pre * (1.0 - sig)))).astype(BF16)
        gz_ref[k] = gz
        d = (up + dot(w_ref[...], gz, 1, 0)).astype(BF16)
        d_ref[k] = d
        vs.append(dot(d, b_ref[...], 1, 0))
    vs = local_levels(vs, coef_ref[...], first_adj)
    for k in range(nb):
        v_ref[k] = vs[k].astype(BF16)


def grads_body(nb, act_ref, gz_ref, d_ref, u_ref, gw_ref, gb_ref):
    gw, gb = 0.0, 0.0
    for k in range(nb):
        gw = gw + dot(act_ref[k], gz_ref[k], 1, 1)
        gb = gb + dot(d_ref[k], u_ref[k], 0, 0)
    gw_ref[...] = gw
    gb_ref[...] = gb


def finish_body(nb, first, coef_ref, own_ref, other_ref, d_ref, *outs):
    for s in range(0, own_ref.shape[1], CH):
        c0 = coef_ref[s : s + CH, first : first + 1]
        c1 = coef_ref[s : s + CH, first + 1 : first + 2]
        for k in range(nb):
            outs[k][s : s + CH, :] = (
                d_ref[k, s : s + CH, :].astype(F32)
                + c0 * own_ref[k, s : s + CH, :].astype(F32)
                + c1 * other_ref[k, s : s + CH, :].astype(F32)
            ).astype(BF16)


def on_device(prev_out, prev_grad, saved_in, seq_mix, coeffs, mixer):
    n_sec, n_seq = lax.axis_size("section"), lax.axis_size("seq")
    weights = mixer[0]
    width, bw = weights.shape
    nb = width // bw
    low = n_seq // nb
    levels = n_seq.bit_length() - 1
    n_low = low.bit_length() - 1
    q = lax.axis_index("seq")
    col = q // low
    z = col.astype(jnp.int32).reshape(1)
    blocks = seq_mix[0]
    rows = prev_out.shape[1]

    def send(x, shift, flip):
        pairs = [
            (s * n_seq + i, (s + shift) % n_sec * n_seq + (i ^ flip)) for s in range(n_sec) for i in range(n_seq)
        ]
        return lax.ppermute(x, ("section", "seq"), pairs)

    cf = lax.dynamic_slice_in_dim(coeffs[0], col * bw, bw, 2)
    bits = [jnp.bitwise_and(jnp.right_shift(q, l), 1) == 1 for l in range(levels)]

    def table(order_lower, order_upper, l):
        return jnp.where(bits[l], cf[l, jnp.array(order_upper)], cf[l, jnp.array(order_lower)])

    cols = []
    for l in range(n_low, levels):
        cols.append(table([0, 1, 3, 2], [3, 2, 0, 1], l))
    for l in range(n_low):
        cols.append(table([0, 1], [3, 2], l))
    for l in range(n_low, levels):
        cols.append(table([0, 2, 3, 1], [3, 1, 0, 2], l))
    for l in range(n_low):
        cols.append(table([0, 2], [3, 1], l))
    coef = jnp.concatenate(cols, 0).T
    n_top = levels - n_low
    fwd_loc, fwd_low = 0, 4 * n_top
    adj_loc = fwd_low + 2 * n_low
    adj_low = adj_loc + 4 * n_top

    w_block = lax.dynamic_slice_in_dim(weights, col * bw, bw, 0)
    w_block_t = w_block.T

    def stacked(n):
        return jax.ShapeDtypeStruct((n, bw, rows), BF16)

    def spread(pieces, name):
        u = call(functools.partial(local_body, nb, fwd_loc), stacked(nb), [coef, *pieces], (), name)
        for l in range(n_low):
            other = send(u, 0, 1 << l)
            if l == n_low - 1:
                return u, other
            u = combine(coef, fwd_low + 2 * l, u, other, name + "_mix")

    f_last = fwd_low + 2 * (n_low - 1)

    piece = jax.ShapeDtypeStruct((bw, rows), BF16)
    fp = pack(z, prev_out[0], nb, "pack_f")
    fr = [send(fp[k], 1, k * low) for k in range(nb)]
    sp = pack(z, saved_in[0], nb, "pack_s")
    sr = [sp[0]] + [send(sp[k], 0, k * low) for k in range(1, nb)]
    up = pack(z, prev_grad[0], nb, "pack_u")
    ur = [send(up[k], -1, k * low) for k in range(nb)]

    f_own, f_other = spread(fr, "levels_f")
    s_own, s_other = spread(sr, "levels_s")
    fo = call(
        functools.partial(forward_body, nb, f_last),
        [piece] * nb,
        [coef, blocks, w_block_t, f_own, f_other, *fr],
        (),
        "layer_f",
    )
    fo = [fo[0]] + [send(fo[k], 0, k * low) for k in range(1, nb)]

    v, d, act, gz, u = call(
        functools.partial(backward_body, nb, f_last, adj_loc),
        [stacked(nb)] * 5,
        [coef, blocks, w_block, w_block_t, s_own, s_other, *sr, *ur],
        (),
        "layer_b",
    )
    for l in range(n_low):
        other = send(v, 0, 1 << l)
        if l < n_low - 1:
            v = combine(coef, adj_low + 2 * l, v, other, "adjoint_mix")
    gw, gb = call(
        functools.partial(grads_body, nb),
        [jax.ShapeDtypeStruct((bw, bw), F32), jax.ShapeDtypeStruct((rows, rows), F32)],
        [act, gz, d, u],
        (),
        "weight_grads",
    )
    do = call(
        functools.partial(finish_body, nb, adj_low + 2 * (n_low - 1)),
        [piece] * nb,
        [coef, v, other, d],
        (),
        "finish_b",
    )
    do = [do[0]] + [send(do[k], 0, k * low) for k in range(1, nb)]

    for l in range(n_low):
        half = gw.reshape(low >> l + 1, 2, bw // low, bw)
        mine = jnp.where(bits[l], half[:, 1], half[:, 0])
        theirs = jnp.where(bits[l], half[:, 0], half[:, 1]).astype(BF16)
        gw = mine + send(theirs, 0, 1 << l).astype(F32)
    grad_w = gw.reshape(bw // low, bw)
    for l in range(levels):
        gb = gb + send(gb, 0, 1 << l)
    out_f = unpack(z, fo, "unpack_f")
    out_d = unpack(z, do, "unpack_b")
    return out_f[None], out_d[None], grad_w[None], gb[None]


def solution(mesh):
    placed = (
        P("section", "seq", None),
        P("section", "seq", None),
        P("section", "seq", None),
        P("section", None, None),
        P("section", None, None, None),
        P("section", None, None),
    )
    return jax.shard_map(
        on_device,
        mesh=mesh,
        in_specs=placed,
        out_specs=(
            P("section", "seq", None),
            P("section", "seq", None),
            P("section", "seq", None),
            P("section", None, None),
        ),
        check_vma=False,
    )
```

time: 302 us -> 141 us (0.47)
  waiting for transfers between devices: 227 us -> 36.1 us
  Pallas kernels: 0 us -> 37.2 us
  starting transfers between devices: 14.1 us -> 39.7 us
  other arithmetic: 22.3 us -> 3.62 us
  between operations: 14.3 us -> 1 us
  matrix products: 8.92 us -> 0 us
  local copies, waits for them, and re-layouts: 15.1 us -> 23.1 us
    ppermute x14 -> x29, waiting for transfers between devices: 120 us -> 36.1 us  [send(): return lax.ppermute(x, ('section', 'seq'), pairs)]
    reduce_scatter x1 -> x0, waiting for transfers between devices: 75.1 us -> none  [on_device(): lax.psum_scatter(weight_term, 'seq', scatter_dimension=0, tiled=True)]
    pallas_call x0 -> x14, Pallas kernels: none -> 37.2 us  [call(): pl.pallas_call(body, out_shape=outs, in_specs=[SMEM if a.dtype == jnp.int...]
    psum x1 -> x0, waiting for transfers between devices: 31.9 us -> none  [on_device(): grad_block = lax.psum(block_term, 'seq')]
    ppermute x14 -> x29, starting transfers between devices: 13.8 us -> 39.7 us  [send(): return lax.ppermute(x, ('section', 'seq'), pairs)]
    convert_element_type x13 -> x2, other arithmetic: 22.3 us -> 1.22 us  [on_device(): theirs = jnp.where(bits[l], half[:, 0], half[:, 1]).astype(BF16)]
    gather x0 -> x16, local copies, waits for them, and re-layouts: none -> 11 us  [the longest x8 5.71 us: table(): cf[l, jnp.array(order_upper)]]
    dot_general x8 -> x0, matrix products: 8.92 us -> none  [the longest x1 3.68 us: on_device(): jnp.einsum('tbi,tbo->bio', act_two, gz, preferred_element_type=jnp.float32)]
  transfers between devices with their start and end apart: 16 -> 29, of which waited for: 13 -> 8; matrix products, arithmetic and copies ran while one was open for 10% -> 13% of each run, Pallas kernels for 0% -> 22%
where the time goes in v1:
time: 141 us
  starting transfers between devices  39.7 us (28%)
  Pallas kernels  37.2 us (26%)
  waiting for transfers between devices  36.1 us (26%)
  local copies, waits for them, and re-layouts  23.1 us (16%)
  other arithmetic  3.62 us (3%)
    ppermute x29, starting transfers between devices, send(): return lax.ppermute(x, ('section', 'seq'), pairs)  39.7 us
    pallas_call x14, Pallas kernels, call(): pl.pallas_call(body, out_shape=outs, in_specs=[SMEM if a.dtype == jnp.int...  37.2 us
    ppermute x29, waiting for transfers between devices, send(): return lax.ppermute(x, ('section', 'seq'), pairs)  36.1 us
    unnamed x58, local copies, waits for them, and re-layouts  8.06 us
    gather x8, local copies, waits for them, and re-layouts, table(): cf[l, jnp.array(order_upper)]  5.71 us
    gather x8, local copies, waits for them, and re-layouts, table(): cf[l, jnp.array(order_lower)]  5.34 us
    dynamic_slice x2, local copies, waits for them, and re-layouts, on_device(): w_block = lax.dynamic_slice_in_dim(weights, col * bw, bw, 0)  3 us
  transfers between devices with their start and end apart: 29, of which 8 were waited for; matrix products, arithmetic and copies ran while one was open for 13% of the time, Pallas kernels for 22%

profile of v1, /device:TPU:0, one launch (start us, length us, event | category | flops | bytes accessed | tf_op | source)
XLA Modules:
  0.0 140.7 jit_solution(12589276868544579261)
XLA Ops:
  2.7 4.0 %collective-permute-start.10 = (bf16[448,128]{1,0:T(8,128)(2,1)}, bf16[448,128]{1,0:T(8,128)(2,1)S(1)}, u32[]{:S(2)}, u32[]{:S(2)}) collective-permute-start(bf16[448,128]{1,0:T(8,128)(2,1)} %get-tuple-element.41), channel_id=1, source_target_pairs={{0,8},{1,9},{2,10},{3,11},{4,12},{5,13},{6,14},{7,15},{8,0},{9,1},... | collective-permute-start | bytes 344072 | tf_op jit(solution)/shard_map/ppermute | solution.py:199
  21.3 2.6 %levels_s.1.own_ref = bf16[4,448,128]{2,1,0:T(8,128)(2,1)} custom-call(f32[448,24]{1,0:T(8,128)} %bitcast.46, bf16[448,128]{1,0:T(8,128)(2,1)} %get-tuple-element.39.refs_0_, bf16[448,128]{1,0:T(8,128)(2,1)} %copy-done.4, bf16[448,128]{1,0:T(8,128)(2,1)} %copy-done.2, bf16[448,128]{1,0:T(8,128)(2,1)} %copy-done.3), custom_call_target="tpu_custom_call" | custom-call | tf_op jit(solution)/shard_map/levels_s/pallas_call | solution.py:21
  29.1 2.6 %collective-permute-start.2 = (bf16[448,128]{1,0:T(8,128)(2,1)}, bf16[448,128]{1,0:T(8,128)(2,1)S(1)}, u32[]{:S(2)}, u32[]{:S(2)}) collective-permute-start(bf16[448,128]{1,0:T(8,128)(2,1)} %get-tuple-element.33), channel_id=1, source_target_pairs={{0,24},{1,25},{2,26},{3,27},{4,28},{5,29},{6,30},{7,31},{8,16},{9,... | collective-permute-start | bytes 344072 | tf_op jit(solution)/shard_map/ppermute | solution.py:199
  32.6 3.4 %collective-permute-done.refs_0_ = bf16[448,128]{1,0:T(8,128)(2,1)S(1)} collective-permute-done((bf16[448,128]{1,0:T(8,128)(2,1)}, bf16[448,128]{1,0:T(8,128)(2,1)S(1)}, u32[]{:S(2)}, u32[]{:S(2)}) %collective-permute-start) | collective-permute-done | bytes 114720 | tf_op jit(solution)/shard_map/ppermute | solution.py:199
  36.0 5.6 %collective-permute-done.2.refs_2_ = bf16[448,128]{1,0:T(8,128)(2,1)S(1)} collective-permute-done((bf16[448,128]{1,0:T(8,128)(2,1)}, bf16[448,128]{1,0:T(8,128)(2,1)S(1)}, u32[]{:S(2)}, u32[]{:S(2)}) %collective-permute-start.2) | collective-permute-done | bytes 114720 | tf_op jit(solution)/shard_map/ppermute | solution.py:199
  42.9 2.6 %levels_f.1.own_ref = bf16[4,448,128]{2,1,0:T(8,128)(2,1)} custom-call(f32[448,24]{1,0:T(8,128)} %bitcast.47, bf16[448,128]{1,0:T(8,128)(2,1)} %copy-done.5, bf16[448,128]{1,0:T(8,128)(2,1)} %copy-done.6, bf16[448,128]{1,0:T(8,128)(2,1)} %copy-done.7, bf16[448,128]{1,0:T(8,128)(2,1)} %copy-done.8), custom_call_target="tpu_custom_call" | custom-call | tf_op jit(solution)/shard_map/levels_f/pallas_call | solution.py:21
  46.3 2.3 %levels_s_mix.1.own_ref = bf16[4,448,128]{2,1,0:T(8,128)(2,1)} custom-call(f32[448,24]{1,0:T(8,128)} %bitcast.48, bf16[4,448,128]{2,1,0:T(8,128)(2,1)} %levels_s.1.own_ref, bf16[4,448,128]{2,1,0:T(8,128)(2,1)} %copy-done.11), custom_call_target="tpu_custom_call" | custom-call | tf_op jit(solution)/shard_map/levels_s_mix/pallas_call | solution.py:21
  54.7 2.3 %levels_f_mix.1.own_ref = bf16[4,448,128]{2,1,0:T(8,128)(2,1)} custom-call(f32[448,24]{1,0:T(8,128)} %bitcast.49, bf16[4,448,128]{2,1,0:T(8,128)(2,1)} %levels_f.1.own_ref, bf16[4,448,128]{2,1,0:T(8,128)(2,1)} %copy-done.12), custom_call_target="tpu_custom_call" | custom-call | tf_op jit(solution)/shard_map/levels_f_mix/pallas_call | solution.py:21
  62.6 2.0 %dynamic-slice_bitcast_fusion.1 = (bf16[448,448]{0,1:T(8,128)(2,1)S(1)}, bf16[448,448]{1,0:T(8,128)(2,1)}) fusion(bf16[1,1792,448]{1,2,0:T(8,128)(2,1)} %param.27, s32[]{:T(128)S(6)} %select_n.151), kind=kLoop, calls=%fused_computation.22 | loop fusion | bytes 1204228 | tf_op jit(solution)/shard_map/dynamic_slice | solution.py:222
  65.6 5.6 %collective-permute-done.16.refs_6_ = bf16[448,128]{1,0:T(8,128)(2,1)S(1)} collective-permute-done((bf16[448,128]{1,0:T(8,128)(2,1)S(1)}, bf16[448,128]{1,0:T(8,128)(2,1)S(1)}, u32[]{:S(2)}, u32[]{:S(2)}) %collective-permute-start.16) | collective-permute-done | bytes 114720 | tf_op jit(solution)/shard_map/ppermute | solution.py:199
  72.0 6.0 %layer_b.1 = (bf16[4,448,128]{2,1,0:T(8,128)(2,1)}, bf16[4,448,128]{2,1,0:T(8,128)(2,1)}, bf16[4,448,128]{2,1,0:T(8,128)(2,1)}, bf16[4,448,128]{2,1,0:T(8,128)(2,1)}, bf16[4,448,128]{2,1,0:T(8,128)(2,1)}) custom-call(f32[448,24]{1,0:T(8,128)} %bitcast.50, bf16[128,128]{1,0:T(8,128)(2,1)} %bitcast.61, bf16[448,448]{1,0:T(8,128)(2,1)} %copy.46.w_ref, ...), custom_call_target="tpu_custom_call" | custom-call | tf_op jit(solution)/shard_map/layer_b/pallas_call | solution.py:21
  78.0 3.2 %weight_grads.1 = (f32[448,448]{1,0:T(8,128)}, f32[128,128]{1,0:T(8,128)}) custom-call(bf16[4,448,128]{2,1,0:T(8,128)(2,1)} %get-tuple-element.53.act_ref, bf16[4,448,128]{2,1,0:T(8,128)(2,1)} %get-tuple-element.54.gz_ref, bf16[4,448,128]{2,1,0:T(8,128)(2,1)} %get-tuple-element.48.d_ref, bf16[4,448,128]{2,1,0:T(8,128)(2,1)} %get-tuple-element.55.u_ref), custom_call_target="tpu_custom_call" | custom-call | tf_op jit(solution)/shard_map/weight_grads/pallas_call | solution.py:21
  86.3 3.3 %layer_f.1 = (bf16[448,128]{1,0:T(8,128)(2,1)}, bf16[448,128]{1,0:T(8,128)(2,1)}, bf16[448,128]{1,0:T(8,128)(2,1)}, bf16[448,128]{1,0:T(8,128)(2,1)}) custom-call(f32[448,24]{1,0:T(8,128)} %bitcast.51, bf16[128,128]{1,0:T(8,128)(2,1)} %bitcast.62, bf16[448,448]{1,0:T(8,128)(2,1)} %get-tuple-element.59.wt_ref, bf16[4,448,128]{2,1,0:T(8,128)(2,1)} %levels_f_mix.1.own_ref, ...), custom_call_target="tpu_custom_call" | custom-call | tf_op jit(solution)/shard_map/layer_f/pallas_call | solution.py:21
  89.7 2.1 %collective-permute-start.6 = (bf16[448,128]{1,0:T(8,128)(2,1)}, bf16[448,128]{1,0:T(8,128)(2,1)S(1)}, u32[]{:S(2)}, u32[]{:S(2)}) collective-permute-start(bf16[448,128]{1,0:T(8,128)(2,1)} %get-tuple-element.36), channel_id=1, source_target_pairs={{0,4},{1,5},{2,6},{3,7},{4,0},{5,1},{6,2},{7,3},{8,12},{9,13},{10,... | collective-permute-start | bytes 344072 | tf_op jit(solution)/shard_map/ppermute | solution.py:199
  95.6 2.4 %collective-permute-start.27 = (f32[128,128]{1,0:T(8,128)S(1)}, f32[128,128]{1,0:T(8,128)S(1)}, u32[]{:S(2)}, u32[]{:S(2)}) collective-permute-start(f32[128,128]{1,0:T(8,128)S(1)} %add.123), channel_id=1, source_target_pairs={{0,4},{1,5},{2,6},{3,7},{4,0},{5,1},{6,2},{7,3},{8,12},{9,13},{10,... | collective-permute-start | bytes 196616 | tf_op jit(solution)/shard_map/ppermute | solution.py:199
  98.0 5.9 %collective-permute-done.7.refs_2_ = bf16[448,128]{1,0:T(8,128)(2,1)S(1)} collective-permute-done((bf16[448,128]{1,0:T(8,128)(2,1)}, bf16[448,128]{1,0:T(8,128)(2,1)S(1)}, u32[]{:S(2)}, u32[]{:S(2)}) %collective-permute-start.7) | collective-permute-done | bytes 114720 | tf_op jit(solution)/shard_map/ppermute | solution.py:199
  104.5 2.0 %unpack_f.1 = bf16[128,1792]{1,0:T(8,128)(2,1)} custom-call(s32[1]{0:T(128)} %bitcast.z_ref, bf16[448,128]{1,0:T(8,128)(2,1)} %get-tuple-element.35.refs_0_, bf16[448,128]{1,0:T(8,128)(2,1)} %copy-done.16, bf16[448,128]{1,0:T(8,128)(2,1)} %copy-done.18, bf16[448,128]{1,0:T(8,128)(2,1)} %copy-done.21), custom_call_target="tpu_custom_call" | custom-call | tf_op jit(solution)/shard_map/unpack_f/pallas_call | solution.py:21
  106.6 2.9 %collective-permute-start.28 = (f32[128,128]{1,0:T(8,128)S(1)}, f32[128,128]{1,0:T(8,128)S(1)}, u32[]{:S(2)}, u32[]{:S(2)}) collective-permute-start(f32[128,128]{1,0:T(8,128)S(1)} %add.124), channel_id=1, source_target_pairs={{0,8},{1,9},{2,10},{3,11},{4,12},{5,13},{6,14},{7,15},{8,0},{9,1},... | collective-permute-start | bytes 196616 | tf_op jit(solution)/shard_map/ppermute | solution.py:199
  110.3 2.3 %adjoint_mix.1.own_ref = bf16[4,448,128]{2,1,0:T(8,128)(2,1)} custom-call(f32[448,24]{1,0:T(8,128)} %bitcast.52, bf16[4,448,128]{2,1,0:T(8,128)(2,1)} %get-tuple-element.47.own_ref, bf16[4,448,128]{2,1,0:T(8,128)(2,1)} %copy-done.10), custom_call_target="tpu_custom_call" | custom-call | tf_op jit(solution)/shard_map/adjoint_mix/pallas_call | solution.py:21
  115.4 10.1 %collective-permute-done.19.other_ref = bf16[4,448,128]{2,1,0:T(8,128)(2,1)S(1)} collective-permute-done((bf16[4,448,128]{2,1,0:T(8,128)(2,1)}, bf16[4,448,128]{2,1,0:T(8,128)(2,1)S(1)}, u32[]{:S(2)}, u32[]{:S(2)}) %collective-permute-start.19) | collective-permute-done | bytes 458784 | tf_op jit(solution)/shard_map/ppermute | solution.py:199
  126.3 2.5 %finish_b.1 = (bf16[448,128]{1,0:T(8,128)(2,1)}, bf16[448,128]{1,0:T(8,128)(2,1)}, bf16[448,128]{1,0:T(8,128)(2,1)}, bf16[448,128]{1,0:T(8,128)(2,1)}) custom-call(f32[448,24]{1,0:T(8,128)} %bitcast.53, bf16[4,448,128]{2,1,0:T(8,128)(2,1)} %adjoint_mix.1.own_ref, bf16[4,448,128]{2,1,0:T(8,128)(2,1)} %copy-done.13, bf16[4,448,128]{2,1,0:T(8,128)(2,1)} %get-tuple-element.48.d_ref), custom_call_target="tpu_custom_call" | custom-call | tf_op jit(solution)/shard_map/finish_b/pallas_call | solution.py:21
  130.5 2.6 %collective-permute-start.22 = (bf16[448,128]{1,0:T(8,128)(2,1)}, bf16[448,128]{1,0:T(8,128)(2,1)S(1)}, u32[]{:S(2)}, u32[]{:S(2)}) collective-permute-start(bf16[448,128]{1,0:T(8,128)(2,1)} %get-tuple-element.52), channel_id=1, source_target_pairs={{0,12},{1,13},{2,14},{3,15},{4,8},{5,9},{6,10},{7,11},{8,4},{9,5},... | collective-permute-start | bytes 344072 | tf_op jit(solution)/shard_map/ppermute | solution.py:199
  135.0 2.9 %collective-permute-done.21.refs_2_ = bf16[448,128]{1,0:T(8,128)(2,1)S(1)} collective-permute-done((bf16[448,128]{1,0:T(8,128)(2,1)}, bf16[448,128]{1,0:T(8,128)(2,1)S(1)}, u32[]{:S(2)}, u32[]{:S(2)}) %collective-permute-start.21) | collective-permute-done | bytes 114720 | tf_op jit(solution)/shard_map/ppermute | solution.py:199
  138.7 2.0 %unpack_b.1 = bf16[128,1792]{1,0:T(8,128)(2,1)} custom-call(s32[1]{0:T(128)} %bitcast.z_ref, bf16[448,128]{1,0:T(8,128)(2,1)} %get-tuple-element.49.refs_0_, bf16[448,128]{1,0:T(8,128)(2,1)} %copy-done.17, bf16[448,128]{1,0:T(8,128)(2,1)} %copy-done.19, bf16[448,128]{1,0:T(8,128)(2,1)} %copy-done.20), custom_call_target="tpu_custom_call" | custom-call | tf_op jit(solution)/shard_map/unpack_b/pallas_call | solution.py:21
  (142 shorter events, 56.3 us)
Async XLA Ops:
  2.7 17.9 %collective-permute-start.10 = (bf16[448,128]{1,0:T(8,128)(2,1)}, bf16[448,128]{1,0:T(8,128)(2,1)S(1)}, u32[]{:S(2)}, u32[]{:S(2)}) collective-permute-start(bf16[448,128]{1,0:T(8,128)(2,1)} %get-tuple-element.41), channel_id=1, source_target_pairs={{0,8},{1,9},{2,10},{3,11},{4,12},{5,13},{6,14},{7,15},{8,0},{9,1},... | collective-permute-start | bytes 344072 | tf_op jit(solution)/shard_map/ppermute | solution.py:199
  6.7 13.8 %collective-permute-start.11 = (bf16[448,128]{1,0:T(8,128)(2,1)}, bf16[448,128]{1,0:T(8,128)(2,1)S(1)}, u32[]{:S(2)}, u32[]{:S(2)}) collective-permute-start(bf16[448,128]{1,0:T(8,128)(2,1)} %get-tuple-element.42), channel_id=1, source_target_pairs={{0,12},{1,13},{2,14},{3,15},{4,8},{5,9},{6,10},{7,11},{8,4},{9,5},... | collective-permute-start | bytes 344072 | tf_op jit(solution)/shard_map/ppermute | solution.py:199
  8.0 12.5 %collective-permute-start.9 = (bf16[448,128]{1,0:T(8,128)(2,1)}, bf16[448,128]{1,0:T(8,128)(2,1)S(1)}, u32[]{:S(2)}, u32[]{:S(2)}) collective-permute-start(bf16[448,128]{1,0:T(8,128)(2,1)} %get-tuple-element.40), channel_id=1, source_target_pairs={{0,4},{1,5},{2,6},{3,7},{4,0},{5,1},{6,2},{7,3},{8,12},{9,13},{10,... | collective-permute-start | bytes 344072 | tf_op jit(solution)/shard_map/ppermute | solution.py:199
  23.9 21.6 %collective-permute-start.12 = (bf16[4,448,128]{2,1,0:T(8,128)(2,1)}, bf16[4,448,128]{2,1,0:T(8,128)(2,1)S(1)}, u32[]{:S(2)}, u32[]{:S(2)}) collective-permute-start(bf16[4,448,128]{2,1,0:T(8,128)(2,1)} %levels_s.1.own_ref), channel_id=1, source_target_pairs={{0,1},{1,0},{2,3},{3,2},{4,5},{5,4},{6,7},{7,6},{8,9},{9,8},{10,11... | collective-permute-start | bytes 1376264 | tf_op jit(solution)/shard_map/ppermute | solution.py:199
  25.8 10.2 %collective-permute-start = (bf16[448,128]{1,0:T(8,128)(2,1)}, bf16[448,128]{1,0:T(8,128)(2,1)S(1)}, u32[]{:S(2)}, u32[]{:S(2)}) collective-permute-start(bf16[448,128]{1,0:T(8,128)(2,1)} %get-tuple-element.31), channel_id=1, source_target_pairs={{0,16},{1,17},{2,18},{3,19},{4,20},{5,21},{6,22},{7,23},{8,24},{9,... | collective-permute-start | bytes 344072 | tf_op jit(solution)/shard_map/ppermute | solution.py:199
  27.3 8.7 %collective-permute-start.1 = (bf16[448,128]{1,0:T(8,128)(2,1)}, bf16[448,128]{1,0:T(8,128)(2,1)S(1)}, u32[]{:S(2)}, u32[]{:S(2)}) collective-permute-start(bf16[448,128]{1,0:T(8,128)(2,1)} %get-tuple-element.32), channel_id=1, source_target_pairs={{0,20},{1,21},{2,22},{3,23},{4,16},{5,17},{6,18},{7,19},{8,28},{9,... | collective-permute-start | bytes 344072 | tf_op jit(solution)/shard_map/ppermute | solution.py:199
  29.1 12.5 %collective-permute-start.2 = (bf16[448,128]{1,0:T(8,128)(2,1)}, bf16[448,128]{1,0:T(8,128)(2,1)S(1)}, u32[]{:S(2)}, u32[]{:S(2)}) collective-permute-start(bf16[448,128]{1,0:T(8,128)(2,1)} %get-tuple-element.33), channel_id=1, source_target_pairs={{0,24},{1,25},{2,26},{3,27},{4,28},{5,29},{6,30},{7,31},{8,16},{9,... | collective-permute-start | bytes 344072 | tf_op jit(solution)/shard_map/ppermute | solution.py:199
  31.7 9.9 %collective-permute-start.3 = (bf16[448,128]{1,0:T(8,128)(2,1)}, bf16[448,128]{1,0:T(8,128)(2,1)S(1)}, u32[]{:S(2)}, u32[]{:S(2)}) collective-permute-start(bf16[448,128]{1,0:T(8,128)(2,1)} %get-tuple-element.34), channel_id=1, source_target_pairs={{0,28},{1,29},{2,30},{3,31},{4,24},{5,25},{6,26},{7,27},{8,20},{9,... | collective-permute-start | bytes 344072 | tf_op jit(solution)/shard_map/ppermute | solution.py:199
  45.5 8.5 %collective-permute-start.4 = (bf16[4,448,128]{2,1,0:T(8,128)(2,1)}, bf16[4,448,128]{2,1,0:T(8,128)(2,1)S(1)}, u32[]{:S(2)}, u32[]{:S(2)}) collective-permute-start(bf16[4,448,128]{2,1,0:T(8,128)(2,1)} %levels_f.1.own_ref), channel_id=1, source_target_pairs={{0,1},{1,0},{2,3},{3,2},{4,5},{5,4},{6,7},{7,6},{8,9},{9,8},{10,11... | collective-permute-start | bytes 1376264 | tf_op jit(solution)/shard_map/ppermute | solution.py:199
  48.6 22.6 %collective-permute-start.13 = (bf16[4,448,128]{2,1,0:T(8,128)(2,1)}, bf16[4,448,128]{2,1,0:T(8,128)(2,1)S(1)}, u32[]{:S(2)}, u32[]{:S(2)}) collective-permute-start(bf16[4,448,128]{2,1,0:T(8,128)(2,1)} %levels_s_mix.1.own_ref), channel_id=1, source_target_pairs={{0,2},{1,3},{2,0},{3,1},{4,6},{5,7},{6,4},{7,5},{8,10},{9,11},{10,... | collective-permute-start | bytes 1376264 | tf_op jit(solution)/shard_map/ppermute | solution.py:199
  52.1 8.9 %collective-permute-start.14 = (bf16[448,128]{1,0:T(8,128)(2,1)}, bf16[448,128]{1,0:T(8,128)(2,1)S(1)}, u32[]{:S(2)}, u32[]{:S(2)}) collective-permute-start(bf16[448,128]{1,0:T(8,128)(2,1)} %get-tuple-element.43), channel_id=1, source_target_pairs={{0,16},{1,17},{2,18},{3,19},{4,20},{5,21},{6,22},{7,23},{8,24},{9,... | collective-permute-start | bytes 344072 | tf_op jit(solution)/shard_map/ppermute | solution.py:199
  57.0 28.5 %collective-permute-start.5 = (bf16[4,448,128]{2,1,0:T(8,128)(2,1)}, bf16[4,448,128]{2,1,0:T(8,128)(2,1)S(1)}, u32[]{:S(2)}, u32[]{:S(2)}) collective-permute-start(bf16[4,448,128]{2,1,0:T(8,128)(2,1)} %levels_f_mix.1.own_ref), channel_id=1, source_target_pairs={{0,2},{1,3},{2,0},{3,1},{4,6},{5,7},{6,4},{7,5},{8,10},{9,11},{10,... | collective-permute-start | bytes 1376264 | tf_op jit(solution)/shard_map/ppermute | solution.py:199
  59.1 12.1 %collective-permute-start.16 = (bf16[448,128]{1,0:T(8,128)(2,1)S(1)}, bf16[448,128]{1,0:T(8,128)(2,1)S(1)}, u32[]{:S(2)}, u32[]{:S(2)}) collective-permute-start(bf16[448,128]{1,0:T(8,128)(2,1)S(1)} %copy-done.27), channel_id=1, source_target_pairs={{0,24},{1,25},{2,26},{3,27},{4,28},{5,29},{6,30},{7,31},{8,16},{9,... | collective-permute-start | bytes 344072 | tf_op jit(solution)/shard_map/ppermute | solution.py:199
  61.0 10.2 %collective-permute-start.17 = (bf16[448,128]{1,0:T(8,128)(2,1)S(1)}, bf16[448,128]{1,0:T(8,128)(2,1)S(1)}, u32[]{:S(2)}, u32[]{:S(2)}) collective-permute-start(bf16[448,128]{1,0:T(8,128)(2,1)S(1)} %copy-done.26), channel_id=1, source_target_pairs={{0,28},{1,29},{2,30},{3,31},{4,24},{5,25},{6,26},{7,27},{8,20},{9,... | collective-permute-start | bytes 344072 | tf_op jit(solution)/shard_map/ppermute | solution.py:199
  81.3 28.3 %collective-permute-start.18 = (bf16[4,448,128]{2,1,0:T(8,128)(2,1)S(1)}, bf16[4,448,128]{2,1,0:T(8,128)(2,1)S(1)}, u32[]{:S(2)}, u32[]{:S(2)}) collective-permute-start(bf16[4,448,128]{2,1,0:T(8,128)(2,1)S(1)} %copy-done.9), channel_id=1, source_target_pairs={{0,1},{1,0},{2,3},{3,2},{4,5},{5,4},{6,7},{7,6},{8,9},{9,8},{10,11... | collective-permute-start | bytes 1376264 | tf_op jit(solution)/shard_map/ppermute | solution.py:199
  83.0 26.4 %collective-permute-start.23 = (bf16[2,112,448]{2,1,0:T(8,128)(2,1)S(1)}, bf16[2,112,448]{2,1,0:T(8,128)(2,1)S(1)}, u32[]{:S(2)}, u32[]{:S(2)}) collective-permute-start(bf16[2,112,448]{2,1,0:T(8,128)(2,1)S(1)} %fusion.1), channel_id=1, source_target_pairs={{0,1},{1,0},{2,3},{3,2},{4,5},{5,4},{6,7},{7,6},{8,9},{9,8},{10,11... | collective-permute-start | bytes 602120 | tf_op jit(solution)/shard_map/ppermute | solution.py:199
  84.0 8.7 %collective-permute-start.26 = (f32[128,128]{1,0:T(8,128)S(1)}, f32[128,128]{1,0:T(8,128)S(1)}, u32[]{:S(2)}, u32[]{:S(2)}) collective-permute-start(f32[128,128]{1,0:T(8,128)S(1)} %add.122), channel_id=1, source_target_pairs={{0,2},{1,3},{2,0},{3,1},{4,6},{5,7},{6,4},{7,5},{8,10},{9,11},{10,... | collective-permute-start | bytes 196616 | tf_op jit(solution)/shard_map/ppermute | solution.py:199
  91.7 12.1 %collective-permute-start.7 = (bf16[448,128]{1,0:T(8,128)(2,1)}, bf16[448,128]{1,0:T(8,128)(2,1)S(1)}, u32[]{:S(2)}, u32[]{:S(2)}) collective-permute-start(bf16[448,128]{1,0:T(8,128)(2,1)} %get-tuple-element.37), channel_id=1, source_target_pairs={{0,8},{1,9},{2,10},{3,11},{4,12},{5,13},{6,14},{7,15},{8,0},{9,1},... | collective-permute-start | bytes 344072 | tf_op jit(solution)/shard_map/ppermute | solution.py:199
  92.7 11.1 %collective-permute-start.8 = (bf16[448,128]{1,0:T(8,128)(2,1)}, bf16[448,128]{1,0:T(8,128)(2,1)S(1)}, u32[]{:S(2)}, u32[]{:S(2)}) collective-permute-start(bf16[448,128]{1,0:T(8,128)(2,1)} %get-tuple-element.38), channel_id=1, source_target_pairs={{0,12},{1,13},{2,14},{3,15},{4,8},{5,9},{6,10},{7,11},{8,4},{9,5},... | collective-permute-start | bytes 344072 | tf_op jit(solution)/shard_map/ppermute | solution.py:199
  95.6 11.0 %collective-permute-start.27 = (f32[128,128]{1,0:T(8,128)S(1)}, f32[128,128]{1,0:T(8,128)S(1)}, u32[]{:S(2)}, u32[]{:S(2)}) collective-permute-start(f32[128,128]{1,0:T(8,128)S(1)} %add.123), channel_id=1, source_target_pairs={{0,4},{1,5},{2,6},{3,7},{4,0},{5,1},{6,2},{7,3},{8,12},{9,13},{10,... | collective-permute-start | bytes 196616 | tf_op jit(solution)/shard_map/ppermute | solution.py:199
  106.6 8.2 %collective-permute-start.28 = (f32[128,128]{1,0:T(8,128)S(1)}, f32[128,128]{1,0:T(8,128)S(1)}, u32[]{:S(2)}, u32[]{:S(2)}) collective-permute-start(f32[128,128]{1,0:T(8,128)S(1)} %add.124), channel_id=1, source_target_pairs={{0,8},{1,9},{2,10},{3,11},{4,12},{5,13},{6,14},{7,15},{8,0},{9,1},... | collective-permute-start | bytes 196616 | tf_op jit(solution)/shard_map/ppermute | solution.py:199
  112.6 12.9 %collective-permute-start.19 = (bf16[4,448,128]{2,1,0:T(8,128)(2,1)}, bf16[4,448,128]{2,1,0:T(8,128)(2,1)S(1)}, u32[]{:S(2)}, u32[]{:S(2)}) collective-permute-start(bf16[4,448,128]{2,1,0:T(8,128)(2,1)} %adjoint_mix.1.own_ref), channel_id=1, source_target_pairs={{0,2},{1,3},{2,0},{3,1},{4,6},{5,7},{6,4},{7,5},{8,10},{9,11},{10,... | collective-permute-start | bytes 1376264 | tf_op jit(solution)/shard_map/ppermute | solution.py:199
  113.1 20.0 %collective-permute-start.24 = (bf16[1,112,448]{2,1,0:T(8,128)(2,1)S(1)}, bf16[1,112,448]{2,1,0:T(8,128)(2,1)S(1)}, u32[]{:S(2)}, u32[]{:S(2)}) collective-permute-start(bf16[1,112,448]{2,1,0:T(8,128)(2,1)S(1)} %fusion.2), channel_id=1, source_target_pairs={{0,2},{1,3},{2,0},{3,1},{4,6},{5,7},{6,4},{7,5},{8,10},{9,11},{10,... | collective-permute-start | bytes 301064 | tf_op jit(solution)/shard_map/ppermute | solution.py:199
  128.8 9.2 %collective-permute-start.21 = (bf16[448,128]{1,0:T(8,128)(2,1)}, bf16[448,128]{1,0:T(8,128)(2,1)S(1)}, u32[]{:S(2)}, u32[]{:S(2)}) collective-permute-start(bf16[448,128]{1,0:T(8,128)(2,1)} %get-tuple-element.51), channel_id=1, source_target_pairs={{0,8},{1,9},{2,10},{3,11},{4,12},{5,13},{6,14},{7,15},{8,0},{9,1},... | collective-permute-start | bytes 344072 | tf_op jit(solution)/shard_map/ppermute | solution.py:199
  (34 other events, 137.4 us)

commit v2 on v0

v2 whole, which is shorter than its diff:
```python
import functools

import jax
import jax.numpy as jnp
from jax import lax
from jax.experimental import pallas as pl
from jax.experimental.pallas import tpu as pltpu
from jax.sharding import PartitionSpec as P

F32 = jnp.float32
BF16 = jnp.bfloat16
LANES = 128
CH = 64


def dot(a, b, ca, cb):
    return lax.dot_general(a, b, (((ca,), (cb,)), ((), ())), preferred_element_type=F32)


def near_memory(x):
    return pltpu.with_memory_space_constraint(x, pltpu.VMEM)


def call(body, outs, ins, scratch=(), name=None, deps=(), out_hbm=False):
    n_in, n_dep = len(ins), len(deps)

    def kernel(*refs):
        body(*refs[:n_in], *refs[n_in + n_dep :])

    specs = []
    args = []
    for a in ins:
        if a.dtype == jnp.int32:
            specs.append(pl.BlockSpec(memory_space=pltpu.SMEM))
            args.append(a)
        else:
            specs.append(pl.BlockSpec(memory_space=pltpu.VMEM))
            args.append(near_memory(a))
    for a in deps:
        specs.append(pl.BlockSpec(memory_space=pl.ANY))
        args.append(a)
    shapes = jax.tree.map(
        lambda o: o if out_hbm else pltpu.VMEM(o.shape, o.dtype),
        outs,
    )
    return pl.pallas_call(
        kernel,
        out_shape=shapes,
        in_specs=specs,
        out_specs=jax.tree.map(lambda _: pl.BlockSpec(memory_space=pltpu.VMEM), outs),
        scratch_shapes=scratch,
        name=name,
        compiler_params=pltpu.CompilerParams(vmem_limit_bytes=16 << 20),
        cost_estimate=pl.CostEstimate(flops=1000, bytes_accessed=1000, transcendentals=0),
    )(*args)


def shape(*dims, dtype=BF16):
    return jax.ShapeDtypeStruct(dims, dtype)


def pack_body(nb, at_ref, x_ref, *refs):
    outs, buf = refs[:nb], refs[nb]
    width = x_ref.shape[1]
    bw = width // nb
    for j in range(0, width, LANES):
        buf[j : j + LANES, :] = x_ref[:, j : j + LANES].T
    for k in range(nb):
        start = pl.multiple_of(jnp.bitwise_xor(at_ref[0], k) * bw, 16)
        outs[k][...] = buf[pl.ds(start, bw), :]


def unpack_body(nb, at_ref, *refs):
    ins, out, buf = refs[:nb], refs[nb], refs[nb + 1]
    width = out.shape[1]
    bw = width // nb
    for k in range(nb):
        start = pl.multiple_of(jnp.bitwise_xor(at_ref[0], k) * bw, 16)
        buf[pl.ds(start, bw), :] = ins[k][...]
    for j in range(0, width, LANES):
        out[:, j : j + LANES] = buf[j : j + LANES, :].T


def prep_body(nb, n_low, at_ref, c_ref, w_ref, coef_ref, wo_ref, wt_ref, buf):
    levels, _, width = c_ref.shape
    bw = width // nb
    for l in range(levels):
        for j in range(0, width, LANES):
            buf[j : j + LANES, 4 * l : 4 * l + 4] = c_ref[l, :, j : j + LANES].T
    start = pl.multiple_of(at_ref[0] * bw, 16)
    cf = buf[pl.ds(start, bw), :]
    col = 0
    for lower, upper, span in (
        ((0, 1, 3, 2), (3, 2, 0, 1), range(n_low, levels)),
        ((0, 1), (3, 2), range(n_low)),
        ((0, 2, 3, 1), (3, 1, 0, 2), range(n_low, levels)),
        ((0, 2), (3, 1), range(n_low)),
    ):
        for l in span:
            for a, b in zip(lower, upper):
                high = at_ref[1 + l] == 1
                coef_ref[:, col : col + 1] = jnp.where(
                    high, cf[:, 4 * l + b : 4 * l + b + 1], cf[:, 4 * l + a : 4 * l + a + 1]
                )
                col += 1
    w = w_ref[pl.ds(start, bw), :]
    wo_ref[...] = w
    wt_ref[...] = w.T


def stack_body(*refs):
    out = refs[-1]
    for k, r in enumerate(refs[:-1]):
        out[k] = r[...]


def pair(coef_ref, first, s):
    return (coef_ref[s : s + CH, first : first + 1], coef_ref[s : s + CH, first + 1 : first + 2])


def combine_body(first, coef_ref, own_ref, other_ref, out_ref):
    for s in range(0, out_ref.shape[1], CH):
        c0, c1 = pair(coef_ref, first, s)
        for k in range(out_ref.shape[0]):
            own = own_ref[k, s : s + CH, :].astype(F32)
            other = other_ref[k, s : s + CH, :].astype(F32)
            out_ref[k, s : s + CH, :] = (c0 * own + c1 * other).astype(BF16)


def local_levels(vals, coef, first):
    vals = list(vals)
    nb = len(vals)
    for j in range(nb.bit_length() - 1):
        c = [coef[:, first + 4 * j + i : first + 4 * j + i + 1] for i in range(4)]
        for k in range(nb):
            if not k >> j & 1:
                m = k | 1 << j
                a, b = vals[k], vals[m]
                vals[k] = c[0] * a + c[1] * b
                vals[m] = c[2] * b + c[3] * a
    return vals


def finish_state(first, loc, coef_ref, chunks, u_ref):
    for s in range(0, u_ref.shape[1], CH):
        c0, c1 = pair(coef_ref, first, s)
        vals = []
        for own_ref, other_ref in chunks:
            for k in range(own_ref.shape[0]):
                vals.append(c0 * own_ref[k, s : s + CH, :].astype(F32) + c1 * other_ref[k, s : s + CH, :].astype(F32))
        vals = local_levels(vals, coef_ref[s : s + CH, :], loc)
        for k, v in enumerate(vals):
            u_ref[k, s : s + CH, :] = v.astype(BF16)


def forward_body(nb, first, loc, coef_ref, b_ref, wt_ref, o0, x0, o1, x1, *refs):
    ins, outs, u_ref = refs[:nb], refs[nb : 2 * nb], refs[2 * nb]
    finish_state(first, loc, coef_ref, ((o0, x0), (o1, x1)), u_ref)
    for k in range(nb):
        act = (ins[k][...].astype(F32) + dot(u_ref[k], b_ref[...], 1, 1)).astype(BF16)
        pre = dot(wt_ref[...], act, 1, 0)
        outs[k][...] = (act.astype(F32) + pre * jax.nn.sigmoid(pre)).astype(BF16)


def backward_body(nb, first, loc, adj, coef_ref, b_ref, w_ref, wt_ref, o0, x0, o1, x1, *refs):
    ins, ups = refs[:nb], refs[nb : 2 * nb]
    v0_ref, v1_ref, d_ref, act_ref, gz_ref, u_ref, v_ref = refs[2 * nb :]
    finish_state(first, loc, coef_ref, ((o0, x0), (o1, x1)), u_ref)
    for k in range(nb):
        act = (ins[k][...].astype(F32) + dot(u_ref[k], b_ref[...], 1, 1)).astype(BF16)
        act_ref[k] = act
        pre = dot(wt_ref[...], act, 1, 0)
        sig = jax.nn.sigmoid(pre)
        up = ups[k][...].astype(F32)
        gz = (up * (sig * (1.0 + pre * (1.0 - sig)))).astype(BF16)
        gz_ref[k] = gz
        d = (up + dot(w_ref[...], gz, 1, 0)).astype(BF16)
        d_ref[k] = d
        v_ref[k] = dot(d, b_ref[...], 1, 0)
    half = nb // 2
    for s in range(0, d_ref.shape[1], CH):
        vals = local_levels([v_ref[k, s : s + CH, :] for k in range(nb)], coef_ref[s : s + CH, :], adj)
        for k in range(half):
            v0_ref[k, s : s + CH, :] = vals[k].astype(BF16)
            v1_ref[k, s : s + CH, :] = vals[half + k].astype(BF16)


def finish_body(k0, n, first, coef_ref, own_ref, other_ref, d_ref, *outs):
    for s in range(0, own_ref.shape[1], CH):
        c0, c1 = pair(coef_ref, first, s)
        for k in range(n):
            outs[k][s : s + CH, :] = (
                d_ref[k0 + k, s : s + CH, :].astype(F32)
                + c0 * own_ref[k, s : s + CH, :].astype(F32)
                + c1 * other_ref[k, s : s + CH, :].astype(F32)
            ).astype(BF16)


def halve(at_ref, l, src, keep_ref, send_ref):
    bit = at_ref[1 + l]
    for j in range(keep_ref.shape[0]):
        keep_ref[j] = src[2 * j + bit]
        send_ref[j] = src[2 * j + 1 - bit].astype(BF16)


def grads_body(nb, at_ref, act_ref, gz_ref, d_ref, u_ref, keep_ref, send_ref, gb_ref, buf):
    gw, gb = 0.0, 0.0
    for k in range(nb):
        gw = gw + dot(act_ref[k], gz_ref[k], 1, 1)
        gb = gb + dot(d_ref[k], u_ref[k], 0, 0)
    gb_ref[...] = gb
    part = buf.shape[1]
    for n in range(buf.shape[0]):
        buf[n] = gw[n * part : (n + 1) * part, :]
    halve(at_ref, 0, buf, keep_ref, send_ref)


def halve_body(l, at_ref, own_ref, other_ref, keep_ref, send_ref, buf):
    buf[...] = own_ref[...] + other_ref[...].astype(F32)
    halve(at_ref, l, buf, keep_ref, send_ref)


def add_body(own_ref, other_ref, out_ref):
    out_ref[...] = own_ref[...] + other_ref[...].astype(F32)


def on_device(prev_out, prev_grad, saved_in, seq_mix, coeffs, mixer):
    n_sec, n_seq = lax.axis_size("section"), lax.axis_size("seq")
    weights = mixer[0]
    width, bw = weights.shape
    nb = width // bw
    low = n_seq // nb
    levels = n_seq.bit_length() - 1
    n_low = low.bit_length() - 1
    n_top = levels - n_low
    q = lax.axis_index("seq").astype(jnp.int32)
    at = jnp.stack([q // low] + [jnp.bitwise_and(jnp.right_shift(q, l), 1) for l in range(levels)])
    blocks = seq_mix[0]
    rows = prev_out.shape[1]
    half = nb // 2
    fwd_loc, fwd_low = 0, 4 * n_top
    adj_loc = fwd_low + 2 * n_low
    adj_low = adj_loc + 4 * n_top
    n_coef = adj_low + 2 * n_low

    def send(x, shift, flip):
        pairs = [
            (s * n_seq + i, (s + shift) % n_sec * n_seq + (i ^ flip)) for s in range(n_sec) for i in range(n_seq)
        ]
        return lax.ppermute(x, ("section", "seq"), pairs)

    def pack(x, name, deps=()):
        return call(
            functools.partial(pack_body, nb),
            [shape(bw, rows)] * nb,
            [at, x],
            [pltpu.VMEM((width, rows), BF16)],
            name,
            deps,
        )

    def unpack(pieces, name):
        return call(
            functools.partial(unpack_body, nb),
            shape(rows, width),
            [at, *pieces],
            [pltpu.VMEM((width, rows), BF16)],
            name,
            (),
            True,
        )

    def exchange(u, first, name):
        for l in range(n_low):
            other = send(u, 0, 1 << l)
            if l < n_low - 1:
                u = call(
                    functools.partial(combine_body, first + 2 * l), shape(*u.shape), [coef, u, other], (), name
                )
        return u, other

    far_first = list(range(nb - 1, -1, -1))

    fp = pack(prev_out[0], "pack_f")
    fr = {k: send(fp[k], 1, k * low) for k in far_first}
    sp = pack(saved_in[0], "pack_s", [fp[0]])
    sr = {k: send(sp[k], 0, k * low) for k in far_first[:-1]}
    sr[0] = sp[0]
    up = pack(prev_grad[0], "pack_u", [sp[0]])
    ur = {k: send(up[k], -1, k * low) for k in far_first}

    coef, w_own, w_own_t = call(
        functools.partial(prep_body, nb, n_low),
        [shape(bw, n_coef, dtype=F32), shape(bw, bw), shape(bw, bw)],
        [at, coeffs[0], weights],
        [pltpu.VMEM((width, 4 * levels), F32)],
        "prep",
        [up[0]],
    )

    def stack(pieces, name):
        return call(stack_body, shape(len(pieces), bw, rows), pieces, (), name)

    f_near = exchange(stack([fr[k] for k in range(half)], "stack_f"), fwd_low, "mix_f")
    f_far = exchange(stack([fr[k] for k in range(half, nb)], "stack_f"), fwd_low, "mix_f")
    s_near = exchange(stack([sr[k] for k in range(half)], "stack_s"), fwd_low, "mix_s")
    s_far = exchange(stack([sr[k] for k in range(half, nb)], "stack_s"), fwd_low, "mix_s")

    f_last = fwd_low + 2 * (n_low - 1)
    a_last = adj_low + 2 * (n_low - 1)
    fo = call(
        functools.partial(forward_body, nb, f_last, fwd_loc),
        [shape(bw, rows)] * nb,
        [coef, blocks, w_own_t, *f_near, *f_far, *[fr[k] for k in range(nb)]],
        [pltpu.VMEM((nb, bw, rows), BF16)],
        "layer_f",
    )
    of = {k: send(fo[k], 0, k * low) for k in far_first[:-1]}
    of[0] = fo[0]

    v_near, v_far, d, act, gz, u = call(
        functools.partial(backward_body, nb, f_last, fwd_loc, adj_loc),
        [shape(half, bw, rows), shape(nb - half, bw, rows)] + [shape(nb, bw, rows)] * 4,
        [
            coef,
            blocks,
            w_own,
            w_own_t,
            *s_near,
            *s_far,
            *[sr[k] for k in range(nb)],
            *[ur[k] for k in range(nb)],
        ],
        [pltpu.VMEM((nb, bw, rows), F32)],
        "layer_b",
    )
    od = {}
    for v, k0, n in ((v_far, half, nb - half), (v_near, 0, half)):
        own, other = exchange(v, adj_low, "mix_d")
        outs = call(
            functools.partial(finish_body, k0, n, a_last),
            [shape(bw, rows)] * n,
            [coef, own, other, d],
            (),
            "finish_d",
        )
        for k in reversed(range(n)):
            od[k0 + k] = send(outs[k], 0, (k0 + k) * low) if k0 + k else outs[k]

    part = bw // low
    keep, give, gb = call(
        functools.partial(grads_body, nb),
        [shape(low // 2, part, bw, dtype=F32), shape(low // 2, part, bw), shape(rows, rows, dtype=F32)],
        [at, act, gz, d, u],
        [pltpu.VMEM((low, part, bw), F32)],
        "weight_grads",
    )
    for l in range(n_low):
        got = send(give, 0, 1 << l)
        if l < n_low - 1:
            n = low >> l + 2
            keep, give = call(
                functools.partial(halve_body, l + 1),
                [shape(n, part, bw, dtype=F32), shape(n, part, bw)],
                [at, keep, got],
                [pltpu.VMEM((2 * n, part, bw), F32)],
                "sum_w",
            )
    grad_w = call(add_body, shape(1, part, bw, dtype=F32), [keep, got], (), "sum_w", (), True)
    for l in range(levels):
        gb = call(add_body, shape(rows, rows, dtype=F32), [gb, send(gb, 0, 1 << l)], (), "sum_b", (), l == levels - 1)
    out_f = unpack([of[k] for k in range(nb)], "unpack_f")
    out_d = unpack([od[k] for k in range(nb)], "unpack_d")
    return out_f[None], out_d[None], grad_w, gb[None]


def solution(mesh):
    placed = (
        P("section", "seq", None),
        P("section", "seq", None),
        P("section", "seq", None),
        P("section", None, None),
        P("section", None, None, None),
        P("section", None, None),
    )
    return jax.shard_map(
        on_device,
        mesh=mesh,
        in_specs=placed,
        out_specs=(
            P("section", "seq", None),
            P("section", "seq", None),
            P("section", "seq", None),
            P("section", None, None),
        ),
        check_vma=False,
    )
```

time: 302 us -> 113 us (0.37)
  waiting for transfers between devices: 227 us -> 36.9 us
  starting transfers between devices: 14.1 us -> 44.7 us
  other arithmetic: 22.3 us -> 0 us
  Pallas kernels: 0 us -> 21.5 us
  between operations: 14.3 us -> 0.95 us
  matrix products: 8.92 us -> 0 us
  local copies, waits for them, and re-layouts: 15.1 us -> 9.07 us
    ppermute x14 -> x35, waiting for transfers between devices: 120 us -> 36.9 us  [send(): return lax.ppermute(x, ('section', 'seq'), pairs)]
    reduce_scatter x1 -> x0, waiting for transfers between devices: 75.1 us -> none  [on_device(): lax.psum_scatter(weight_term, 'seq', scatter_dimension=0, tiled=True)]
    psum x1 -> x0, waiting for transfers between devices: 31.9 us -> none  [on_device(): grad_block = lax.psum(block_term, 'seq')]
    ppermute x14 -> x35, starting transfers between devices: 13.8 us -> 44.7 us  [send(): return lax.ppermute(x, ('section', 'seq'), pairs)]
    convert_element_type x13 -> x0, other arithmetic: 22.3 us -> none  [the longest x4 8.65 us: mix_adjoint(): state = jnp.where(upper_side, as_upper, as_lower).astype(jnp.bfloat16)]
    pallas_call x0 -> x27, Pallas kernels: none -> 21.5 us  [call(): pl.pallas_call(kernel, out_shape=shapes, in_specs=specs, out_specs=jax.tr...]
    dot_general x8 -> x0, matrix products: 8.92 us -> none  [the longest x1 3.68 us: on_device(): jnp.einsum('tbi,tbo->bio', act_two, gz, preferred_element_type=jnp.float32)]
    unnamed x30 -> x33, local copies, waits for them, and re-layouts: 11 us -> 8.98 us
  transfers between devices with their start and end apart: 16 -> 35, of which waited for: 13 -> 10; matrix products, arithmetic and copies ran while one was open for 10% -> 2% of each run, Pallas kernels for 0% -> 16%
where the time goes in v2:
time: 113 us
  starting transfers between devices  44.7 us (40%)
  waiting for transfers between devices  36.9 us (33%)
  Pallas kernels  21.5 us (19%)
  local copies, waits for them, and re-layouts  9.07 us (8%)
    ppermute x35, starting transfers between devices, send(): return lax.ppermute(x, ('section', 'seq'), pairs)  44.7 us
    ppermute x35, waiting for transfers between devices, send(): return lax.ppermute(x, ('section', 'seq'), pairs)  36.9 us
    pallas_call x27, Pallas kernels, call(): pl.pallas_call(kernel, out_shape=shapes, in_specs=specs, out_specs=jax.tr...  21.5 us
    unnamed x33, local copies, waits for them, and re-layouts  8.98 us
  transfers between devices with their start and end apart: 35, of which 10 were waited for; matrix products, arithmetic and copies ran while one was open for 2% of the time, Pallas kernels for 16%

profile of v2, /device:TPU:0, one launch (start us, length us, event | category | flops | bytes accessed | tf_op | source)
XLA Modules:
  0.0 113.1 jit_solution(495972157508107006)
XLA Ops:
  5.0 3.1 %collective-permute-start.11 = (bf16[448,128]{1,0:T(8,128)(2,1)S(1)}, bf16[448,128]{1,0:T(8,128)(2,1)S(1)}, u32[]{:S(2)}, u32[]{:S(2)}) collective-permute-start(bf16[448,128]{1,0:T(8,128)(2,1)S(1)} %get-tuple-element.51), channel_id=1, source_target_pairs={{0,4},{1,5},{2,6},{3,7},{4,0},{5,1},{6,2},{7,3},{8,12},{9,13},{10,... | collective-permute-start | bytes 344072 | tf_op jit(solution)/shard_map/ppermute | solution.py:250
  8.1 2.6 %collective-permute-start.14 = (bf16[448,128]{1,0:T(8,128)(2,1)S(1)}, bf16[448,128]{1,0:T(8,128)(2,1)S(1)}, u32[]{:S(2)}, u32[]{:S(2)}) collective-permute-start(bf16[448,128]{1,0:T(8,128)(2,1)S(1)} %get-tuple-element.52), channel_id=1, source_target_pairs={{0,8},{1,9},{2,10},{3,11},{4,12},{5,13},{6,14},{7,15},{8,0},{9,1},... | collective-permute-start | bytes 344072 | tf_op jit(solution)/shard_map/ppermute | solution.py:250
  11.4 8.4 %collective-permute-done.14.refs_0_.refs_10_ = bf16[448,128]{1,0:T(8,128)(2,1)S(1)} collective-permute-done((bf16[448,128]{1,0:T(8,128)(2,1)S(1)}, bf16[448,128]{1,0:T(8,128)(2,1)S(1)}, u32[]{:S(2)}, u32[]{:S(2)}) %collective-permute-start.14) | collective-permute-done | bytes 114720 | tf_op jit(solution)/shard_map/ppermute | solution.py:250
  21.5 1.8 %collective-permute-start.1 = (bf16[448,128]{1,0:T(8,128)(2,1)}, bf16[448,128]{1,0:T(8,128)(2,1)S(1)}, u32[]{:S(2)}, u32[]{:S(2)}) collective-permute-start(bf16[448,128]{1,0:T(8,128)(2,1)} %get-tuple-element.43), channel_id=1, source_target_pairs={{0,20},{1,21},{2,22},{3,23},{4,16},{5,17},{6,18},{7,19},{8,28},{9,... | collective-permute-start | bytes 344072 | tf_op jit(solution)/shard_map/ppermute | solution.py:250
  23.2 2.2 %collective-permute-start.4 = (bf16[448,128]{1,0:T(8,128)(2,1)}, bf16[448,128]{1,0:T(8,128)(2,1)S(1)}, u32[]{:S(2)}, u32[]{:S(2)}) collective-permute-start(bf16[448,128]{1,0:T(8,128)(2,1)} %get-tuple-element.44), channel_id=1, source_target_pairs={{0,24},{1,25},{2,26},{3,27},{4,28},{5,29},{6,30},{7,31},{8,16},{9,... | collective-permute-start | bytes 344072 | tf_op jit(solution)/shard_map/ppermute | solution.py:250
  30.1 2.8 %copy.10 = bf16[1,1792,448]{2,1,0:T(8,128)(2,1)S(1)} copy(bf16[1,1792,448]{1,2,0:T(8,128)(2,1)} %param.11) | data formatting | bytes 3211264 | tf_op args[5]
  34.4 4.2 %prep.1 = (f32[448,24]{1,0:T(8,128)S(1)}, bf16[448,448]{1,0:T(8,128)(2,1)S(1)}, bf16[448,448]{1,0:T(8,128)(2,1)S(1)}) custom-call(s32[5]{0:T(128)S(1)} %copy-done.8, f32[4,4,1792]{2,1,0:T(4,128)S(1)} %bitcast.20, bf16[1792,448]{1,0:T(8,128)(2,1)S(1)} %bitcast.14, bf16[448,128]{1,0:T(8,128)(2,1)S(1)} %copy-done.6), custom_call_target="tpu_custom_call" | custom-call | flops 1000 | bytes 1000 | tf_op jit(solution)/shard_map/prep/pallas_call | solution.py:46
  41.6 1.6 %collective-permute-start.13 = (bf16[2,448,128]{2,1,0:T(8,128)(2,1)S(1)}, bf16[2,448,128]{2,1,0:T(8,128)(2,1)S(1)}, u32[]{:S(2)}, u32[]{:S(2)}) collective-permute-start(bf16[2,448,128]{2,1,0:T(8,128)(2,1)S(1)} %mix_s.2.refs_4_), channel_id=1, source_target_pairs={{0,2},{1,3},{2,0},{3,1},{4,6},{5,7},{6,4},{7,5},{8,10},{9,11},{10,... | collective-permute-start | bytes 688136 | tf_op jit(solution)/shard_map/ppermute | solution.py:250
  44.5 3.1 %collective-permute-start.20 = (bf16[448,128]{1,0:T(8,128)(2,1)S(1)}, bf16[448,128]{1,0:T(8,128)(2,1)S(1)}, u32[]{:S(2)}, u32[]{:S(2)}) collective-permute-start(bf16[448,128]{1,0:T(8,128)(2,1)S(1)} %copy-done.13), channel_id=1, source_target_pairs={{0,24},{1,25},{2,26},{3,27},{4,28},{5,29},{6,30},{7,31},{8,16},{9,... | collective-permute-start | bytes 344072 | tf_op jit(solution)/shard_map/ppermute | solution.py:250
  49.6 6.3 %collective-permute-done.20.refs_14_ = bf16[448,128]{1,0:T(8,128)(2,1)S(1)} collective-permute-done((bf16[448,128]{1,0:T(8,128)(2,1)S(1)}, bf16[448,128]{1,0:T(8,128)(2,1)S(1)}, u32[]{:S(2)}, u32[]{:S(2)}) %collective-permute-start.20) | collective-permute-done | bytes 114720 | tf_op jit(solution)/shard_map/ppermute | solution.py:250
  55.9 3.6 %layer_b.1 = (bf16[2,448,128]{2,1,0:T(8,128)(2,1)S(1)}, bf16[2,448,128]{2,1,0:T(8,128)(2,1)S(1)}, bf16[4,448,128]{2,1,0:T(8,128)(2,1)S(1)}, bf16[4,448,128]{2,1,...) custom-call(f32[448,24]{1,0:T(8,128)S(1)} %get-tuple-element.41.refs_0_, ...), custom_call_target="tpu_custom_call" | custom-call | flops 1000 | bytes 1000 | tf_op jit(solution)/shard_map/layer_b/pallas_call | solution.py:46
  60.4 1.6 %collective-permute-start.3 = (bf16[2,448,128]{2,1,0:T(8,128)(2,1)S(1)}, bf16[2,448,128]{2,1,0:T(8,128)(2,1)S(1)}, u32[]{:S(2)}, u32[]{:S(2)}) collective-permute-start(bf16[2,448,128]{2,1,0:T(8,128)(2,1)S(1)} %mix_f.2.refs_3_), channel_id=1, source_target_pairs={{0,2},{1,3},{2,0},{3,1},{4,6},{5,7},{6,4},{7,5},{8,10},{9,11},{10,... | collective-permute-start | bytes 688136 | tf_op jit(solution)/shard_map/ppermute | solution.py:250
  63.0 1.6 %collective-permute-start.23 = (bf16[2,448,128]{2,1,0:T(8,128)(2,1)S(1)}, bf16[2,448,128]{2,1,0:T(8,128)(2,1)S(1)}, u32[]{:S(2)}, u32[]{:S(2)}) collective-permute-start(bf16[2,448,128]{2,1,0:T(8,128)(2,1)S(1)} %mix_d.2.refs_1_), channel_id=1, source_target_pairs={{0,2},{1,3},{2,0},{3,1},{4,6},{5,7},{6,4},{7,5},{8,10},{9,11},{10,... | collective-permute-start | bytes 688136 | tf_op jit(solution)/shard_map/ppermute | solution.py:250
  70.4 3.4 %collective-permute-done.7.refs_6_ = bf16[2,448,128]{2,1,0:T(8,128)(2,1)S(1)} collective-permute-done((bf16[2,448,128]{2,1,0:T(8,128)(2,1)S(1)}, bf16[2,448,128]{2,1,0:T(8,128)(2,1)S(1)}, u32[]{:S(2)}, u32[]{:S(2)}) %collective-permute-start.7) | collective-permute-done | bytes 229408 | tf_op jit(solution)/shard_map/ppermute | solution.py:250
  73.8 1.7 %layer_f.1 = (bf16[448,128]{1,0:T(8,128)(2,1)S(1)}, bf16[448,128]{1,0:T(8,128)(2,1)S(1)}, bf16[448,128]{1,0:T(8,128)(2,1)S(1)}, bf16[448,128]{1,0:T(8,128)(2,1)S(1)}) custom-call(f32[448,24]{1,0:T(8,128)S(1)} %get-tuple-element.41.refs_0_, bf16[128,128]{1,0:T(8,128)(2,1)S(1)} %bitcast.19, bf16[448,448]{1,0:T(8,128)(2,1)S(1)} %get-tuple-element.42.refs_2_.refs_3_, ...), custom_call_target="tpu_custom_call" | custom-call | flops 1000 | bytes 1000 | tf_op jit(solution)/shard_map/layer_f/pallas_call | solution.py:46
  75.5 1.8 %collective-permute-start.8 = (bf16[448,128]{1,0:T(8,128)(2,1)S(1)}, bf16[448,128]{1,0:T(8,128)(2,1)S(1)}, u32[]{:S(2)}, u32[]{:S(2)}) collective-permute-start(bf16[448,128]{1,0:T(8,128)(2,1)S(1)} %get-tuple-element.47), channel_id=1, source_target_pairs={{0,4},{1,5},{2,6},{3,7},{4,0},{5,1},{6,2},{7,3},{8,12},{9,13},{10,... | collective-permute-start | bytes 344072 | tf_op jit(solution)/shard_map/ppermute | solution.py:250
  77.3 7.3 %collective-permute-done.32.refs_1_ = f32[128,128]{1,0:T(8,128)S(1)} collective-permute-done((f32[128,128]{1,0:T(8,128)S(1)}, f32[128,128]{1,0:T(8,128)S(1)}, u32[]{:S(2)}, u32[]{:S(2)}) %collective-permute-start.32) | collective-permute-done | bytes 65568 | tf_op jit(solution)/shard_map/ppermute | solution.py:250
  84.6 2.2 %collective-permute-start.9 = (bf16[448,128]{1,0:T(8,128)(2,1)S(1)}, bf16[448,128]{1,0:T(8,128)(2,1)S(1)}, u32[]{:S(2)}, u32[]{:S(2)}) collective-permute-start(bf16[448,128]{1,0:T(8,128)(2,1)S(1)} %get-tuple-element.48), channel_id=1, source_target_pairs={{0,8},{1,9},{2,10},{3,11},{4,12},{5,13},{6,14},{7,15},{8,0},{9,1},... | collective-permute-start | bytes 344072 | tf_op jit(solution)/shard_map/ppermute | solution.py:250
  88.9 2.1 %collective-permute-start.24 = (bf16[448,128]{1,0:T(8,128)(2,1)S(1)}, bf16[448,128]{1,0:T(8,128)(2,1)S(1)}, u32[]{:S(2)}, u32[]{:S(2)}) collective-permute-start(bf16[448,128]{1,0:T(8,128)(2,1)S(1)} %get-tuple-element.60), channel_id=1, source_target_pairs={{0,4},{1,5},{2,6},{3,7},{4,0},{5,1},{6,2},{7,3},{8,12},{9,13},{10,... | collective-permute-start | bytes 344072 | tf_op jit(solution)/shard_map/ppermute | solution.py:250
  90.9 4.7 %collective-permute-done.9.refs_3_ = bf16[448,128]{1,0:T(8,128)(2,1)S(1)} collective-permute-done((bf16[448,128]{1,0:T(8,128)(2,1)S(1)}, bf16[448,128]{1,0:T(8,128)(2,1)S(1)}, u32[]{:S(2)}, u32[]{:S(2)}) %collective-permute-start.9) | collective-permute-done | bytes 114720 | tf_op jit(solution)/shard_map/ppermute | solution.py:250
  95.6 2.4 %collective-permute-start.28 = (bf16[448,128]{1,0:T(8,128)(2,1)S(1)}, bf16[448,128]{1,0:T(8,128)(2,1)S(1)}, u32[]{:S(2)}, u32[]{:S(2)}) collective-permute-start(bf16[448,128]{1,0:T(8,128)(2,1)S(1)} %get-tuple-element.63), channel_id=1, source_target_pairs={{0,12},{1,13},{2,14},{3,15},{4,8},{5,9},{6,10},{7,11},{8,4},{9,5},... | collective-permute-start | bytes 344072 | tf_op jit(solution)/shard_map/ppermute | solution.py:250
  98.6 1.6 %collective-permute-start.30 = (bf16[1,112,448]{2,1,0:T(8,128)(2,1)S(1)}, bf16[1,112,448]{2,1,0:T(8,128)(2,1)S(1)}, u32[]{:S(2)}, u32[]{:S(2)}) collective-permute-start(bf16[1,112,448]{2,1,0:T(8,128)(2,1)S(1)} %get-tuple-element.70), channel_id=1, source_target_pairs={{0,2},{1,3},{2,0},{3,1},{4,6},{5,7},{6,4},{7,5},{8,10},{9,11},{10,... | collective-permute-start | bytes 301064 | tf_op jit(solution)/shard_map/ppermute | solution.py:250
  100.2 4.9 %collective-permute-start.34 = (f32[128,128]{1,0:T(8,128)S(1)}, f32[128,128]{1,0:T(8,128)S(1)}, u32[]{:S(2)}, u32[]{:S(2)}) collective-permute-start(f32[128,128]{1,0:T(8,128)S(1)} %sum_b.6.refs_0_), channel_id=1, source_target_pairs={{0,8},{1,9},{2,10},{3,11},{4,12},{5,13},{6,14},{7,15},{8,0},{9,1},... | collective-permute-start | bytes 196616 | tf_op jit(solution)/shard_map/ppermute | solution.py:250
  106.6 3.7 %collective-permute-done.34.refs_1_ = f32[128,128]{1,0:T(8,128)S(1)} collective-permute-done((f32[128,128]{1,0:T(8,128)S(1)}, f32[128,128]{1,0:T(8,128)S(1)}, u32[]{:S(2)}, u32[]{:S(2)}) %collective-permute-start.34) | collective-permute-done | bytes 65568 | tf_op jit(solution)/shard_map/ppermute | solution.py:250
  (107 shorter events, 33.8 us)
Async XLA Ops:
  8.1 11.7 %collective-permute-start.14 = (bf16[448,128]{1,0:T(8,128)(2,1)S(1)}, bf16[448,128]{1,0:T(8,128)(2,1)S(1)}, u32[]{:S(2)}, u32[]{:S(2)}) collective-permute-start(bf16[448,128]{1,0:T(8,128)(2,1)S(1)} %get-tuple-element.52), channel_id=1, source_target_pairs={{0,8},{1,9},{2,10},{3,11},{4,12},{5,13},{6,14},{7,15},{8,0},{9,1},... | collective-permute-start | bytes 344072 | tf_op jit(solution)/shard_map/ppermute | solution.py:250
  11.3 14.1 %collective-permute-start.12 = (bf16[2,448,128]{2,1,0:T(8,128)(2,1)S(1)}, bf16[2,448,128]{2,1,0:T(8,128)(2,1)S(1)}, u32[]{:S(2)}, u32[]{:S(2)}) collective-permute-start(bf16[2,448,128]{2,1,0:T(8,128)(2,1)S(1)} %stack_s.2.refs_1_), channel_id=1, source_target_pairs={{0,1},{1,0},{2,3},{3,2},{4,5},{5,4},{6,7},{7,6},{8,9},{9,8},{10,11... | collective-permute-start | bytes 688136 | tf_op jit(solution)/shard_map/ppermute | solution.py:250
  19.8 19.0 %collective-permute-start.16 = (bf16[2,448,128]{2,1,0:T(8,128)(2,1)S(1)}, bf16[2,448,128]{2,1,0:T(8,128)(2,1)}, u32[]{:S(2)}, u32[]{:S(2)}) collective-permute-start(bf16[2,448,128]{2,1,0:T(8,128)(2,1)S(1)} %stack_s.3.refs_1_), channel_id=1, source_target_pairs={{0,1},{1,0},{2,3},{3,2},{4,5},{5,4},{6,7},{7,6},{8,9},{9,8},{10,11... | collective-permute-start | bytes 688136 | tf_op jit(solution)/shard_map/ppermute | solution.py:250
  19.9 21.7 %collective-permute-start = (bf16[448,128]{1,0:T(8,128)(2,1)}, bf16[448,128]{1,0:T(8,128)(2,1)S(1)}, u32[]{:S(2)}, u32[]{:S(2)}) collective-permute-start(bf16[448,128]{1,0:T(8,128)(2,1)} %get-tuple-element.38.refs_2_), channel_id=1, source_target_pairs={{0,16},{1,17},{2,18},{3,19},{4,20},{5,21},{6,22},{7,23},{8,24},{9,... | collective-permute-start | bytes 344072 | tf_op jit(solution)/shard_map/ppermute | solution.py:250
  21.5 21.7 %collective-permute-start.1 = (bf16[448,128]{1,0:T(8,128)(2,1)}, bf16[448,128]{1,0:T(8,128)(2,1)S(1)}, u32[]{:S(2)}, u32[]{:S(2)}) collective-permute-start(bf16[448,128]{1,0:T(8,128)(2,1)} %get-tuple-element.43), channel_id=1, source_target_pairs={{0,20},{1,21},{2,22},{3,23},{4,16},{5,17},{6,18},{7,19},{8,28},{9,... | collective-permute-start | bytes 344072 | tf_op jit(solution)/shard_map/ppermute | solution.py:250
  23.2 20.5 %collective-permute-start.4 = (bf16[448,128]{1,0:T(8,128)(2,1)}, bf16[448,128]{1,0:T(8,128)(2,1)S(1)}, u32[]{:S(2)}, u32[]{:S(2)}) collective-permute-start(bf16[448,128]{1,0:T(8,128)(2,1)} %get-tuple-element.44), channel_id=1, source_target_pairs={{0,24},{1,25},{2,26},{3,27},{4,28},{5,29},{6,30},{7,31},{8,16},{9,... | collective-permute-start | bytes 344072 | tf_op jit(solution)/shard_map/ppermute | solution.py:250
  25.4 19.1 %collective-permute-start.5 = (bf16[448,128]{1,0:T(8,128)(2,1)}, bf16[448,128]{1,0:T(8,128)(2,1)S(1)}, u32[]{:S(2)}, u32[]{:S(2)}) collective-permute-start(bf16[448,128]{1,0:T(8,128)(2,1)} %get-tuple-element.45), channel_id=1, source_target_pairs={{0,28},{1,29},{2,30},{3,31},{4,24},{5,25},{6,26},{7,27},{8,20},{9,... | collective-permute-start | bytes 344072 | tf_op jit(solution)/shard_map/ppermute | solution.py:250
  41.6 14.3 %collective-permute-start.13 = (bf16[2,448,128]{2,1,0:T(8,128)(2,1)S(1)}, bf16[2,448,128]{2,1,0:T(8,128)(2,1)S(1)}, u32[]{:S(2)}, u32[]{:S(2)}) collective-permute-start(bf16[2,448,128]{2,1,0:T(8,128)(2,1)S(1)} %mix_s.2.refs_4_), channel_id=1, source_target_pairs={{0,2},{1,3},{2,0},{3,1},{4,6},{5,7},{6,4},{7,5},{8,10},{9,11},{10,... | collective-permute-start | bytes 688136 | tf_op jit(solution)/shard_map/ppermute | solution.py:250
  43.2 12.7 %collective-permute-start.17 = (bf16[2,448,128]{2,1,0:T(8,128)(2,1)S(1)}, bf16[2,448,128]{2,1,0:T(8,128)(2,1)S(1)}, u32[]{:S(2)}, u32[]{:S(2)}) collective-permute-start(bf16[2,448,128]{2,1,0:T(8,128)(2,1)S(1)} %mix_s.3.refs_6_), channel_id=1, source_target_pairs={{0,2},{1,3},{2,0},{3,1},{4,6},{5,7},{6,4},{7,5},{8,10},{9,11},{10,... | collective-permute-start | bytes 688136 | tf_op jit(solution)/shard_map/ppermute | solution.py:250
  44.5 11.3 %collective-permute-start.20 = (bf16[448,128]{1,0:T(8,128)(2,1)S(1)}, bf16[448,128]{1,0:T(8,128)(2,1)S(1)}, u32[]{:S(2)}, u32[]{:S(2)}) collective-permute-start(bf16[448,128]{1,0:T(8,128)(2,1)S(1)} %copy-done.13), channel_id=1, source_target_pairs={{0,24},{1,25},{2,26},{3,27},{4,28},{5,29},{6,30},{7,31},{8,16},{9,... | collective-permute-start | bytes 344072 | tf_op jit(solution)/shard_map/ppermute | solution.py:250
  49.6 10.6 %collective-permute-start.2 = (bf16[2,448,128]{2,1,0:T(8,128)(2,1)S(1)}, bf16[2,448,128]{2,1,0:T(8,128)(2,1)S(1)}, u32[]{:S(2)}, u32[]{:S(2)}) collective-permute-start(bf16[2,448,128]{2,1,0:T(8,128)(2,1)S(1)} %stack_f.2.refs_1_), channel_id=1, source_target_pairs={{0,1},{1,0},{2,3},{3,2},{4,5},{5,4},{6,7},{7,6},{8,9},{9,8},{10,11... | collective-permute-start | bytes 688136 | tf_op jit(solution)/shard_map/ppermute | solution.py:250
  62.2 11.6 %collective-permute-start.7 = (bf16[2,448,128]{2,1,0:T(8,128)(2,1)S(1)}, bf16[2,448,128]{2,1,0:T(8,128)(2,1)S(1)}, u32[]{:S(2)}, u32[]{:S(2)}) collective-permute-start(bf16[2,448,128]{2,1,0:T(8,128)(2,1)S(1)} %mix_f.3.refs_5_), channel_id=1, source_target_pairs={{0,2},{1,3},{2,0},{3,1},{4,6},{5,7},{6,4},{7,5},{8,10},{9,11},{10,... | collective-permute-start | bytes 688136 | tf_op jit(solution)/shard_map/ppermute | solution.py:250
  63.0 23.8 %collective-permute-start.23 = (bf16[2,448,128]{2,1,0:T(8,128)(2,1)S(1)}, bf16[2,448,128]{2,1,0:T(8,128)(2,1)S(1)}, u32[]{:S(2)}, u32[]{:S(2)}) collective-permute-start(bf16[2,448,128]{2,1,0:T(8,128)(2,1)S(1)} %mix_d.2.refs_1_), channel_id=1, source_target_pairs={{0,2},{1,3},{2,0},{3,1},{4,6},{5,7},{6,4},{7,5},{8,10},{9,11},{10,... | collective-permute-start | bytes 688136 | tf_op jit(solution)/shard_map/ppermute | solution.py:250
  64.8 23.5 %collective-permute-start.26 = (bf16[2,448,128]{2,1,0:T(8,128)(2,1)S(1)}, bf16[2,448,128]{2,1,0:T(8,128)(2,1)S(1)}, u32[]{:S(2)}, u32[]{:S(2)}) collective-permute-start(bf16[2,448,128]{2,1,0:T(8,128)(2,1)S(1)} %mix_d.3.refs_1_), channel_id=1, source_target_pairs={{0,2},{1,3},{2,0},{3,1},{4,6},{5,7},{6,4},{7,5},{8,10},{9,11},{10,... | collective-permute-start | bytes 688136 | tf_op jit(solution)/shard_map/ppermute | solution.py:250
  68.1 27.5 %collective-permute-start.29 = (bf16[2,112,448]{2,1,0:T(8,128)(2,1)S(1)}, bf16[2,112,448]{2,1,0:T(8,128)(2,1)S(1)}, u32[]{:S(2)}, u32[]{:S(2)}) collective-permute-start(bf16[2,112,448]{2,1,0:T(8,128)(2,1)S(1)} %get-tuple-element.68), channel_id=1, source_target_pairs={{0,1},{1,0},{2,3},{3,2},{4,5},{5,4},{6,7},{7,6},{8,9},{9,8},{10,11... | collective-permute-start | bytes 602120 | tf_op jit(solution)/shard_map/ppermute | solution.py:250
  68.9 15.7 %collective-permute-start.32 = (f32[128,128]{1,0:T(8,128)S(1)}, f32[128,128]{1,0:T(8,128)S(1)}, u32[]{:S(2)}, u32[]{:S(2)}) collective-permute-start(f32[128,128]{1,0:T(8,128)S(1)} %sum_b.4.refs_0_), channel_id=1, source_target_pairs={{0,2},{1,3},{2,0},{3,1},{4,6},{5,7},{6,4},{7,5},{8,10},{9,11},{10,... | collective-permute-start | bytes 196616 | tf_op jit(solution)/shard_map/ppermute | solution.py:250
  75.5 13.4 %collective-permute-start.8 = (bf16[448,128]{1,0:T(8,128)(2,1)S(1)}, bf16[448,128]{1,0:T(8,128)(2,1)S(1)}, u32[]{:S(2)}, u32[]{:S(2)}) collective-permute-start(bf16[448,128]{1,0:T(8,128)(2,1)S(1)} %get-tuple-element.47), channel_id=1, source_target_pairs={{0,4},{1,5},{2,6},{3,7},{4,0},{5,1},{6,2},{7,3},{8,12},{9,13},{10,... | collective-permute-start | bytes 344072 | tf_op jit(solution)/shard_map/ppermute | solution.py:250
  84.6 11.0 %collective-permute-start.9 = (bf16[448,128]{1,0:T(8,128)(2,1)S(1)}, bf16[448,128]{1,0:T(8,128)(2,1)S(1)}, u32[]{:S(2)}, u32[]{:S(2)}) collective-permute-start(bf16[448,128]{1,0:T(8,128)(2,1)S(1)} %get-tuple-element.48), channel_id=1, source_target_pairs={{0,8},{1,9},{2,10},{3,11},{4,12},{5,13},{6,14},{7,15},{8,0},{9,1},... | collective-permute-start | bytes 344072 | tf_op jit(solution)/shard_map/ppermute | solution.py:250
  86.8 13.4 %collective-permute-start.10 = (bf16[448,128]{1,0:T(8,128)(2,1)S(1)}, bf16[448,128]{1,0:T(8,128)(2,1)S(1)}, u32[]{:S(2)}, u32[]{:S(2)}) collective-permute-start(bf16[448,128]{1,0:T(8,128)(2,1)S(1)} %get-tuple-element.49), channel_id=1, source_target_pairs={{0,12},{1,13},{2,14},{3,15},{4,8},{5,9},{6,10},{7,11},{8,4},{9,5},... | collective-permute-start | bytes 344072 | tf_op jit(solution)/shard_map/ppermute | solution.py:250
  88.3 10.3 %collective-permute-start.33 = (f32[128,128]{1,0:T(8,128)S(1)}, f32[128,128]{1,0:T(8,128)S(1)}, u32[]{:S(2)}, u32[]{:S(2)}) collective-permute-start(f32[128,128]{1,0:T(8,128)S(1)} %sum_b.5.refs_0_), channel_id=1, source_target_pairs={{0,4},{1,5},{2,6},{3,7},{4,0},{5,1},{6,2},{7,3},{8,12},{9,13},{10,... | collective-permute-start | bytes 196616 | tf_op jit(solution)/shard_map/ppermute | solution.py:250
  88.9 22.7 %collective-permute-start.24 = (bf16[448,128]{1,0:T(8,128)(2,1)S(1)}, bf16[448,128]{1,0:T(8,128)(2,1)S(1)}, u32[]{:S(2)}, u32[]{:S(2)}) collective-permute-start(bf16[448,128]{1,0:T(8,128)(2,1)S(1)} %get-tuple-element.60), channel_id=1, source_target_pairs={{0,4},{1,5},{2,6},{3,7},{4,0},{5,1},{6,2},{7,3},{8,12},{9,13},{10,... | collective-permute-start | bytes 344072 | tf_op jit(solution)/shard_map/ppermute | solution.py:250
  95.6 16.0 %collective-permute-start.27 = (bf16[448,128]{1,0:T(8,128)(2,1)S(1)}, bf16[448,128]{1,0:T(8,128)(2,1)S(1)}, u32[]{:S(2)}, u32[]{:S(2)}) collective-permute-start(bf16[448,128]{1,0:T(8,128)(2,1)S(1)} %get-tuple-element.62), channel_id=1, source_target_pairs={{0,8},{1,9},{2,10},{3,11},{4,12},{5,13},{6,14},{7,15},{8,0},{9,1},... | collective-permute-start | bytes 344072 | tf_op jit(solution)/shard_map/ppermute | solution.py:250
  95.6 16.0 %collective-permute-start.28 = (bf16[448,128]{1,0:T(8,128)(2,1)S(1)}, bf16[448,128]{1,0:T(8,128)(2,1)S(1)}, u32[]{:S(2)}, u32[]{:S(2)}) collective-permute-start(bf16[448,128]{1,0:T(8,128)(2,1)S(1)} %get-tuple-element.63), channel_id=1, source_target_pairs={{0,12},{1,13},{2,14},{3,15},{4,8},{5,9},{6,10},{7,11},{8,4},{9,5},... | collective-permute-start | bytes 344072 | tf_op jit(solution)/shard_map/ppermute | solution.py:250
  98.6 12.3 %collective-permute-start.30 = (bf16[1,112,448]{2,1,0:T(8,128)(2,1)S(1)}, bf16[1,112,448]{2,1,0:T(8,128)(2,1)S(1)}, u32[]{:S(2)}, u32[]{:S(2)}) collective-permute-start(bf16[1,112,448]{2,1,0:T(8,128)(2,1)S(1)} %get-tuple-element.70), channel_id=1, source_target_pairs={{0,2},{1,3},{2,0},{3,1},{4,6},{5,7},{6,4},{7,5},{8,10},{9,11},{10,... | collective-permute-start | bytes 301064 | tf_op jit(solution)/shard_map/ppermute | solution.py:250
  (27 other events, 187.0 us)

commit v3 on v2

v3 whole, which is shorter than its diff:
```python
import functools

import jax
import jax.numpy as jnp
from jax import lax
from jax.experimental import pallas as pl
from jax.experimental.pallas import tpu as pltpu
from jax.sharding import PartitionSpec as P

F32 = jnp.float32
BF16 = jnp.bfloat16
LANES = 128
CH = 64
DECLARED = 8_000_000_000


def dot(a, b, ca, cb):
    return lax.dot_general(a, b, (((ca,), (cb,)), ((), ())), preferred_element_type=F32)


def near_memory(x):
    return pltpu.with_memory_space_constraint(x, pltpu.VMEM)


def call(body, outs, ins, scratch=(), name=None, deps=(), in_hbm=(), out_hbm=False, declared=0):
    n_in, n_dep = len(ins) + len(in_hbm), len(deps)

    def kernel(*refs):
        body(*refs[:n_in], *refs[n_in + n_dep :])

    specs = []
    args = []
    for a in ins:
        if a.dtype == jnp.int32:
            specs.append(pl.BlockSpec(memory_space=pltpu.SMEM))
            args.append(a)
        else:
            specs.append(pl.BlockSpec(memory_space=pltpu.VMEM))
            args.append(near_memory(a))
    for a in in_hbm:
        specs.append(pl.BlockSpec(memory_space=pltpu.HBM))
        args.append(pltpu.with_memory_space_constraint(a, pltpu.HBM))
    for a in deps:
        specs.append(pl.BlockSpec(memory_space=pl.ANY))
        args.append(a)
    shapes = jax.tree.map(lambda o: pltpu.VMEM(o.shape, o.dtype), outs)
    if out_hbm:
        shapes = [shapes[0], *[pltpu.HBM(o.shape, o.dtype) for o in outs[1:]]]
    return pl.pallas_call(
        kernel,
        out_shape=shapes,
        in_specs=specs,
        out_specs=jax.tree.map(lambda _: pl.BlockSpec(memory_space=pltpu.VMEM), outs),
        scratch_shapes=scratch,
        name=name,
        compiler_params=pltpu.CompilerParams(vmem_limit_bytes=6 << 20),
        cost_estimate=pl.CostEstimate(flops=declared, bytes_accessed=0, transcendentals=0),
    )(*args)


def shape(*dims, dtype=BF16):
    return jax.ShapeDtypeStruct(dims, dtype)


def pack_body(nb, at_ref, x_ref, *refs):
    outs, buf = refs[:nb], refs[nb]
    width = x_ref.shape[1]
    bw = width // nb
    for j in range(0, width, LANES):
        buf[j : j + LANES, :] = x_ref[:, j : j + LANES].T
    for k in range(nb):
        start = pl.multiple_of(jnp.bitwise_xor(at_ref[0], k) * bw, 16)
        outs[k][...] = buf[pl.ds(start, bw), :]


def open_body(nb, at_ref, x_hbm, *refs):
    n = (len(refs) - nb - 3) // 2
    hbm, outs, held = refs[:n], refs[n : n + nb], refs[n + nb : 2 * n + nb]
    x_ref, buf, sems = refs[2 * n + nb :]
    copies = [pltpu.make_async_copy(x_hbm, x_ref, sems.at[0])]
    copies += [pltpu.make_async_copy(a, b, sems.at[1 + i]) for i, (a, b) in enumerate(zip(hbm, held))]
    for c in copies:
        c.start()
    copies[0].wait()
    pack_body(nb, at_ref, x_ref, *outs, buf)
    for c in copies[1:]:
        c.wait()


def unpack_body(nb, at_ref, *refs):
    ins, token, out, buf = refs[:nb], refs[nb], refs[nb + 1], refs[nb + 2]
    width = out.shape[1]
    bw = width // nb
    for k in range(nb):
        start = pl.multiple_of(jnp.bitwise_xor(at_ref[0], k) * bw, 16)
        buf[pl.ds(start, bw), :] = ins[k][...]
    for j in range(0, width, LANES):
        out[:, j : j + LANES] = buf[j : j + LANES, :].T
    token[...] = jnp.zeros_like(token)


def prep_body(nb, n_low, at_ref, c_ref, w_ref, coef_ref, wo_ref, wt_ref, buf, table):
    levels, _, width = c_ref.shape
    bw = width // nb
    for b in range(nb):

        @pl.when(at_ref[0] == b)
        def _():
            cols = slice(b * bw, (b + 1) * bw)
            for l in range(levels):
                buf[4 * l : 4 * l + 4, :] = c_ref[l, :, cols]
            wt = w_ref[:, cols]
            wt_ref[...] = wt
            wo_ref[...] = wt.T

    row = 0
    for lower, upper, span in (
        ((0, 1, 3, 2), (3, 2, 0, 1), range(n_low, levels)),
        ((0, 1), (3, 2), range(n_low)),
        ((0, 2, 3, 1), (3, 1, 0, 2), range(n_low, levels)),
        ((0, 2), (3, 1), range(n_low)),
    ):
        for l in span:
            for a, b in zip(lower, upper):
                high = at_ref[1 + l] == 1
                i, j = 4 * l + b, 4 * l + a
                table[row : row + 1, :] = jnp.where(high, buf[i : i + 1, :], buf[j : j + 1, :])
                row += 1
    coef_ref[...] = table[...].T


def copy_body(*refs):
    n = len(refs) // 2
    for k in range(n):
        refs[n + k][...] = refs[k][...]


def mark_body(out_ref):
    out_ref[...] = jnp.zeros_like(out_ref)


def join_body(*refs):
    outs = refs[len(refs) // 3 * 2 :]
    for k, out in enumerate(outs):
        out[0] = refs[k][...]
        out[1] = refs[len(outs) + k][...]


def stack_body(*refs):
    out = refs[-1]
    for k, r in enumerate(refs[:-1]):
        out[k] = r[...]


def pair(coef_ref, first, s):
    return (coef_ref[s : s + CH, first : first + 1], coef_ref[s : s + CH, first + 1 : first + 2])


def combine_body(first, coef_ref, own_ref, other_ref, out_ref):
    for s in range(0, out_ref.shape[1], CH):
        c0, c1 = pair(coef_ref, first, s)
        for k in range(out_ref.shape[0]):
            own = own_ref[k, s : s + CH, :].astype(F32)
            other = other_ref[k, s : s + CH, :].astype(F32)
            out_ref[k, s : s + CH, :] = (c0 * own + c1 * other).astype(BF16)


def local_levels(vals, coef, first):
    vals = list(vals)
    nb = len(vals)
    for j in range(nb.bit_length() - 1):
        c = [coef[:, first + 4 * j + i : first + 4 * j + i + 1] for i in range(4)]
        for k in range(nb):
            if not k >> j & 1:
                m = k | 1 << j
                a, b = vals[k], vals[m]
                vals[k] = c[0] * a + c[1] * b
                vals[m] = c[2] * b + c[3] * a
    return vals


def finish_state(first, loc, coef_ref, chunks, u_ref):
    for s in range(0, u_ref.shape[1], CH):
        c0, c1 = pair(coef_ref, first, s)
        vals = []
        for own_ref, other_ref in chunks:
            for k in range(own_ref.shape[0]):
                vals.append(c0 * own_ref[k, s : s + CH, :].astype(F32) + c1 * other_ref[k, s : s + CH, :].astype(F32))
        vals = local_levels(vals, coef_ref[s : s + CH, :], loc)
        for k, v in enumerate(vals):
            u_ref[k, s : s + CH, :] = v.astype(BF16)


def mix_rows(u_ref, b_ref, ins, act_ref):
    for k, r in enumerate(ins):
        lanes = slice(k * LANES, (k + 1) * LANES)
        act_ref[:, lanes] = (r[...].astype(F32) + dot(u_ref[k], b_ref[...], 1, 1)).astype(BF16)


def forward_body(nb, first, loc, coef_ref, b_ref, wt_ref, own_ref, other_ref, *refs):
    ins, outs, u_ref, act_ref = refs[:nb], refs[nb : 2 * nb], refs[2 * nb], refs[2 * nb + 1]
    finish_state(first, loc, coef_ref, ((own_ref, other_ref),), u_ref)
    mix_rows(u_ref, b_ref, ins, act_ref)
    act = act_ref[...]
    pre = dot(wt_ref[...], act, 1, 0)
    out = (act.astype(F32) + pre * jax.nn.sigmoid(pre)).astype(BF16)
    for k in range(nb):
        outs[k][...] = out[:, k * LANES : (k + 1) * LANES]


def backward_body(nb, first, loc, adj, coef_ref, b_ref, w_ref, wt_ref, own_ref, other_ref, *refs):
    ins, ups = refs[:nb], refs[nb : 2 * nb]
    v0_ref, v1_ref, d_ref, act_ref, gz_ref, u_ref, v_ref, up_ref = refs[2 * nb :]
    finish_state(first, loc, coef_ref, ((own_ref, other_ref),), u_ref)
    mix_rows(u_ref, b_ref, ins, act_ref)
    for k in range(nb):
        up_ref[:, k * LANES : (k + 1) * LANES] = ups[k][...]
    pre = dot(wt_ref[...], act_ref[...], 1, 0)
    sig = jax.nn.sigmoid(pre)
    gz_ref[...] = (up_ref[...].astype(F32) * (sig * (1.0 + pre * (1.0 - sig)))).astype(BF16)
    back = dot(w_ref[...], gz_ref[...], 1, 0)
    d = (up_ref[...].astype(F32) + back).astype(BF16)
    for k in range(nb):
        d_ref[k] = d[:, k * LANES : (k + 1) * LANES]
        v_ref[k] = dot(d_ref[k], b_ref[...], 1, 0)
    half = nb // 2
    for s in range(0, d_ref.shape[1], CH):
        vals = local_levels([v_ref[k, s : s + CH, :] for k in range(nb)], coef_ref[s : s + CH, :], adj)
        for k in range(half):
            v0_ref[k, s : s + CH, :] = vals[k].astype(BF16)
            v1_ref[k, s : s + CH, :] = vals[half + k].astype(BF16)


def finish_body(k0, n, first, coef_ref, own_ref, other_ref, d_ref, *outs):
    for s in range(0, own_ref.shape[1], CH):
        c0, c1 = pair(coef_ref, first, s)
        for k in range(n):
            outs[k][s : s + CH, :] = (
                d_ref[k0 + k, s : s + CH, :].astype(F32)
                + c0 * own_ref[k, s : s + CH, :].astype(F32)
                + c1 * other_ref[k, s : s + CH, :].astype(F32)
            ).astype(BF16)


def halve(at_ref, l, src, keep_ref, send_ref):
    bit = at_ref[1 + l]
    for j in range(keep_ref.shape[0]):
        keep_ref[j] = src[2 * j + bit]
        send_ref[j] = src[2 * j + 1 - bit].astype(BF16)


def riders(n, rows, part, bw):
    places = []
    for i, r in enumerate(range(0, rows, part)):
        places.append((n + i // (bw // LANES), i % (bw // LANES) * LANES, r, min(part, rows - r)))
    return places, places[-1][0] + 1 - n


def grads_body(nb, act_ref, gz_ref, d_ref, u_ref, gw_ref, gb_ref):
    gw, gb = dot(act_ref[...], gz_ref[...], 1, 1), 0.0
    for k in range(nb):
        gb = gb + dot(d_ref[k], u_ref[k], 0, 0)
    gb_ref[...] = gb.astype(BF16)
    part = gw_ref.shape[1]
    for n in range(gw_ref.shape[0]):
        gw_ref[n] = gw[n * part : (n + 1) * part, :]


def ride(own, send_ref, n):
    for m, lane, r, count in riders(n, own.shape[0], send_ref.shape[1], send_ref.shape[2])[0]:
        send_ref[m, :count, lane : lane + LANES] = own[r : r + count, :].astype(BF16)


def first_half_body(at_ref, gw_ref, gb_ref, keep_ref, send_ref):
    halve(at_ref, 0, gw_ref, keep_ref, send_ref)
    ride(gb_ref, send_ref, keep_ref.shape[0])


def sum_riders(n, own_ref, other_ref, out_ref):
    rows, part, bw = own_ref.shape[0], other_ref.shape[1], other_ref.shape[2]
    for m, lane, r, count in riders(n, rows, part, bw)[0]:
        out_ref[r : r + count, :] = (
            own_ref[r : r + count, :].astype(F32) + other_ref[m, :count, lane : lane + LANES].astype(F32)
        ).astype(out_ref.dtype)


def halve_body(l, at_ref, own_ref, other_ref, gb_ref, keep_ref, send_ref, sum_ref, buf, wide):
    n = own_ref.shape[0]
    for j in range(n):
        buf[j] = own_ref[j] + other_ref[j].astype(F32)
    halve(at_ref, l, buf, keep_ref, send_ref)
    sum_riders(n, gb_ref, other_ref, wide)
    sum_ref[...] = wide[...].astype(BF16)
    ride(wide, send_ref, keep_ref.shape[0])


def last_body(own_ref, other_ref, gb_ref, token, out_ref, sum_ref):
    token[...] = jnp.zeros_like(token)
    n = own_ref.shape[0]
    for j in range(n):
        out_ref[j] = own_ref[j] + other_ref[j].astype(F32)
    sum_riders(n, gb_ref, other_ref, sum_ref)


def add_body(own_ref, other_ref, out_ref):
    out_ref[...] = (own_ref[...].astype(F32) + other_ref[...].astype(F32)).astype(out_ref.dtype)


class Chain:
    def __init__(self):
        self.last = []

    def __call__(self, *args, deps=(), **kwargs):
        outs = call(*args, deps=[*self.last, *deps], **kwargs)
        self.last = [jax.tree.leaves(outs)[0]]
        return outs


def on_device(prev_out, prev_grad, saved_in, seq_mix, coeffs, mixer):
    n_sec, n_seq = lax.axis_size("section"), lax.axis_size("seq")
    weights = mixer[0]
    width, bw = weights.shape
    nb = width // bw
    low = n_seq // nb
    levels = n_seq.bit_length() - 1
    n_low = low.bit_length() - 1
    n_top = levels - n_low
    q = lax.axis_index("seq").astype(jnp.int32)
    at = jnp.stack([q // low] + [jnp.bitwise_and(jnp.right_shift(q, l), 1) for l in range(levels)])
    rows = prev_out.shape[1]
    half = nb // 2
    fwd_loc, fwd_low = 0, 4 * n_top
    adj_loc = fwd_low + 2 * n_low
    adj_low = adj_loc + 4 * n_top
    n_coef = adj_low + 2 * n_low

    def send(x, shift, flip, name="p"):
        with jax.named_scope(name):
            return send_(x, shift, flip)

    def send_(x, shift, flip):
        pairs = [
            (s * n_seq + i, (s + shift) % n_sec * n_seq + (i ^ flip)) for s in range(n_sec) for i in range(n_seq)
        ]
        return lax.ppermute(x, ("section", "seq"), pairs)

    run = Chain()

    def pack(x, name, deps=()):
        return run(
            functools.partial(pack_body, nb),
            [shape(bw, rows)] * nb,
            [at, x],
            [pltpu.VMEM((width, rows), BF16)],
            name,
            deps=deps,
        )

    token = shape(8, LANES, dtype=F32)

    def unpack(pieces, name):
        return run(
            functools.partial(unpack_body, nb),
            [token, shape(rows, width)],
            [at, *[pieces[k] for k in range(nb)]],
            [pltpu.VMEM((width, rows), BF16)],
            name,
            out_hbm=True,
        )[1]

    def release(pieces, name, deps=()):
        return run(copy_body, [shape(*p.shape) for p in pieces], pieces, (), name, deps=deps)

    def stack(pieces, name, deps=()):
        return run(stack_body, shape(nb, bw, rows), [pieces[k] for k in range(nb)], (), name, deps=deps)

    def cross(u, flip, name):
        if name in ():
            return send(u, 0, flip, name), u
        mark = call(mark_body, shape(8, LANES, dtype=F32), [], (), "mark", [u], declared=DECLARED)
        return send(u, 0, flip, name), mark

    def open_step(u, name):
        return u, *cross(u, 1, f"{name}_level0")

    def more_steps(opened, first, name):
        u, other, mark = opened
        for l in range(1, n_low):
            u = run(
                functools.partial(combine_body, first + 2 * (l - 1)),
                shape(*u.shape),
                [coef, u, other],
                (),
                f"mix_{name}",
                deps=[mark],
            )
            other, mark = cross(u, 1 << l, f"{name}_level{l}")
        return u, other, mark

    far = range(half, nb)
    far_first = [*reversed(far), *reversed(range(1, half))]

    def spread(pieces, shift, ks, name):
        return {k: send(pieces[k], shift, k * low, f"{name}{k}") for k in ks}

    held = [saved_in[0], prev_grad[0], coeffs[0], weights.T, seq_mix[0]]
    *fp, saved, upstream, factors, w_t, blocks = run(
        functools.partial(open_body, nb),
        [shape(bw, rows)] * nb + [shape(*a.shape, dtype=a.dtype) for a in held],
        [at],
        [
            pltpu.VMEM((rows, width), BF16),
            pltpu.VMEM((width, rows), BF16),
            pltpu.SemaphoreType.DMA((1 + len(held),)),
        ],
        "pack_f",
        in_hbm=[prev_out[0], *held],
    )
    fr = spread(fp, 1, [*range(1, half), 0, *far], "in_f")
    sp = pack(saved, "pack_s", [fr[k] for k in range(half)])
    sr = {0: sp[0], **spread(sp, 0, range(1, nb), "in_s")}
    coef, w_own, w_own_t = run(
        functools.partial(prep_body, nb, n_low),
        [shape(bw, n_coef, dtype=F32), shape(bw, bw), shape(bw, bw)],
        [at, factors, w_t],
        [pltpu.VMEM((4 * levels, bw), F32), pltpu.VMEM((n_coef, bw), F32)],
        "prep",
    )
    f_open = open_step(stack(fr, "stack_f", [sr[k] for k in range(1, half)]), "f")
    f_all = more_steps(f_open, fwd_low, "f")
    up = pack(upstream, "pack_u")
    ur = spread(up, -1, far, "in_u")
    s_open = open_step(stack(sr, "stack_s"), "s")
    s_all = more_steps(s_open, fwd_low, "s")
    u_near = release(up[:half], "release_u")
    ur.update(spread(u_near, -1, range(half), "in_u"))

    f_last = fwd_low + 2 * (n_low - 1)
    a_last = adj_low + 2 * (n_low - 1)
    fo = run(
        functools.partial(forward_body, nb, f_last, fwd_loc),
        [shape(bw, rows)] * nb,
        [coef, blocks, w_own_t, *f_all[:2], *[fr[k] for k in range(nb)]],
        [pltpu.VMEM((nb, bw, rows), BF16), pltpu.VMEM((bw, nb * rows), BF16)],
        "layer_f",
        deps=[f_all[2]],
    )
    of = {0: fo[0], **spread(fo, 0, far_first, "out_f")}

    v_near, v_far, d, act, gz, u = run(
        functools.partial(backward_body, nb, f_last, fwd_loc, adj_loc),
        [shape(half, bw, rows), shape(nb - half, bw, rows), shape(nb, bw, rows)]
        + [shape(bw, nb * rows)] * 2
        + [shape(nb, bw, rows)],
        [
            coef,
            blocks,
            w_own,
            w_own_t,
            *s_all[:2],
            *[sr[k] for k in range(nb)],
            *[ur[k] for k in range(nb)],
        ],
        [pltpu.VMEM((nb, bw, rows), F32), pltpu.VMEM((bw, nb * rows), BF16)],
        "layer_b",
        deps=[s_all[2]],
    )
    far_open, near_open = open_step(v_far, "d_far"), open_step(v_near, "d_near")
    part = bw // low
    gb_slabs = riders(0, rows, part, bw)[1]
    gw, gb = run(
        functools.partial(grads_body, nb),
        [shape(low, part, bw, dtype=F32), shape(rows, rows)],
        [act, gz, d, u],
        (),
        "weight_grads",
    )
    d_far = more_steps(far_open, adj_low, "d_far")
    d_near = more_steps(near_open, adj_low, "d_near")
    out_f = unpack(of, "unpack_f")
    od = {}

    def finish(opened, k0, n):
        own, other, mark = opened
        outs = run(
            functools.partial(finish_body, k0, n, a_last),
            [shape(bw, rows)] * n,
            [coef, own, other, d],
            (),
            "finish_d",
            deps=[mark],
        )
        for k in reversed(range(n)):
            od[k0 + k] = send(outs[k], 0, (k0 + k) * low, f"out_d{k0 + k}") if k0 + k else outs[k]

    def sum_b(gb, l):
        got, mark = cross(gb, 1 << l, f"sum_b{l}")
        return run(add_body, shape(rows, rows), [gb, got], (), "sum_b", deps=[mark])

    gb = sum_b(gb, n_low)
    finish(d_far, half, nb - half)
    for l in range(n_low + 1, levels):
        gb = sum_b(gb, l)
    keep, give = run(
        first_half_body,
        [shape(low // 2, part, bw, dtype=F32), shape(low // 2 + gb_slabs, part, bw)],
        [at, gw, gb],
        (),
        "sum_w",
    )
    got, mark = cross(give, 1, "sum_w0")
    finish(d_near, 0, half)
    for l in range(n_low - 1):
        m = low >> l + 2
        keep, give, gb = run(
            functools.partial(halve_body, l + 1),
            [shape(m, part, bw, dtype=F32), shape(m + gb_slabs, part, bw), shape(rows, rows)],
            [at, keep, got, gb],
            [pltpu.VMEM((2 * m, part, bw), F32), pltpu.VMEM((rows, rows), F32)],
            "sum_w",
            deps=[mark],
        )
        got, mark = cross(give, 2 << l, f"sum_w{l + 1}")
    _, grad_w, grad_b = run(
        last_body,
        [token, shape(1, part, bw, dtype=F32), shape(rows, rows, dtype=F32)],
        [keep, got, gb],
        (),
        "sum_w",
        deps=[mark],
        out_hbm=True,
    )
    out_d = unpack(od, "unpack_d")
    return out_f[None], out_d[None], grad_w, grad_b[None]


def solution(mesh):
    placed = (
        P("section", "seq", None),
        P("section", "seq", None),
        P("section", "seq", None),
        P("section", None, None),
        P("section", None, None, None),
        P("section", None, None),
    )
    return jax.shard_map(
        on_device,
        mesh=mesh,
        in_specs=placed,
        out_specs=(
            P("section", "seq", None),
            P("section", "seq", None),
            P("section", "seq", None),
            P("section", None, None),
        ),
        check_vma=False,
    )
```

time: 113 us -> 81.7 us (0.72)
  waiting for transfers between devices: 36.9 us -> 18.7 us
  local copies, waits for them, and re-layouts: 9.07 us -> 0.08 us
  Pallas kernels: 21.5 us -> 15.6 us
  starting transfers between devices: 44.7 us -> 46.3 us
    ppermute x35 -> x29, waiting for transfers between devices: 36.9 us -> 18.7 us  [send_(): return lax.ppermute(x, ('section', 'seq'), pairs)]
    unnamed x33 -> x0, local copies, waits for them, and re-layouts: 8.98 us -> none
    pallas_call x27 -> x35, Pallas kernels: 21.5 us -> 15.6 us  [call(): pl.pallas_call(kernel, out_shape=shapes, in_specs=specs, out_specs=jax.tr...]
    ppermute x35 -> x29, starting transfers between devices: 44.7 us -> 46.3 us  [send_(): return lax.ppermute(x, ('section', 'seq'), pairs)]
  transfers between devices with their start and end apart: 35 -> 29, of which waited for: 10 -> 9; matrix products, arithmetic and copies ran while one was open for 2% -> 0% of each run, Pallas kernels for 16% -> 14%
where the time goes in v3:
time: 81.7 us; the launch traced here: 81.6 us
  starting transfers between devices  46.3 us (57%)
  waiting for transfers between devices  18.7 us (23%)
  Pallas kernels  15.6 us (19%)
  between operations  0.93 us (1%)
    ppermute x29, starting transfers between devices, send_(): return lax.ppermute(x, ('section', 'seq'), pairs)  46.3 us
    ppermute x29, waiting for transfers between devices, send_(): return lax.ppermute(x, ('section', 'seq'), pairs)  18.7 us
    pallas_call x35, Pallas kernels, call(): pl.pallas_call(kernel, out_shape=shapes, in_specs=specs, out_specs=jax.tr...  15.6 us
  transfers between devices with their start and end apart: 29, of which 9 were waited for; matrix products, arithmetic and copies ran while one was open for 0% of the time, Pallas kernels for 14%

profile of v3, /device:TPU:0, one launch (start us, length us, event | category | flops | bytes accessed | tf_op | source)
XLA Modules:
  0.0 81.6 jit_solution(5293189822352285318)
XLA Ops:
  0.7 2.5 %pack_f.1 = (bf16[448,128]{1,0:T(8,128)(2,1)S(1)}, bf16[448,128]{1,0:T(8,128)(2,1)S(1)}, bf16[448,128]{1,0:T(8,128)(2,1)S(1)}, bf16[448,128]{1,0:T(8,128)(2,1)S(...) custom-call(s32[5]{0:T(128)S(1)} %stack.23.refs_0_, ...), custom_call_target="tpu_custom_call" | custom-call | tf_op jit(solution)/shard_map/pack_f/pallas_call | solution.py:49
  3.2 3.0 %collective-permute-start = (bf16[448,128]{1,0:T(8,128)(2,1)S(1)}, bf16[448,128]{1,0:T(8,128)(2,1)S(1)}, u32[]{:S(2)}, u32[]{:S(2)}) collective-permute-start(bf16[448,128]{1,0:T(8,128)(2,1)S(1)} %get-tuple-element.56.refs_2_), channel_id=1, source_target_pairs={{0,16},{1,17},{2,18},{3,19},{4,20},{5,21},{6,22},{7,23},{8,24},{9,... | collective-permute-start | bytes 344072 | tf_op jit(solution)/shard_map/in_f0/ppermute | solution.py:345
  6.2 1.5 %collective-permute-start.1 = (bf16[448,128]{1,0:T(8,128)(2,1)S(1)}, bf16[448,128]{1,0:T(8,128)(2,1)S(1)}, u32[]{:S(2)}, u32[]{:S(2)}) collective-permute-start(bf16[448,128]{1,0:T(8,128)(2,1)S(1)} %get-tuple-element.57), channel_id=1, source_target_pairs={{0,20},{1,21},{2,22},{3,23},{4,16},{5,17},{6,18},{7,19},{8,28},{9,... | collective-permute-start | bytes 344072 | tf_op jit(solution)/shard_map/in_f1/ppermute | solution.py:345
  7.8 3.5 %collective-permute-start.2 = (bf16[448,128]{1,0:T(8,128)(2,1)S(1)}, bf16[448,128]{1,0:T(8,128)(2,1)S(1)}, u32[]{:S(2)}, u32[]{:S(2)}) collective-permute-start(bf16[448,128]{1,0:T(8,128)(2,1)S(1)} %get-tuple-element.62), channel_id=1, source_target_pairs={{0,24},{1,25},{2,26},{3,27},{4,28},{5,29},{6,30},{7,31},{8,16},{9,... | collective-permute-start | bytes 344072 | tf_op jit(solution)/shard_map/in_f2/ppermute | solution.py:345
  11.6 1.6 %collective-permute-done.1.refs_4_.refs_1_.refs_6_ = bf16[448,128]{1,0:T(8,128)(2,1)S(1)} collective-permute-done((bf16[448,128]{1,0:T(8,128)(2,1)S(1)}, bf16[448,128]{1,0:T(8,128)(2,1)S(1)}, u32[]{:S(2)}, u32[]{:S(2)}) %collective-permute-start.1) | collective-permute-done | bytes 114720 | tf_op jit(solution)/shard_map/in_f1/ppermute | solution.py:345
  13.9 1.5 %collective-permute-start.4 = (bf16[448,128]{1,0:T(8,128)(2,1)S(1)}, bf16[448,128]{1,0:T(8,128)(2,1)S(1)}, u32[]{:S(2)}, u32[]{:S(2)}) collective-permute-start(bf16[448,128]{1,0:T(8,128)(2,1)S(1)} %get-tuple-element.64), channel_id=1, source_target_pairs={{0,4},{1,5},{2,6},{3,7},{4,0},{5,1},{6,2},{7,3},{8,12},{9,13},{10,... | collective-permute-start | bytes 344072 | tf_op jit(solution)/shard_map/in_s1/ppermute | solution.py:345
  15.4 3.4 %collective-permute-start.7 = (bf16[448,128]{1,0:T(8,128)(2,1)S(1)}, bf16[448,128]{1,0:T(8,128)(2,1)S(1)}, u32[]{:S(2)}, u32[]{:S(2)}) collective-permute-start(bf16[448,128]{1,0:T(8,128)(2,1)S(1)} %get-tuple-element.68), channel_id=1, source_target_pairs={{0,8},{1,9},{2,10},{3,11},{4,12},{5,13},{6,14},{7,15},{8,0},{9,1},... | collective-permute-start | bytes 344072 | tf_op jit(solution)/shard_map/in_s2/ppermute | solution.py:345
  20.2 1.8 %collective-permute-done.5.refs_2_ = bf16[4,448,128]{2,1,0:T(8,128)(2,1)S(1)} collective-permute-done((bf16[4,448,128]{2,1,0:T(8,128)(2,1)S(1)}, bf16[4,448,128]{2,1,0:T(8,128)(2,1)S(1)}, u32[]{:S(2)}, u32[]{:S(2)}) %collective-permute-start.5) | collective-permute-done | bytes 458784 | tf_op jit(solution)/shard_map/f_level0/ppermute | solution.py:345
  22.3 1.6 %collective-permute-start.6 = (bf16[4,448,128]{2,1,0:T(8,128)(2,1)S(1)}, bf16[4,448,128]{2,1,0:T(8,128)(2,1)S(1)}, u32[]{:S(2)}, u32[]{:S(2)}) collective-permute-start(bf16[4,448,128]{2,1,0:T(8,128)(2,1)S(1)} %mix_f.1.refs_2_.refs_0_.refs_3_), channel_id=1, source_target_pairs={{0,2},{1,3},{2,0},{3,1},{4,6},{5,7},{6,4},{7,5},{8,10},{9,11},{10,... | collective-permute-start | bytes 1376264 | tf_op jit(solution)/shard_map/f_level1/ppermute | solution.py:345
  24.6 5.0 %collective-permute-done.7.refs_2_.refs_8_ = bf16[448,128]{1,0:T(8,128)(2,1)S(1)} collective-permute-done((bf16[448,128]{1,0:T(8,128)(2,1)S(1)}, bf16[448,128]{1,0:T(8,128)(2,1)S(1)}, u32[]{:S(2)}, u32[]{:S(2)}) %collective-permute-start.7) | collective-permute-done | bytes 114720 | tf_op jit(solution)/shard_map/in_s2/ppermute | solution.py:345
  29.7 4.9 %collective-permute-start.16 = (bf16[448,128]{1,0:T(8,128)(2,1)S(1)}, bf16[448,128]{1,0:T(8,128)(2,1)S(1)}, u32[]{:S(2)}, u32[]{:S(2)}) collective-permute-start(bf16[448,128]{1,0:T(8,128)(2,1)S(1)} %get-tuple-element.77), channel_id=1, source_target_pairs={{0,24},{1,25},{2,26},{3,27},{4,28},{5,29},{6,30},{7,31},{8,16},{9,... | collective-permute-start | bytes 344072 | tf_op jit(solution)/shard_map/in_u2/ppermute | solution.py:345
  38.1 6.1 %collective-permute-start.15 = (bf16[448,128]{1,0:T(8,128)(2,1)S(1)}, bf16[448,128]{1,0:T(8,128)(2,1)S(1)}, u32[]{:S(2)}, u32[]{:S(2)}) collective-permute-start(bf16[448,128]{1,0:T(8,128)(2,1)S(1)} %get-tuple-element.76), channel_id=1, source_target_pairs={{0,20},{1,21},{2,22},{3,23},{4,16},{5,17},{6,18},{7,19},{8,28},{9,... | collective-permute-start | bytes 344072 | tf_op jit(solution)/shard_map/in_u1/ppermute | solution.py:345
  44.2 1.5 %layer_f.1 = (bf16[448,128]{1,0:T(8,128)(2,1)S(1)}, bf16[448,128]{1,0:T(8,128)(2,1)S(1)}, bf16[448,128]{1,0:T(8,128)(2,1)S(1)}, bf16[448,128]{1,0:T(8,128)(2,1)S(1)}) custom-call(f32[448,24]{1,0:T(8,128)S(1)} %get-tuple-element.59.refs_4_.refs_0_, bf16[128,128]{1,0:T(8,128)(2,1)S(1)} %get-tuple-element.60.refs_1_, ...), custom_call_target="tpu_custom_call" | custom-call | tf_op jit(solution)/shard_map/layer_f/pallas_call | solution.py:49
  45.8 3.3 %collective-permute-start.11 = (bf16[448,128]{1,0:T(8,128)(2,1)S(1)}, bf16[448,128]{1,0:T(8,128)(2,1)S(1)}, u32[]{:S(2)}, u32[]{:S(2)}) collective-permute-start(bf16[448,128]{1,0:T(8,128)(2,1)S(1)} %get-tuple-element.73), channel_id=1, source_target_pairs={{0,8},{1,9},{2,10},{3,11},{4,12},{5,13},{6,14},{7,15},{8,0},{9,1},... | collective-permute-start | bytes 344072 | tf_op jit(solution)/shard_map/out_f2/ppermute | solution.py:345
  50.2 2.2 %layer_b.1 = (bf16[2,448,128]{2,1,0:T(8,128)(2,1)S(1)}, bf16[2,448,128]{2,1,0:T(8,128)(2,1)S(1)}, bf16[4,448,128]{2,1,0:T(8,128)(2,1)S(1)}, bf16[448,512]{1,0:T(...) custom-call(f32[448,24]{1,0:T(8,128)S(1)} %get-tuple-element.59.refs_4_.refs_0_, ...), custom_call_target="tpu_custom_call" | custom-call | tf_op jit(solution)/shard_map/layer_b/pallas_call | solution.py:49
  53.9 2.3 %collective-permute-start.21 = (bf16[128,128]{1,0:T(8,128)(2,1)S(1)}, bf16[128,128]{1,0:T(8,128)(2,1)S(1)}, u32[]{:S(2)}, u32[]{:S(2)}) collective-permute-start(bf16[128,128]{1,0:T(8,128)(2,1)S(1)} %get-tuple-element.87.refs_0_), channel_id=1, source_target_pairs={{0,4},{1,5},{2,6},{3,7},{4,0},{5,1},{6,2},{7,3},{8,12},{9,13},{10,... | collective-permute-start | bytes 98312 | tf_op jit(solution)/shard_map/sum_b2/ppermute | solution.py:345
  56.4 1.6 %collective-permute-start.23 = (bf16[2,448,128]{2,1,0:T(8,128)(2,1)S(1)}, bf16[2,448,128]{2,1,0:T(8,128)(2,1)S(1)}, u32[]{:S(2)}, u32[]{:S(2)}) collective-permute-start(bf16[2,448,128]{2,1,0:T(8,128)(2,1)S(1)} %mix_d_far.1.refs_3_.refs_0_.refs_1_), channel_id=1, source_target_pairs={{0,2},{1,3},{2,0},{3,1},{4,6},{5,7},{6,4},{7,5},{8,10},{9,11},{10,... | collective-permute-start | bytes 688136 | tf_op jit(solution)/shard_map/d_far_level1/ppermute | solution.py:345
  58.8 1.5 %unpack_f.1 = (f32[8,128]{1,0:T(8,128)S(1)}, bf16[128,1792]{1,0:T(8,128)(2,1)}) custom-call(s32[5]{0:T(128)S(1)} %stack.23.refs_0_, bf16[448,128]{1,0:T(8,128)(2,1)S(1)} %get-tuple-element.71.refs_14_.refs_1_, bf16[448,128]{1,0:T(8,128)(2,1)S(1)} %collective-permute-done.10.refs_2_, bf16[448,128]{1,0:T(8,128)(2,1)S(1)} %collective-permute-done.11.refs_3_, ...), custom_call_target="tpu_custom_call" | custom-call | tf_op jit(solution)/shard_map/unpack_f/pallas_call | solution.py:49
  60.3 1.5 %collective-permute-start.22 = (bf16[128,128]{1,0:T(8,128)(2,1)S(1)}, bf16[128,128]{1,0:T(8,128)(2,1)S(1)}, u32[]{:S(2)}, u32[]{:S(2)}) collective-permute-start(bf16[128,128]{1,0:T(8,128)(2,1)S(1)} %sum_b.2.refs_4_.refs_0_), channel_id=1, source_target_pairs={{0,8},{1,9},{2,10},{3,11},{4,12},{5,13},{6,14},{7,15},{8,0},{9,1},... | collective-permute-start | bytes 98312 | tf_op jit(solution)/shard_map/sum_b3/ppermute | solution.py:345
  61.8 3.1 %collective-permute-done.23.refs_2_ = bf16[2,448,128]{2,1,0:T(8,128)(2,1)S(1)} collective-permute-done((bf16[2,448,128]{2,1,0:T(8,128)(2,1)S(1)}, bf16[2,448,128]{2,1,0:T(8,128)(2,1)S(1)}, u32[]{:S(2)}, u32[]{:S(2)}) %collective-permute-start.23) | collective-permute-done | bytes 229408 | tf_op jit(solution)/shard_map/d_far_level1/ppermute | solution.py:345
  69.7 2.6 %collective-permute-start.26 = (bf16[448,128]{1,0:T(8,128)(2,1)S(1)}, bf16[448,128]{1,0:T(8,128)(2,1)S(1)}, u32[]{:S(2)}, u32[]{:S(2)}) collective-permute-start(bf16[448,128]{1,0:T(8,128)(2,1)S(1)} %get-tuple-element.93), channel_id=1, source_target_pairs={{0,12},{1,13},{2,14},{3,15},{4,8},{5,9},{6,10},{7,11},{8,4},{9,5},... | collective-permute-start | bytes 344072 | tf_op jit(solution)/shard_map/out_d3/ppermute | solution.py:345
  72.9 1.6 %collective-permute-start.28 = (bf16[2,112,448]{2,1,0:T(8,128)(2,1)S(1)}, bf16[2,112,448]{2,1,0:T(8,128)(2,1)S(1)}, u32[]{:S(2)}, u32[]{:S(2)}) collective-permute-start(bf16[2,112,448]{2,1,0:T(8,128)(2,1)S(1)} %get-tuple-element.96.refs_0_), channel_id=1, source_target_pairs={{0,2},{1,3},{2,0},{3,1},{4,6},{5,7},{6,4},{7,5},{8,10},{9,11},{10,... | collective-permute-start | bytes 602120 | tf_op jit(solution)/shard_map/sum_w1/ppermute | solution.py:345
  74.5 4.8 %collective-permute-done.28.refs_1_ = bf16[2,112,448]{2,1,0:T(8,128)(2,1)S(1)} collective-permute-done((bf16[2,112,448]{2,1,0:T(8,128)(2,1)S(1)}, bf16[2,112,448]{2,1,0:T(8,128)(2,1)S(1)}, u32[]{:S(2)}, u32[]{:S(2)}) %collective-permute-start.28) | collective-permute-done | bytes 200736 | tf_op jit(solution)/shard_map/sum_w1/ppermute | solution.py:345
  80.0 1.5 %unpack_d.1 = (f32[8,128]{1,0:T(8,128)}, bf16[128,1792]{1,0:T(8,128)(2,1)}) custom-call(s32[5]{0:T(128)S(1)} %stack.23.refs_0_, bf16[448,128]{1,0:T(8,128)(2,1)S(1)} %get-tuple-element.91.refs_4_.refs_1_, bf16[448,128]{1,0:T(8,128)(2,1)S(1)} %collective-permute-done.24.refs_2_, bf16[448,128]{1,0:T(8,128)(2,1)S(1)} %collective-permute-done.25.refs_3_, ...), custom_call_target="tpu_custom_call" | custom-call | tf_op jit(solution)/shard_map/unpack_d/pallas_call | solution.py:49
  (70 shorter events, 16.9 us)
Async XLA Ops:
  3.2 8.3 %collective-permute-start = (bf16[448,128]{1,0:T(8,128)(2,1)S(1)}, bf16[448,128]{1,0:T(8,128)(2,1)S(1)}, u32[]{:S(2)}, u32[]{:S(2)}) collective-permute-start(bf16[448,128]{1,0:T(8,128)(2,1)S(1)} %get-tuple-element.56.refs_2_), channel_id=1, source_target_pairs={{0,16},{1,17},{2,18},{3,19},{4,20},{5,21},{6,22},{7,23},{8,24},{9,... | collective-permute-start | bytes 344072 | tf_op jit(solution)/shard_map/in_f0/ppermute | solution.py:345
  6.2 6.9 %collective-permute-start.1 = (bf16[448,128]{1,0:T(8,128)(2,1)S(1)}, bf16[448,128]{1,0:T(8,128)(2,1)S(1)}, u32[]{:S(2)}, u32[]{:S(2)}) collective-permute-start(bf16[448,128]{1,0:T(8,128)(2,1)S(1)} %get-tuple-element.57), channel_id=1, source_target_pairs={{0,20},{1,21},{2,22},{3,23},{4,16},{5,17},{6,18},{7,19},{8,28},{9,... | collective-permute-start | bytes 344072 | tf_op jit(solution)/shard_map/in_f1/ppermute | solution.py:345
  7.8 11.9 %collective-permute-start.2 = (bf16[448,128]{1,0:T(8,128)(2,1)S(1)}, bf16[448,128]{1,0:T(8,128)(2,1)S(1)}, u32[]{:S(2)}, u32[]{:S(2)}) collective-permute-start(bf16[448,128]{1,0:T(8,128)(2,1)S(1)} %get-tuple-element.62), channel_id=1, source_target_pairs={{0,24},{1,25},{2,26},{3,27},{4,28},{5,29},{6,30},{7,31},{8,16},{9,... | collective-permute-start | bytes 344072 | tf_op jit(solution)/shard_map/in_f2/ppermute | solution.py:345
  11.3 8.8 %collective-permute-start.3 = (bf16[448,128]{1,0:T(8,128)(2,1)S(1)}, bf16[448,128]{1,0:T(8,128)(2,1)S(1)}, u32[]{:S(2)}, u32[]{:S(2)}) collective-permute-start(bf16[448,128]{1,0:T(8,128)(2,1)S(1)} %get-tuple-element.63), channel_id=1, source_target_pairs={{0,28},{1,29},{2,30},{3,31},{4,24},{5,25},{6,26},{7,27},{8,20},{9,... | collective-permute-start | bytes 344072 | tf_op jit(solution)/shard_map/in_f3/ppermute | solution.py:345
  15.4 14.2 %collective-permute-start.7 = (bf16[448,128]{1,0:T(8,128)(2,1)S(1)}, bf16[448,128]{1,0:T(8,128)(2,1)S(1)}, u32[]{:S(2)}, u32[]{:S(2)}) collective-permute-start(bf16[448,128]{1,0:T(8,128)(2,1)S(1)} %get-tuple-element.68), channel_id=1, source_target_pairs={{0,8},{1,9},{2,10},{3,11},{4,12},{5,13},{6,14},{7,15},{8,0},{9,1},... | collective-permute-start | bytes 344072 | tf_op jit(solution)/shard_map/in_s2/ppermute | solution.py:345
  18.8 10.8 %collective-permute-start.8 = (bf16[448,128]{1,0:T(8,128)(2,1)S(1)}, bf16[448,128]{1,0:T(8,128)(2,1)S(1)}, u32[]{:S(2)}, u32[]{:S(2)}) collective-permute-start(bf16[448,128]{1,0:T(8,128)(2,1)S(1)} %get-tuple-element.69), channel_id=1, source_target_pairs={{0,12},{1,13},{2,14},{3,15},{4,8},{5,9},{6,10},{7,11},{8,4},{9,5},... | collective-permute-start | bytes 344072 | tf_op jit(solution)/shard_map/in_s3/ppermute | solution.py:345
  22.3 15.8 %collective-permute-start.6 = (bf16[4,448,128]{2,1,0:T(8,128)(2,1)S(1)}, bf16[4,448,128]{2,1,0:T(8,128)(2,1)S(1)}, u32[]{:S(2)}, u32[]{:S(2)}) collective-permute-start(bf16[4,448,128]{2,1,0:T(8,128)(2,1)S(1)} %mix_f.1.refs_2_.refs_0_.refs_3_), channel_id=1, source_target_pairs={{0,2},{1,3},{2,0},{3,1},{4,6},{5,7},{6,4},{7,5},{8,10},{9,11},{10,... | collective-permute-start | bytes 1376264 | tf_op jit(solution)/shard_map/f_level1/ppermute | solution.py:345
  29.6 6.2 %collective-permute-start.9 = (bf16[4,448,128]{2,1,0:T(8,128)(2,1)S(1)}, bf16[4,448,128]{2,1,0:T(8,128)(2,1)S(1)}, u32[]{:S(2)}, u32[]{:S(2)}) collective-permute-start(bf16[4,448,128]{2,1,0:T(8,128)(2,1)S(1)} %stack_s.1.refs_0_.refs_1_.refs_3_), channel_id=1, source_target_pairs={{0,1},{1,0},{2,3},{3,2},{4,5},{5,4},{6,7},{7,6},{8,9},{9,8},{10,11... | collective-permute-start | bytes 1376264 | tf_op jit(solution)/shard_map/s_level0/ppermute | solution.py:345
  29.7 16.0 %collective-permute-start.16 = (bf16[448,128]{1,0:T(8,128)(2,1)S(1)}, bf16[448,128]{1,0:T(8,128)(2,1)S(1)}, u32[]{:S(2)}, u32[]{:S(2)}) collective-permute-start(bf16[448,128]{1,0:T(8,128)(2,1)S(1)} %get-tuple-element.77), channel_id=1, source_target_pairs={{0,24},{1,25},{2,26},{3,27},{4,28},{5,29},{6,30},{7,31},{8,16},{9,... | collective-permute-start | bytes 344072 | tf_op jit(solution)/shard_map/in_u2/ppermute | solution.py:345
  34.6 11.2 %collective-permute-start.17 = (bf16[448,128]{1,0:T(8,128)(2,1)S(1)}, bf16[448,128]{1,0:T(8,128)(2,1)S(1)}, u32[]{:S(2)}, u32[]{:S(2)}) collective-permute-start(bf16[448,128]{1,0:T(8,128)(2,1)S(1)} %get-tuple-element.78), channel_id=1, source_target_pairs={{0,28},{1,29},{2,30},{3,31},{4,24},{5,25},{6,26},{7,27},{8,20},{9,... | collective-permute-start | bytes 344072 | tf_op jit(solution)/shard_map/in_u3/ppermute | solution.py:345
  36.1 14.1 %collective-permute-start.13 = (bf16[4,448,128]{2,1,0:T(8,128)(2,1)S(1)}, bf16[4,448,128]{2,1,0:T(8,128)(2,1)S(1)}, u32[]{:S(2)}, u32[]{:S(2)}) collective-permute-start(bf16[4,448,128]{2,1,0:T(8,128)(2,1)S(1)} %mix_s.1.refs_2_.refs_0_.refs_4_), channel_id=1, source_target_pairs={{0,2},{1,3},{2,0},{3,1},{4,6},{5,7},{6,4},{7,5},{8,10},{9,11},{10,... | collective-permute-start | bytes 1376264 | tf_op jit(solution)/shard_map/s_level1/ppermute | solution.py:345
  37.0 12.1 %collective-permute-start.14 = (bf16[448,128]{1,0:T(8,128)(2,1)S(1)}, bf16[448,128]{1,0:T(8,128)(2,1)S(1)}, u32[]{:S(2)}, u32[]{:S(2)}) collective-permute-start(bf16[448,128]{1,0:T(8,128)(2,1)S(1)} %get-tuple-element.70.refs_9_), channel_id=1, source_target_pairs={{0,16},{1,17},{2,18},{3,19},{4,20},{5,21},{6,22},{7,23},{8,24},{9,... | collective-permute-start | bytes 344072 | tf_op jit(solution)/shard_map/in_u0/ppermute | solution.py:345
  38.1 12.1 %collective-permute-start.15 = (bf16[448,128]{1,0:T(8,128)(2,1)S(1)}, bf16[448,128]{1,0:T(8,128)(2,1)S(1)}, u32[]{:S(2)}, u32[]{:S(2)}) collective-permute-start(bf16[448,128]{1,0:T(8,128)(2,1)S(1)} %get-tuple-element.76), channel_id=1, source_target_pairs={{0,20},{1,21},{2,22},{3,23},{4,16},{5,17},{6,18},{7,19},{8,28},{9,... | collective-permute-start | bytes 344072 | tf_op jit(solution)/shard_map/in_u1/ppermute | solution.py:345
  45.7 12.5 %collective-permute-start.10 = (bf16[448,128]{1,0:T(8,128)(2,1)S(1)}, bf16[448,128]{1,0:T(8,128)(2,1)S(1)}, u32[]{:S(2)}, u32[]{:S(2)}) collective-permute-start(bf16[448,128]{1,0:T(8,128)(2,1)S(1)} %get-tuple-element.72), channel_id=1, source_target_pairs={{0,4},{1,5},{2,6},{3,7},{4,0},{5,1},{6,2},{7,3},{8,12},{9,13},{10,... | collective-permute-start | bytes 344072 | tf_op jit(solution)/shard_map/out_f1/ppermute | solution.py:345
  45.8 13.0 %collective-permute-start.11 = (bf16[448,128]{1,0:T(8,128)(2,1)S(1)}, bf16[448,128]{1,0:T(8,128)(2,1)S(1)}, u32[]{:S(2)}, u32[]{:S(2)}) collective-permute-start(bf16[448,128]{1,0:T(8,128)(2,1)S(1)} %get-tuple-element.73), channel_id=1, source_target_pairs={{0,8},{1,9},{2,10},{3,11},{4,12},{5,13},{6,14},{7,15},{8,0},{9,1},... | collective-permute-start | bytes 344072 | tf_op jit(solution)/shard_map/out_f2/ppermute | solution.py:345
  49.1 9.7 %collective-permute-start.12 = (bf16[448,128]{1,0:T(8,128)(2,1)S(1)}, bf16[448,128]{1,0:T(8,128)(2,1)S(1)}, u32[]{:S(2)}, u32[]{:S(2)}) collective-permute-start(bf16[448,128]{1,0:T(8,128)(2,1)S(1)} %get-tuple-element.74), channel_id=1, source_target_pairs={{0,12},{1,13},{2,14},{3,15},{4,8},{5,9},{6,10},{7,11},{8,4},{9,5},... | collective-permute-start | bytes 344072 | tf_op jit(solution)/shard_map/out_f3/ppermute | solution.py:345
  53.9 6.4 %collective-permute-start.21 = (bf16[128,128]{1,0:T(8,128)(2,1)S(1)}, bf16[128,128]{1,0:T(8,128)(2,1)S(1)}, u32[]{:S(2)}, u32[]{:S(2)}) collective-permute-start(bf16[128,128]{1,0:T(8,128)(2,1)S(1)} %get-tuple-element.87.refs_0_), channel_id=1, source_target_pairs={{0,4},{1,5},{2,6},{3,7},{4,0},{5,1},{6,2},{7,3},{8,12},{9,13},{10,... | collective-permute-start | bytes 98312 | tf_op jit(solution)/shard_map/sum_b2/ppermute | solution.py:345
  56.4 8.6 %collective-permute-start.23 = (bf16[2,448,128]{2,1,0:T(8,128)(2,1)S(1)}, bf16[2,448,128]{2,1,0:T(8,128)(2,1)S(1)}, u32[]{:S(2)}, u32[]{:S(2)}) collective-permute-start(bf16[2,448,128]{2,1,0:T(8,128)(2,1)S(1)} %mix_d_far.1.refs_3_.refs_0_.refs_1_), channel_id=1, source_target_pairs={{0,2},{1,3},{2,0},{3,1},{4,6},{5,7},{6,4},{7,5},{8,10},{9,11},{10,... | collective-permute-start | bytes 688136 | tf_op jit(solution)/shard_map/d_far_level1/ppermute | solution.py:345
  58.2 10.5 %collective-permute-start.20 = (bf16[2,448,128]{2,1,0:T(8,128)(2,1)S(1)}, bf16[2,448,128]{2,1,0:T(8,128)(2,1)S(1)}, u32[]{:S(2)}, u32[]{:S(2)}) collective-permute-start(bf16[2,448,128]{2,1,0:T(8,128)(2,1)S(1)} %mix_d_near.1.refs_5_.refs_0_.refs_1_), channel_id=1, source_target_pairs={{0,2},{1,3},{2,0},{3,1},{4,6},{5,7},{6,4},{7,5},{8,10},{9,11},{10,... | collective-permute-start | bytes 688136 | tf_op jit(solution)/shard_map/d_near_level1/ppermute | solution.py:345
  60.3 6.3 %collective-permute-start.22 = (bf16[128,128]{1,0:T(8,128)(2,1)S(1)}, bf16[128,128]{1,0:T(8,128)(2,1)S(1)}, u32[]{:S(2)}, u32[]{:S(2)}) collective-permute-start(bf16[128,128]{1,0:T(8,128)(2,1)S(1)} %sum_b.2.refs_4_.refs_0_), channel_id=1, source_target_pairs={{0,8},{1,9},{2,10},{3,11},{4,12},{5,13},{6,14},{7,15},{8,0},{9,1},... | collective-permute-start | bytes 98312 | tf_op jit(solution)/shard_map/sum_b3/ppermute | solution.py:345
  65.2 14.8 %collective-permute-start.25 = (bf16[448,128]{1,0:T(8,128)(2,1)S(1)}, bf16[448,128]{1,0:T(8,128)(2,1)S(1)}, u32[]{:S(2)}, u32[]{:S(2)}) collective-permute-start(bf16[448,128]{1,0:T(8,128)(2,1)S(1)} %get-tuple-element.89.refs_2_), channel_id=1, source_target_pairs={{0,8},{1,9},{2,10},{3,11},{4,12},{5,13},{6,14},{7,15},{8,0},{9,1},... | collective-permute-start | bytes 344072 | tf_op jit(solution)/shard_map/out_d2/ppermute | solution.py:345
  69.0 11.0 %collective-permute-start.24 = (bf16[448,128]{1,0:T(8,128)(2,1)S(1)}, bf16[448,128]{1,0:T(8,128)(2,1)S(1)}, u32[]{:S(2)}, u32[]{:S(2)}) collective-permute-start(bf16[448,128]{1,0:T(8,128)(2,1)S(1)} %get-tuple-element.92), channel_id=1, source_target_pairs={{0,4},{1,5},{2,6},{3,7},{4,0},{5,1},{6,2},{7,3},{8,12},{9,13},{10,... | collective-permute-start | bytes 344072 | tf_op jit(solution)/shard_map/out_d1/ppermute | solution.py:345
  69.7 10.3 %collective-permute-start.26 = (bf16[448,128]{1,0:T(8,128)(2,1)S(1)}, bf16[448,128]{1,0:T(8,128)(2,1)S(1)}, u32[]{:S(2)}, u32[]{:S(2)}) collective-permute-start(bf16[448,128]{1,0:T(8,128)(2,1)S(1)} %get-tuple-element.93), channel_id=1, source_target_pairs={{0,12},{1,13},{2,14},{3,15},{4,8},{5,9},{6,10},{7,11},{8,4},{9,5},... | collective-permute-start | bytes 344072 | tf_op jit(solution)/shard_map/out_d3/ppermute | solution.py:345
  72.9 6.4 %collective-permute-start.28 = (bf16[2,112,448]{2,1,0:T(8,128)(2,1)S(1)}, bf16[2,112,448]{2,1,0:T(8,128)(2,1)S(1)}, u32[]{:S(2)}, u32[]{:S(2)}) collective-permute-start(bf16[2,112,448]{2,1,0:T(8,128)(2,1)S(1)} %get-tuple-element.96.refs_0_), channel_id=1, source_target_pairs={{0,2},{1,3},{2,0},{3,1},{4,6},{5,7},{6,4},{7,5},{8,10},{9,11},{10,... | collective-permute-start | bytes 602120 | tf_op jit(solution)/shard_map/sum_w1/ppermute | solution.py:345
  (5 other events, 18.6 us)

commit v4 on v3

--- a/solution.py
+++ b/solution.py
@@ -12,6 +12,7 @@
 LANES = 128
 CH = 64
 DECLARED = 8_000_000_000
+STEP = 200_000_000
 
 
 def dot(a, b, ca, cb):
@@ -73,6 +74,13 @@
         outs[k][...] = buf[pl.ds(start, bw), :]
 
 
+def unpack_last_body(nb, at_ref, *refs):
+    ins, own_ref = refs[:nb], refs[nb]
+    token, out, sum_ref, buf = refs[nb + 1 :]
+    add_last_body(own_ref, ins[nb // 2], token, sum_ref)
+    unpack_body(nb, at_ref, *ins, token, out, buf)
+
+
 def open_body(nb, at_ref, x_hbm, *refs):
     n = (len(refs) - nb - 3) // 2
     hbm, outs, held = refs[:n], refs[n : n + nb], refs[n + nb : 2 * n + nb]
@@ -93,7 +101,7 @@
     bw = width // nb
     for k in range(nb):
         start = pl.multiple_of(jnp.bitwise_xor(at_ref[0], k) * bw, 16)
-        buf[pl.ds(start, bw), :] = ins[k][...]
+        buf[pl.ds(start, bw), :] = ins[k][0:bw, :]
     for j in range(0, width, LANES):
         out[:, j : j + LANES] = buf[j : j + LANES, :].T
     token[...] = jnp.zeros_like(token)
@@ -139,13 +147,6 @@
     out_ref[...] = jnp.zeros_like(out_ref)
 
 
-def join_body(*refs):
-    outs = refs[len(refs) // 3 * 2 :]
-    for k, out in enumerate(outs):
-        out[0] = refs[k][...]
-        out[1] = refs[len(outs) + k][...]
-
-
 def stack_body(*refs):
     out = refs[-1]
     for k, r in enumerate(refs[:-1]):
@@ -197,9 +198,9 @@
         act_ref[:, lanes] = (r[...].astype(F32) + dot(u_ref[k], b_ref[...], 1, 1)).astype(BF16)
 
 
-def forward_body(nb, first, loc, coef_ref, b_ref, wt_ref, own_ref, other_ref, *refs):
+def forward_body(nb, first, loc, coef_ref, b_ref, wt_ref, own0, other0, own1, other1, *refs):
     ins, outs, u_ref, act_ref = refs[:nb], refs[nb : 2 * nb], refs[2 * nb], refs[2 * nb + 1]
-    finish_state(first, loc, coef_ref, ((own_ref, other_ref),), u_ref)
+    finish_state(first, loc, coef_ref, ((own0, other0), (own1, other1)), u_ref)
     mix_rows(u_ref, b_ref, ins, act_ref)
     act = act_ref[...]
     pre = dot(wt_ref[...], act, 1, 0)
@@ -249,61 +250,74 @@
         send_ref[j] = src[2 * j + 1 - bit].astype(BF16)
 
 
-def riders(n, rows, part, bw):
-    places = []
-    for i, r in enumerate(range(0, rows, part)):
-        places.append((n + i // (bw // LANES), i % (bw // LANES) * LANES, r, min(part, rows - r)))
-    return places, places[-1][0] + 1 - n
-
-
 def grads_body(nb, act_ref, gz_ref, d_ref, u_ref, gw_ref, gb_ref):
     gw, gb = dot(act_ref[...], gz_ref[...], 1, 1), 0.0
     for k in range(nb):
         gb = gb + dot(d_ref[k], u_ref[k], 0, 0)
     gb_ref[...] = gb.astype(BF16)
     part = gw_ref.shape[1]
-    for n in range(gw_ref.shape[0]):
-        gw_ref[n] = gw[n * part : (n + 1) * part, :]
-
-
-def ride(own, send_ref, n):
-    for m, lane, r, count in riders(n, own.shape[0], send_ref.shape[1], send_ref.shape[2])[0]:
-        send_ref[m, :count, lane : lane + LANES] = own[r : r + count, :].astype(BF16)
-
-
-def first_half_body(at_ref, gw_ref, gb_ref, keep_ref, send_ref):
+    for m in range(gw_ref.shape[0]):
+        gw_ref[m] = gw[m * part : (m + 1) * part, :]
+
+
+def join_gb_body(v_ref, gb_ref, near_ref):
+    n, bw, _ = v_ref.shape
+    for k in range(n):
+        near_ref[k * bw : (k + 1) * bw, :] = v_ref[k]
+    near_ref[n * bw :, :] = gb_ref[...]
+
+
+def first_half_body(at_ref, gw_ref, keep_ref, send_ref):
     halve(at_ref, 0, gw_ref, keep_ref, send_ref)
-    ride(gb_ref, send_ref, keep_ref.shape[0])
-
-
-def sum_riders(n, own_ref, other_ref, out_ref):
-    rows, part, bw = own_ref.shape[0], other_ref.shape[1], other_ref.shape[2]
-    for m, lane, r, count in riders(n, rows, part, bw)[0]:
-        out_ref[r : r + count, :] = (
-            own_ref[r : r + count, :].astype(F32) + other_ref[m, :count, lane : lane + LANES].astype(F32)
-        ).astype(out_ref.dtype)
-
-
-def halve_body(l, at_ref, own_ref, other_ref, gb_ref, keep_ref, send_ref, sum_ref, buf, wide):
-    n = own_ref.shape[0]
-    for j in range(n):
+
+
+def halve_body(l, at_ref, own_ref, other_ref, keep_ref, send_ref, buf):
+    for j in range(own_ref.shape[0]):
         buf[j] = own_ref[j] + other_ref[j].astype(F32)
     halve(at_ref, l, buf, keep_ref, send_ref)
-    sum_riders(n, gb_ref, other_ref, wide)
-    sum_ref[...] = wide[...].astype(BF16)
-    ride(wide, send_ref, keep_ref.shape[0])
-
-
-def last_body(own_ref, other_ref, gb_ref, token, out_ref, sum_ref):
+
+
+def last_body(own_ref, other_ref, token, out_ref):
     token[...] = jnp.zeros_like(token)
-    n = own_ref.shape[0]
-    for j in range(n):
-        out_ref[j] = own_ref[j] + other_ref[j].astype(F32)
-    sum_riders(n, gb_ref, other_ref, sum_ref)
-
-
-def add_body(own_ref, other_ref, out_ref):
-    out_ref[...] = (own_ref[...].astype(F32) + other_ref[...].astype(F32)).astype(out_ref.dtype)
+    out_ref[...] = own_ref[...] + other_ref[...].astype(F32)
+
+
+def combine_riding_body(first, n, coef_ref, own_ref, other_ref, out_ref):
+    bw = coef_ref.shape[0]
+    for s in range(0, bw, CH):
+        c0, c1 = pair(coef_ref, first, s)
+        for k in range(n):
+            r = slice(k * bw + s, k * bw + s + CH)
+            out_ref[r, :] = (c0 * own_ref[r, :].astype(F32) + c1 * other_ref[r, :].astype(F32)).astype(BF16)
+    r = slice(n * bw, out_ref.shape[0])
+    out_ref[r, :] = (own_ref[r, :].astype(F32) + other_ref[r, :].astype(F32)).astype(BF16)
+
+
+def finish_riding_body(n, first, coef_ref, own_ref, other_ref, d_ref, *outs):
+    bw = coef_ref.shape[0]
+    for s in range(0, bw, CH):
+        c0, c1 = pair(coef_ref, first, s)
+        for k in range(n):
+            r = slice(k * bw + s, k * bw + s + CH)
+            outs[k][s : s + CH, :] = (
+                d_ref[k, s : s + CH, :].astype(F32)
+                + c0 * own_ref[r, :].astype(F32)
+                + c1 * other_ref[r, :].astype(F32)
+            ).astype(BF16)
+    r = slice(n * bw, own_ref.shape[0])
+    outs[n][...] = (own_ref[r, :].astype(F32) + other_ref[r, :].astype(F32)).astype(BF16)
+
+
+def join_sum_body(piece_ref, own_ref, other_ref, out_ref):
+    n = piece_ref.shape[0]
+    out_ref[0:n, :] = piece_ref[...]
+    out_ref[n:, :] = (own_ref[...].astype(F32) + other_ref[...].astype(F32)).astype(BF16)
+
+
+def add_last_body(own_ref, other_ref, token, out_ref):
+    token[...] = jnp.zeros_like(token)
+    r = slice(own_ref.shape[0] - out_ref.shape[0], own_ref.shape[0])
+    out_ref[...] = own_ref[r, :].astype(F32) + other_ref[r, :].astype(F32)
 
 
 class Chain:
@@ -311,7 +325,7 @@
         self.last = []
 
     def __call__(self, *args, deps=(), **kwargs):
-        outs = call(*args, deps=[*self.last, *deps], **kwargs)
+        outs = call(*args, deps=[*self.last, *deps], declared=STEP, **kwargs)
         self.last = [jax.tree.leaves(outs)[0]]
         return outs
 
@@ -372,18 +386,21 @@
         return run(copy_body, [shape(*p.shape) for p in pieces], pieces, (), name, deps=deps)
 
     def stack(pieces, name, deps=()):
-        return run(stack_body, shape(nb, bw, rows), [pieces[k] for k in range(nb)], (), name, deps=deps)
+        return run(stack_body, shape(len(pieces), bw, rows), pieces, (), name, deps=deps)
+
+    def beside(u, work):
+        return call(mark_body, shape(8, LANES, dtype=F32), [], (), "mark", [u], declared=work)
 
     def cross(u, flip, name):
-        if name in ():
+        if name in ("fn_level1", "ff_level1", "s_level1", "d_far_level1", "d_near_level1"):
             return send(u, 0, flip, name), u
-        mark = call(mark_body, shape(8, LANES, dtype=F32), [], (), "mark", [u], declared=DECLARED)
+        mark = call(mark_body, shape(8, LANES, dtype=F32), [], (), "mark", [u], declared=11500 * u.size * 2)
         return send(u, 0, flip, name), mark
 
     def open_step(u, name):
         return u, *cross(u, 1, f"{name}_level0")
 
-    def more_steps(opened, first, name):
+    def more_steps(opened, first, name, deps=()):
         u, other, mark = opened
         for l in range(1, n_low):
             u = run(
@@ -392,7 +409,7 @@
                 [coef, u, other],
                 (),
                 f"mix_{name}",
-                deps=[mark],
+                deps=[mark, *deps],
             )
             other, mark = cross(u, 1 << l, f"{name}_level{l}")
         return u, other, mark
@@ -403,8 +420,8 @@
     def spread(pieces, shift, ks, name):
         return {k: send(pieces[k], shift, k * low, f"{name}{k}") for k in ks}
 
-    held = [saved_in[0], prev_grad[0], coeffs[0], weights.T, seq_mix[0]]
-    *fp, saved, upstream, factors, w_t, blocks = run(
+    held = [prev_grad[0], prev_out[0], coeffs[0], weights.T, seq_mix[0]]
+    *sp, upstream, incoming, factors, w_t, blocks = run(
         functools.partial(open_body, nb),
         [shape(bw, rows)] * nb + [shape(*a.shape, dtype=a.dtype) for a in held],
         [at],
@@ -413,40 +430,32 @@
             pltpu.VMEM((width, rows), BF16),
             pltpu.SemaphoreType.DMA((1 + len(held),)),
         ],
-        "pack_f",
-        in_hbm=[prev_out[0], *held],
-    )
-    fr = spread(fp, 1, [*range(1, half), 0, *far], "in_f")
-    sp = pack(saved, "pack_s", [fr[k] for k in range(half)])
+        "pack_s",
+        in_hbm=[saved_in[0], *held],
+    )
     sr = {0: sp[0], **spread(sp, 0, range(1, nb), "in_s")}
+    up = pack(upstream, "pack_u")
+    ur = spread(up, -1, [*reversed(range(half)), *far[:-1]], "in_u")
     coef, w_own, w_own_t = run(
         functools.partial(prep_body, nb, n_low),
         [shape(bw, n_coef, dtype=F32), shape(bw, bw), shape(bw, bw)],
         [at, factors, w_t],
         [pltpu.VMEM((4 * levels, bw), F32), pltpu.VMEM((n_coef, bw), F32)],
         "prep",
-    )
-    f_open = open_step(stack(fr, "stack_f", [sr[k] for k in range(1, half)]), "f")
-    f_all = more_steps(f_open, fwd_low, "f")
-    up = pack(upstream, "pack_u")
-    ur = spread(up, -1, far, "in_u")
-    s_open = open_step(stack(sr, "stack_s"), "s")
-    s_all = more_steps(s_open, fwd_low, "s")
-    u_near = release(up[:half], "release_u")
-    ur.update(spread(u_near, -1, range(half), "in_u"))
+        deps=[sr[1]],
+    )
+    s_open = open_step(stack([sr[k] for k in range(nb)], "stack_s"), "s")
+    fp = pack(incoming, "pack_f")
+    s_all = more_steps(s_open, fwd_low, "s", [ur[k] for k in range(half)])
+    fr = spread(fp, 1, reversed(range(half)), "in_f")
+    ur[nb - 1] = spread({nb - 1: release(up[nb - 1 :], "release_u", [ur[half]])[0]}, -1, [nb - 1], "in_u")[nb - 1]
+    f_far = release(fp[half:], "release_f", [ur[half]])
+    fr.update(spread(dict(zip(far, f_far)), 1, far, "in_f"))
+    near_open = open_step(stack([fr[k] for k in range(half)], "stack_fn"), "fn")
+    fn = more_steps(near_open, fwd_low, "fn")
 
     f_last = fwd_low + 2 * (n_low - 1)
     a_last = adj_low + 2 * (n_low - 1)
-    fo = run(
-        functools.partial(forward_body, nb, f_last, fwd_loc),
-        [shape(bw, rows)] * nb,
-        [coef, blocks, w_own_t, *f_all[:2], *[fr[k] for k in range(nb)]],
-        [pltpu.VMEM((nb, bw, rows), BF16), pltpu.VMEM((bw, nb * rows), BF16)],
-        "layer_f",
-        deps=[f_all[2]],
-    )
-    of = {0: fo[0], **spread(fo, 0, far_first, "out_f")}
-
     v_near, v_far, d, act, gz, u = run(
         functools.partial(backward_body, nb, f_last, fwd_loc, adj_loc),
         [shape(half, bw, rows), shape(nb - half, bw, rows), shape(nb, bw, rows)]
@@ -465,9 +474,8 @@
         "layer_b",
         deps=[s_all[2]],
     )
-    far_open, near_open = open_step(v_far, "d_far"), open_step(v_near, "d_near")
+    far_open = open_step(v_far, "d_far")
     part = bw // low
-    gb_slabs = riders(0, rows, part, bw)[1]
     gw, gb = run(
         functools.partial(grads_body, nb),
         [shape(low, part, bw, dtype=F32), shape(rows, rows)],
@@ -475,62 +483,99 @@
         (),
         "weight_grads",
     )
-    d_far = more_steps(far_open, adj_low, "d_far")
-    d_near = more_steps(near_open, adj_low, "d_near")
-    out_f = unpack(of, "unpack_f")
-    od = {}
-
-    def finish(opened, k0, n):
-        own, other, mark = opened
-        outs = run(
-            functools.partial(finish_body, k0, n, a_last),
-            [shape(bw, rows)] * n,
-            [coef, own, other, d],
-            (),
-            "finish_d",
-            deps=[mark],
-        )
-        for k in reversed(range(n)):
-            od[k0 + k] = send(outs[k], 0, (k0 + k) * low, f"out_d{k0 + k}") if k0 + k else outs[k]
-
-    def sum_b(gb, l):
-        got, mark = cross(gb, 1 << l, f"sum_b{l}")
-        return run(add_body, shape(rows, rows), [gb, got], (), "sum_b", deps=[mark])
-
-    gb = sum_b(gb, n_low)
-    finish(d_far, half, nb - half)
-    for l in range(n_low + 1, levels):
-        gb = sum_b(gb, l)
+    near = run(join_gb_body, shape(half * bw + rows, rows), [v_near, gb], (), "join_near")
+    own, other, mark_n = open_step(near, "d_near")
     keep, give = run(
         first_half_body,
-        [shape(low // 2, part, bw, dtype=F32), shape(low // 2 + gb_slabs, part, bw)],
-        [at, gw, gb],
+        [shape(low // 2, part, bw, dtype=F32), shape(low // 2, part, bw)],
+        [at, gw],
         (),
         "sum_w",
     )
     got, mark = cross(give, 1, "sum_w0")
-    finish(d_near, 0, half)
+    d_far = more_steps(far_open, adj_low, "d_far")
+    for l in range(1, n_low):
+        own = run(
+            functools.partial(combine_riding_body, adj_low + 2 * (l - 1), half),
+            shape(*near.shape),
+            [coef, own, other],
+            (),
+            "mix_d_near",
+            deps=[mark_n],
+        )
+        other, mark_n = cross(own, 1 << l, f"d_near_level{l}")
+    d_near = own, other, mark_n
+    ff = more_steps(open_step(stack([fr[k] for k in far], "stack_ff"), "ff"), fwd_low, "ff", [fn[1]])
+    own, other, ready = d_far
+    outs = run(
+        functools.partial(finish_body, half, nb - half, a_last),
+        [shape(bw, rows)] * (nb - half),
+        [coef, own, other, d],
+        (),
+        "finish_far",
+        deps=[ready],
+    )
+    od = spread(dict(zip(far, outs)), 0, reversed(far), "out_d")
     for l in range(n_low - 1):
         m = low >> l + 2
-        keep, give, gb = run(
+        keep, give = run(
             functools.partial(halve_body, l + 1),
-            [shape(m, part, bw, dtype=F32), shape(m + gb_slabs, part, bw), shape(rows, rows)],
-            [at, keep, got, gb],
-            [pltpu.VMEM((2 * m, part, bw), F32), pltpu.VMEM((rows, rows), F32)],
+            [shape(m, part, bw, dtype=F32), shape(m, part, bw)],
+            [at, keep, got],
+            [pltpu.VMEM((2 * m, part, bw), F32)],
             "sum_w",
             deps=[mark],
         )
         got, mark = cross(give, 2 << l, f"sum_w{l + 1}")
-    _, grad_w, grad_b = run(
+    own, other, ready = d_near
+    outs = run(
+        functools.partial(finish_riding_body, half, a_last),
+        [shape(bw, rows)] * half + [shape(rows, rows)],
+        [coef, own, other, d],
+        (),
+        "finish_near",
+        deps=[ready],
+    )
+    *outs, gb = outs
+    od[0] = outs[0]
+    od.update(spread(dict(enumerate(outs)), 0, range(1, half), "out_d"))
+    got_b, mark_b = cross(gb, low, "sum_b0")
+    fo = run(
+        functools.partial(forward_body, nb, f_last, fwd_loc),
+        [shape(bw, rows)] * nb,
+        [coef, blocks, w_own_t, *fn[:2], *ff[:2], *[fr[k] for k in range(nb)]],
+        [pltpu.VMEM((nb, bw, rows), BF16), pltpu.VMEM((bw, nb * rows), BF16)],
+        "layer_f",
+        deps=[fn[2], ff[2]],
+    )
+    of = {0: fo[0], **spread(fo, 0, [k for k in far_first if k != half], "out_f")}
+    last_piece = run(
+        join_sum_body,
+        shape(bw + rows, rows),
+        [fo[half], gb, got_b],
+        (),
+        "join_f",
+        deps=[mark_b, od[nb - 1]],
+    )
+    of[half] = send(last_piece, 0, half * low, f"out_f{half}")
+    out_d = unpack(od, "unpack_d")
+    _, grad_w = run(
         last_body,
-        [token, shape(1, part, bw, dtype=F32), shape(rows, rows, dtype=F32)],
-        [keep, got, gb],
+        [token, shape(1, part, bw, dtype=F32)],
+        [keep, got],
         (),
         "sum_w",
         deps=[mark],
         out_hbm=True,
     )
-    out_d = unpack(od, "unpack_d")
+    _, out_f, grad_b = run(
+        functools.partial(unpack_last_body, nb),
+        [token, shape(rows, width), shape(rows, rows, dtype=F32)],
+        [at, *[of[k] for k in range(nb)], last_piece],
+        [pltpu.VMEM((width, rows), BF16)],
+        "unpack_f",
+        out_hbm=True,
+    )
     return out_f[None], out_d[None], grad_w, grad_b[None]
 
 

time: 81.7 us -> 79.3 us (0.971)
  starting transfers between devices: 46.3 us -> 38.3 us
  waiting for transfers between devices: 18.7 us -> 24.1 us
    ppermute x29 -> x30, starting transfers between devices: 46.3 us -> 38.3 us  [send_(): return lax.ppermute(x, ('section', 'seq'), pairs)]
    ppermute x29 -> x30, waiting for transfers between devices: 18.7 us -> 24.1 us  [send_(): return lax.ppermute(x, ('section', 'seq'), pairs)]
    pallas_call x35 -> x34, Pallas kernels: 15.6 us -> 15.7 us  [call(): pl.pallas_call(kernel, out_shape=shapes, in_specs=specs, out_specs=jax.tr...]
  transfers between devices with their start and end apart: 29 -> 30, of which waited for: 9 -> 11; matrix products, arithmetic and copies ran while one was open for 0% -> 0% of each run, Pallas kernels for 14% -> 14%
where the time goes in v4:
time: 79.3 us; the launch traced here: 79.1 us
  starting transfers between devices  38.3 us (48%)
  waiting for transfers between devices  24.1 us (30%)
  Pallas kernels  15.7 us (20%)
  between operations  0.96 us (1%)
    ppermute x30, starting transfers between devices, send_(): return lax.ppermute(x, ('section', 'seq'), pairs)  38.3 us
    ppermute x30, waiting for transfers between devices, send_(): return lax.ppermute(x, ('section', 'seq'), pairs)  24.1 us
    pallas_call x34, Pallas kernels, call(): pl.pallas_call(kernel, out_shape=shapes, in_specs=specs, out_specs=jax.tr...  15.7 us
  transfers between devices with their start and end apart: 30, of which 11 were waited for; matrix products, arithmetic and copies ran while one was open for 0% of the time, Pallas kernels for 14%

profile of v4, /device:TPU:0, one launch (start us, length us, event | category | flops | bytes accessed | tf_op | source)
XLA Modules:
  0.0 79.1 jit_solution(11857954857846555530)
XLA Ops:
  0.7 2.5 %pack_s.1 = (bf16[448,128]{1,0:T(8,128)(2,1)S(1)}, bf16[448,128]{1,0:T(8,128)(2,1)S(1)}, bf16[448,128]{1,0:T(8,128)(2,1)S(1)}, bf16[448,128]{1,0:T(8,128)(2,1)S(...) custom-call(s32[5]{0:T(128)S(1)} %stack.23.refs_0_, ...), custom_call_target="tpu_custom_call" | custom-call | flops 200000000 | tf_op jit(solution)/shard_map/pack_s/pallas_call | solution.py:50
  3.2 3.1 %collective-permute-start = (bf16[448,128]{1,0:T(8,128)(2,1)S(1)}, bf16[448,128]{1,0:T(8,128)(2,1)S(1)}, u32[]{:S(2)}, u32[]{:S(2)}) collective-permute-start(bf16[448,128]{1,0:T(8,128)(2,1)S(1)} %get-tuple-element.58), channel_id=1, source_target_pairs={{0,4},{1,5},{2,6},{3,7},{4,0},{5,1},{6,2},{7,3},{8,12},{9,13},{10,... | collective-permute-start | bytes 344072 | tf_op jit(solution)/shard_map/in_s1/ppermute | solution.py:359
  6.3 2.6 %collective-permute-start.1 = (bf16[448,128]{1,0:T(8,128)(2,1)S(1)}, bf16[448,128]{1,0:T(8,128)(2,1)S(1)}, u32[]{:S(2)}, u32[]{:S(2)}) collective-permute-start(bf16[448,128]{1,0:T(8,128)(2,1)S(1)} %get-tuple-element.63), channel_id=1, source_target_pairs={{0,8},{1,9},{2,10},{3,11},{4,12},{5,13},{6,14},{7,15},{8,0},{9,1},... | collective-permute-start | bytes 344072 | tf_op jit(solution)/shard_map/in_s2/ppermute | solution.py:359
  9.6 1.8 %collective-permute-start.6 = (bf16[448,128]{1,0:T(8,128)(2,1)S(1)}, bf16[448,128]{1,0:T(8,128)(2,1)S(1)}, u32[]{:S(2)}, u32[]{:S(2)}) collective-permute-start(bf16[448,128]{1,0:T(8,128)(2,1)S(1)} %get-tuple-element.57.refs_3_), channel_id=1, source_target_pairs={{0,16},{1,17},{2,18},{3,19},{4,20},{5,21},{6,22},{7,23},{8,24},{9,... | collective-permute-start | bytes 344072 | tf_op jit(solution)/shard_map/in_u0/ppermute | solution.py:359
  13.0 5.0 %collective-permute-done.1.refs_2_.refs_8_ = bf16[448,128]{1,0:T(8,128)(2,1)S(1)} collective-permute-done((bf16[448,128]{1,0:T(8,128)(2,1)S(1)}, bf16[448,128]{1,0:T(8,128)(2,1)S(1)}, u32[]{:S(2)}, u32[]{:S(2)}) %collective-permute-start.1) | collective-permute-done | bytes 114720 | tf_op jit(solution)/shard_map/in_s2/ppermute | solution.py:359
  20.2 1.6 %collective-permute-start.13 = (bf16[4,448,128]{2,1,0:T(8,128)(2,1)S(1)}, bf16[4,448,128]{2,1,0:T(8,128)(2,1)S(1)}, u32[]{:S(2)}, u32[]{:S(2)}) collective-permute-start(bf16[4,448,128]{2,1,0:T(8,128)(2,1)S(1)} %mix_s.1.refs_1_.refs_4_.refs_15_), channel_id=1, source_target_pairs={{0,2},{1,3},{2,0},{3,1},{4,6},{5,7},{6,4},{7,5},{8,10},{9,11},{10,... | collective-permute-start | bytes 1376264 | tf_op jit(solution)/shard_map/s_level1/ppermute | solution.py:359
  21.8 3.7 %collective-permute-start.8 = (bf16[448,128]{1,0:T(8,128)(2,1)S(1)}, bf16[448,128]{1,0:T(8,128)(2,1)S(1)}, u32[]{:S(2)}, u32[]{:S(2)}) collective-permute-start(bf16[448,128]{1,0:T(8,128)(2,1)S(1)} %get-tuple-element.71), channel_id=1, source_target_pairs={{0,24},{1,25},{2,26},{3,27},{4,28},{5,29},{6,30},{7,31},{8,16},{9,... | collective-permute-start | bytes 344072 | tf_op jit(solution)/shard_map/in_u2/ppermute | solution.py:359
  27.2 4.1 %collective-permute-done.8.refs_2_.refs_3_.refs_12_ = bf16[448,128]{1,0:T(8,128)(2,1)S(1)} collective-permute-done((bf16[448,128]{1,0:T(8,128)(2,1)S(1)}, bf16[448,128]{1,0:T(8,128)(2,1)S(1)}, u32[]{:S(2)}, u32[]{:S(2)}) %collective-permute-start.8) | collective-permute-done | bytes 114720 | tf_op jit(solution)/shard_map/in_u2/ppermute | solution.py:359
  31.3 3.3 %collective-permute-start.14 = (bf16[448,128]{1,0:T(8,128)(2,1)S(1)}, bf16[448,128]{1,0:T(8,128)(2,1)S(1)}, u32[]{:S(2)}, u32[]{:S(2)}) collective-permute-start(bf16[448,128]{1,0:T(8,128)(2,1)S(1)} %release_u.1.refs_2_), channel_id=1, source_target_pairs={{0,28},{1,29},{2,30},{3,31},{4,24},{5,25},{6,26},{7,27},{8,20},{9,... | collective-permute-start | bytes 344072 | tf_op jit(solution)/shard_map/in_u3/ppermute | solution.py:359
  34.7 2.0 %collective-permute-start.11 = (bf16[448,128]{1,0:T(8,128)(2,1)S(1)}, bf16[448,128]{1,0:T(8,128)(2,1)S(1)}, u32[]{:S(2)}, u32[]{:S(2)}) collective-permute-start(bf16[448,128]{1,0:T(8,128)(2,1)S(1)} %get-tuple-element.72.refs_2_), channel_id=1, source_target_pairs={{0,24},{1,25},{2,26},{3,27},{4,28},{5,29},{6,30},{7,31},{8,16},{9,... | collective-permute-start | bytes 344072 | tf_op jit(solution)/shard_map/in_f2/ppermute | solution.py:359
  36.7 3.2 %collective-permute-start.12 = (bf16[448,128]{1,0:T(8,128)(2,1)S(1)}, bf16[448,128]{1,0:T(8,128)(2,1)S(1)}, u32[]{:S(2)}, u32[]{:S(2)}) collective-permute-start(bf16[448,128]{1,0:T(8,128)(2,1)S(1)} %get-tuple-element.73), channel_id=1, source_target_pairs={{0,28},{1,29},{2,30},{3,31},{4,24},{5,25},{6,26},{7,27},{8,20},{9,... | collective-permute-start | bytes 344072 | tf_op jit(solution)/shard_map/in_f3/ppermute | solution.py:359
  40.8 2.1 %layer_b.1 = (bf16[2,448,128]{2,1,0:T(8,128)(2,1)S(1)}, bf16[2,448,128]{2,1,0:T(8,128)(2,1)S(1)}, bf16[4,448,128]{2,1,0:T(8,128)(2,1)S(1)}, bf16[448,512]{1,0:T(...) custom-call(f32[448,24]{1,0:T(8,128)S(1)} %get-tuple-element.59.refs_4_.refs_0_, ...), custom_call_target="tpu_custom_call" | custom-call | flops 200000000 | tf_op jit(solution)/shard_map/layer_b/pallas_call | solution.py:50
  45.8 1.6 %collective-permute-start.21 = (bf16[2,448,128]{2,1,0:T(8,128)(2,1)S(1)}, bf16[2,448,128]{2,1,0:T(8,128)(2,1)S(1)}, u32[]{:S(2)}, u32[]{:S(2)}) collective-permute-start(bf16[2,448,128]{2,1,0:T(8,128)(2,1)S(1)} %mix_d_far.1.refs_3_.refs_1_.refs_5_), channel_id=1, source_target_pairs={{0,2},{1,3},{2,0},{3,1},{4,6},{5,7},{6,4},{7,5},{8,10},{9,11},{10,... | collective-permute-start | bytes 688136 | tf_op jit(solution)/shard_map/d_far_level1/ppermute | solution.py:359
  50.0 1.6 %collective-permute-start.18 = (bf16[2,448,128]{2,1,0:T(8,128)(2,1)S(1)}, bf16[2,448,128]{2,1,0:T(8,128)(2,1)S(1)}, u32[]{:S(2)}, u32[]{:S(2)}) collective-permute-start(bf16[2,448,128]{2,1,0:T(8,128)(2,1)S(1)} %mix_ff.1.refs_4_.refs_5_.refs_13_), channel_id=1, source_target_pairs={{0,2},{1,3},{2,0},{3,1},{4,6},{5,7},{6,4},{7,5},{8,10},{9,11},{10,... | collective-permute-start | bytes 688136 | tf_op jit(solution)/shard_map/ff_level1/ppermute | solution.py:359
  51.6 2.7 %collective-permute-done.21.refs_2_ = bf16[2,448,128]{2,1,0:T(8,128)(2,1)S(1)} collective-permute-done((bf16[2,448,128]{2,1,0:T(8,128)(2,1)S(1)}, bf16[2,448,128]{2,1,0:T(8,128)(2,1)S(1)}, u32[]{:S(2)}, u32[]{:S(2)}) %collective-permute-start.21) | collective-permute-done | bytes 229408 | tf_op jit(solution)/shard_map/d_far_level1/ppermute | solution.py:359
  56.5 3.3 %collective-permute-done.19.refs_2_ = bf16[1024,128]{1,0:T(8,128)(2,1)S(1)} collective-permute-done((bf16[1024,128]{1,0:T(8,128)(2,1)S(1)}, bf16[1024,128]{1,0:T(8,128)(2,1)S(1)}, u32[]{:S(2)}, u32[]{:S(2)}) %collective-permute-start.19) | collective-permute-done | bytes 262176 | tf_op jit(solution)/shard_map/d_near_level1/ppermute | solution.py:359
  60.2 2.0 %collective-permute-start.28 = (bf16[448,128]{1,0:T(8,128)(2,1)S(1)}, bf16[448,128]{1,0:T(8,128)(2,1)S(1)}, u32[]{:S(2)}, u32[]{:S(2)}) collective-permute-start(bf16[448,128]{1,0:T(8,128)(2,1)S(1)} %get-tuple-element.95), channel_id=1, source_target_pairs={{0,4},{1,5},{2,6},{3,7},{4,0},{5,1},{6,2},{7,3},{8,12},{9,13},{10,... | collective-permute-start | bytes 344072 | tf_op jit(solution)/shard_map/out_d1/ppermute | solution.py:359
  62.2 2.0 %collective-permute-done.18.refs_6_ = bf16[2,448,128]{2,1,0:T(8,128)(2,1)S(1)} collective-permute-done((bf16[2,448,128]{2,1,0:T(8,128)(2,1)S(1)}, bf16[2,448,128]{2,1,0:T(8,128)(2,1)S(1)}, u32[]{:S(2)}, u32[]{:S(2)}) %collective-permute-start.18) | collective-permute-done | bytes 229408 | tf_op jit(solution)/shard_map/ff_level1/ppermute | solution.py:359
  66.2 1.6 %collective-permute-start.27 = (bf16[1,112,448]{2,1,0:T(8,128)(2,1)S(1)}, bf16[1,112,448]{2,1,0:T(8,128)(2,1)S(1)}, u32[]{:S(2)}, u32[]{:S(2)}) collective-permute-start(bf16[1,112,448]{2,1,0:T(8,128)(2,1)S(1)} %get-tuple-element.94.refs_0_), channel_id=1, source_target_pairs={{0,2},{1,3},{2,0},{3,1},{4,6},{5,7},{6,4},{7,5},{8,10},{9,11},{10,... | collective-permute-start | bytes 301064 | tf_op jit(solution)/shard_map/sum_w1/ppermute | solution.py:359
  67.8 1.8 %collective-permute-start.22 = (bf16[448,128]{1,0:T(8,128)(2,1)S(1)}, bf16[448,128]{1,0:T(8,128)(2,1)S(1)}, u32[]{:S(2)}, u32[]{:S(2)}) collective-permute-start(bf16[448,128]{1,0:T(8,128)(2,1)S(1)} %get-tuple-element.89), channel_id=1, source_target_pairs={{0,4},{1,5},{2,6},{3,7},{4,0},{5,1},{6,2},{7,3},{8,12},{9,13},{10,... | collective-permute-start | bytes 344072 | tf_op jit(solution)/shard_map/out_f1/ppermute | solution.py:359
  69.6 2.5 %collective-permute-start.26 = (bf16[448,128]{1,0:T(8,128)(2,1)S(1)}, bf16[448,128]{1,0:T(8,128)(2,1)S(1)}, u32[]{:S(2)}, u32[]{:S(2)}) collective-permute-start(bf16[448,128]{1,0:T(8,128)(2,1)S(1)} %get-tuple-element.93), channel_id=1, source_target_pairs={{0,12},{1,13},{2,14},{3,15},{4,8},{5,9},{6,10},{7,11},{8,4},{9,5},... | collective-permute-start | bytes 344072 | tf_op jit(solution)/shard_map/out_f3/ppermute | solution.py:359
  72.1 1.5 %unpack_d.1 = (f32[8,128]{1,0:T(8,128)S(1)}, bf16[128,1792]{1,0:T(8,128)(2,1)}) custom-call(s32[5]{0:T(128)S(1)} %stack.23.refs_0_, bf16[448,128]{1,0:T(8,128)(2,1)S(1)} %get-tuple-element.87.refs_11_.refs_1_, bf16[448,128]{1,0:T(8,128)(2,1)S(1)} %collective-permute-done.28.refs_2_, bf16[448,128]{1,0:T(8,128)(2,1)S(1)} %collective-permute-done.29.refs_3_, ...), custom_call_target="tpu_custom_call" | custom-call | flops 200000000 | tf_op jit(solution)/shard_map/unpack_d/pallas_call | solution.py:50
  74.3 3.3 %collective-permute-done.22.refs_2_ = bf16[448,128]{1,0:T(8,128)(2,1)S(1)} collective-permute-done((bf16[448,128]{1,0:T(8,128)(2,1)S(1)}, bf16[448,128]{1,0:T(8,128)(2,1)S(1)}, u32[]{:S(2)}, u32[]{:S(2)}) %collective-permute-start.22) | collective-permute-done | bytes 114720 | tf_op jit(solution)/shard_map/out_f1/ppermute | solution.py:359
  77.6 1.5 %unpack_f.1 = (f32[8,128]{1,0:T(8,128)}, bf16[128,1792]{1,0:T(8,128)(2,1)}, f32[128,128]{1,0:T(8,128)}) custom-call(s32[5]{0:T(128)S(1)} %stack.23.refs_0_, bf16[448,128]{1,0:T(8,128)(2,1)S(1)} %get-tuple-element.88.refs_3_.refs_1_, bf16[448,128]{1,0:T(8,128)(2,1)S(1)} %collective-permute-done.22.refs_2_, ...), custom_call_target="tpu_custom_call" | custom-call | flops 200000000 | tf_op jit(solution)/shard_map/unpack_f/pallas_call | solution.py:50
  (71 shorter events, 17.7 us)
Async XLA Ops:
  3.2 8.9 %collective-permute-start = (bf16[448,128]{1,0:T(8,128)(2,1)S(1)}, bf16[448,128]{1,0:T(8,128)(2,1)S(1)}, u32[]{:S(2)}, u32[]{:S(2)}) collective-permute-start(bf16[448,128]{1,0:T(8,128)(2,1)S(1)} %get-tuple-element.58), channel_id=1, source_target_pairs={{0,4},{1,5},{2,6},{3,7},{4,0},{5,1},{6,2},{7,3},{8,12},{9,13},{10,... | collective-permute-start | bytes 344072 | tf_op jit(solution)/shard_map/in_s1/ppermute | solution.py:359
  6.3 11.7 %collective-permute-start.1 = (bf16[448,128]{1,0:T(8,128)(2,1)S(1)}, bf16[448,128]{1,0:T(8,128)(2,1)S(1)}, u32[]{:S(2)}, u32[]{:S(2)}) collective-permute-start(bf16[448,128]{1,0:T(8,128)(2,1)S(1)} %get-tuple-element.63), channel_id=1, source_target_pairs={{0,8},{1,9},{2,10},{3,11},{4,12},{5,13},{6,14},{7,15},{8,0},{9,1},... | collective-permute-start | bytes 344072 | tf_op jit(solution)/shard_map/in_s2/ppermute | solution.py:359
  8.9 9.1 %collective-permute-start.2 = (bf16[448,128]{1,0:T(8,128)(2,1)S(1)}, bf16[448,128]{1,0:T(8,128)(2,1)S(1)}, u32[]{:S(2)}, u32[]{:S(2)}) collective-permute-start(bf16[448,128]{1,0:T(8,128)(2,1)S(1)} %get-tuple-element.64), channel_id=1, source_target_pairs={{0,12},{1,13},{2,14},{3,15},{4,8},{5,9},{6,10},{7,11},{8,4},{9,5},... | collective-permute-start | bytes 344072 | tf_op jit(solution)/shard_map/in_s3/ppermute | solution.py:359
  9.6 9.2 %collective-permute-start.6 = (bf16[448,128]{1,0:T(8,128)(2,1)S(1)}, bf16[448,128]{1,0:T(8,128)(2,1)S(1)}, u32[]{:S(2)}, u32[]{:S(2)}) collective-permute-start(bf16[448,128]{1,0:T(8,128)(2,1)S(1)} %get-tuple-element.57.refs_3_), channel_id=1, source_target_pairs={{0,16},{1,17},{2,18},{3,19},{4,20},{5,21},{6,22},{7,23},{8,24},{9,... | collective-permute-start | bytes 344072 | tf_op jit(solution)/shard_map/in_u0/ppermute | solution.py:359
  11.4 7.9 %collective-permute-start.7 = (bf16[448,128]{1,0:T(8,128)(2,1)S(1)}, bf16[448,128]{1,0:T(8,128)(2,1)S(1)}, u32[]{:S(2)}, u32[]{:S(2)}) collective-permute-start(bf16[448,128]{1,0:T(8,128)(2,1)S(1)} %get-tuple-element.70), channel_id=1, source_target_pairs={{0,20},{1,21},{2,22},{3,23},{4,16},{5,17},{6,18},{7,19},{8,28},{9,... | collective-permute-start | bytes 344072 | tf_op jit(solution)/shard_map/in_u1/ppermute | solution.py:359
  20.2 20.6 %collective-permute-start.13 = (bf16[4,448,128]{2,1,0:T(8,128)(2,1)S(1)}, bf16[4,448,128]{2,1,0:T(8,128)(2,1)S(1)}, u32[]{:S(2)}, u32[]{:S(2)}) collective-permute-start(bf16[4,448,128]{2,1,0:T(8,128)(2,1)S(1)} %mix_s.1.refs_1_.refs_4_.refs_15_), channel_id=1, source_target_pairs={{0,2},{1,3},{2,0},{3,1},{4,6},{5,7},{6,4},{7,5},{8,10},{9,11},{10,... | collective-permute-start | bytes 1376264 | tf_op jit(solution)/shard_map/s_level1/ppermute | solution.py:359
  21.8 9.5 %collective-permute-start.8 = (bf16[448,128]{1,0:T(8,128)(2,1)S(1)}, bf16[448,128]{1,0:T(8,128)(2,1)S(1)}, u32[]{:S(2)}, u32[]{:S(2)}) collective-permute-start(bf16[448,128]{1,0:T(8,128)(2,1)S(1)} %get-tuple-element.71), channel_id=1, source_target_pairs={{0,24},{1,25},{2,26},{3,27},{4,28},{5,29},{6,30},{7,31},{8,16},{9,... | collective-permute-start | bytes 344072 | tf_op jit(solution)/shard_map/in_u2/ppermute | solution.py:359
  25.5 9.1 %collective-permute-start.3 = (bf16[448,128]{1,0:T(8,128)(2,1)S(1)}, bf16[448,128]{1,0:T(8,128)(2,1)S(1)}, u32[]{:S(2)}, u32[]{:S(2)}) collective-permute-start(bf16[448,128]{1,0:T(8,128)(2,1)S(1)} %get-tuple-element.65.refs_3_), channel_id=1, source_target_pairs={{0,16},{1,17},{2,18},{3,19},{4,20},{5,21},{6,22},{7,23},{8,24},{9,... | collective-permute-start | bytes 344072 | tf_op jit(solution)/shard_map/in_f0/ppermute | solution.py:359
  26.0 8.6 %collective-permute-start.4 = (bf16[448,128]{1,0:T(8,128)(2,1)S(1)}, bf16[448,128]{1,0:T(8,128)(2,1)S(1)}, u32[]{:S(2)}, u32[]{:S(2)}) collective-permute-start(bf16[448,128]{1,0:T(8,128)(2,1)S(1)} %get-tuple-element.66), channel_id=1, source_target_pairs={{0,20},{1,21},{2,22},{3,23},{4,16},{5,17},{6,18},{7,19},{8,28},{9,... | collective-permute-start | bytes 344072 | tf_op jit(solution)/shard_map/in_f1/ppermute | solution.py:359
  31.3 9.5 %collective-permute-start.14 = (bf16[448,128]{1,0:T(8,128)(2,1)S(1)}, bf16[448,128]{1,0:T(8,128)(2,1)S(1)}, u32[]{:S(2)}, u32[]{:S(2)}) collective-permute-start(bf16[448,128]{1,0:T(8,128)(2,1)S(1)} %release_u.1.refs_2_), channel_id=1, source_target_pairs={{0,28},{1,29},{2,30},{3,31},{4,24},{5,25},{6,26},{7,27},{8,20},{9,... | collective-permute-start | bytes 344072 | tf_op jit(solution)/shard_map/in_u3/ppermute | solution.py:359
  34.7 12.9 %collective-permute-start.11 = (bf16[448,128]{1,0:T(8,128)(2,1)S(1)}, bf16[448,128]{1,0:T(8,128)(2,1)S(1)}, u32[]{:S(2)}, u32[]{:S(2)}) collective-permute-start(bf16[448,128]{1,0:T(8,128)(2,1)S(1)} %get-tuple-element.72.refs_2_), channel_id=1, source_target_pairs={{0,24},{1,25},{2,26},{3,27},{4,28},{5,29},{6,30},{7,31},{8,16},{9,... | collective-permute-start | bytes 344072 | tf_op jit(solution)/shard_map/in_f2/ppermute | solution.py:359
  36.7 11.4 %collective-permute-start.12 = (bf16[448,128]{1,0:T(8,128)(2,1)S(1)}, bf16[448,128]{1,0:T(8,128)(2,1)S(1)}, u32[]{:S(2)}, u32[]{:S(2)}) collective-permute-start(bf16[448,128]{1,0:T(8,128)(2,1)S(1)} %get-tuple-element.73), channel_id=1, source_target_pairs={{0,28},{1,29},{2,30},{3,31},{4,24},{5,25},{6,26},{7,27},{8,20},{9,... | collective-permute-start | bytes 344072 | tf_op jit(solution)/shard_map/in_f3/ppermute | solution.py:359
  40.2 8.1 %collective-permute-start.10 = (bf16[2,448,128]{2,1,0:T(8,128)(2,1)S(1)}, bf16[2,448,128]{2,1,0:T(8,128)(2,1)S(1)}, u32[]{:S(2)}, u32[]{:S(2)}) collective-permute-start(bf16[2,448,128]{2,1,0:T(8,128)(2,1)S(1)} %mix_fn.1.refs_14_.refs_3_.refs_12_), channel_id=1, source_target_pairs={{0,2},{1,3},{2,0},{3,1},{4,6},{5,7},{6,4},{7,5},{8,10},{9,11},{10,... | collective-permute-start | bytes 688136 | tf_op jit(solution)/shard_map/fn_level1/ppermute | solution.py:359
  45.4 10.5 %collective-permute-start.20 = (bf16[2,112,448]{2,1,0:T(8,128)(2,1)S(1)}, bf16[2,112,448]{2,1,0:T(8,128)(2,1)S(1)}, u32[]{:S(2)}, u32[]{:S(2)}) collective-permute-start(bf16[2,112,448]{2,1,0:T(8,128)(2,1)S(1)} %get-tuple-element.84.refs_0_), channel_id=1, source_target_pairs={{0,1},{1,0},{2,3},{3,2},{4,5},{5,4},{6,7},{7,6},{8,9},{9,8},{10,11... | collective-permute-start | bytes 602120 | tf_op jit(solution)/shard_map/sum_w0/ppermute | solution.py:359
  45.8 8.5 %collective-permute-start.21 = (bf16[2,448,128]{2,1,0:T(8,128)(2,1)S(1)}, bf16[2,448,128]{2,1,0:T(8,128)(2,1)S(1)}, u32[]{:S(2)}, u32[]{:S(2)}) collective-permute-start(bf16[2,448,128]{2,1,0:T(8,128)(2,1)S(1)} %mix_d_far.1.refs_3_.refs_1_.refs_5_), channel_id=1, source_target_pairs={{0,2},{1,3},{2,0},{3,1},{4,6},{5,7},{6,4},{7,5},{8,10},{9,11},{10,... | collective-permute-start | bytes 688136 | tf_op jit(solution)/shard_map/d_far_level1/ppermute | solution.py:359
  47.6 12.3 %collective-permute-start.19 = (bf16[1024,128]{1,0:T(8,128)(2,1)S(1)}, bf16[1024,128]{1,0:T(8,128)(2,1)S(1)}, u32[]{:S(2)}, u32[]{:S(2)}) collective-permute-start(bf16[1024,128]{1,0:T(8,128)(2,1)S(1)} %mix_d_near.1.refs_2_.refs_1_.refs_5_), channel_id=1, source_target_pairs={{0,2},{1,3},{2,0},{3,1},{4,6},{5,7},{6,4},{7,5},{8,10},{9,11},{10,... | collective-permute-start | bytes 786440 | tf_op jit(solution)/shard_map/d_near_level1/ppermute | solution.py:359
  50.0 14.3 %collective-permute-start.18 = (bf16[2,448,128]{2,1,0:T(8,128)(2,1)S(1)}, bf16[2,448,128]{2,1,0:T(8,128)(2,1)S(1)}, u32[]{:S(2)}, u32[]{:S(2)}) collective-permute-start(bf16[2,448,128]{2,1,0:T(8,128)(2,1)S(1)} %mix_ff.1.refs_4_.refs_5_.refs_13_), channel_id=1, source_target_pairs={{0,2},{1,3},{2,0},{3,1},{4,6},{5,7},{6,4},{7,5},{8,10},{9,11},{10,... | collective-permute-start | bytes 688136 | tf_op jit(solution)/shard_map/ff_level1/ppermute | solution.py:359
  54.5 11.6 %collective-permute-start.24 = (bf16[448,128]{1,0:T(8,128)(2,1)S(1)}, bf16[448,128]{1,0:T(8,128)(2,1)S(1)}, u32[]{:S(2)}, u32[]{:S(2)}) collective-permute-start(bf16[448,128]{1,0:T(8,128)(2,1)S(1)} %get-tuple-element.92), channel_id=1, source_target_pairs={{0,12},{1,13},{2,14},{3,15},{4,8},{5,9},{6,10},{7,11},{8,4},{9,5},... | collective-permute-start | bytes 344072 | tf_op jit(solution)/shard_map/out_d3/ppermute | solution.py:359
  55.9 13.7 %collective-permute-start.29 = (bf16[448,128]{1,0:T(8,128)(2,1)S(1)}, bf16[448,128]{1,0:T(8,128)(2,1)S(1)}, u32[]{:S(2)}, u32[]{:S(2)}) collective-permute-start(bf16[448,128]{1,0:T(8,128)(2,1)S(1)} %get-tuple-element.85.refs_3_), channel_id=1, source_target_pairs={{0,8},{1,9},{2,10},{3,11},{4,12},{5,13},{6,14},{7,15},{8,0},{9,1},... | collective-permute-start | bytes 344072 | tf_op jit(solution)/shard_map/out_d2/ppermute | solution.py:359
  60.2 11.9 %collective-permute-start.28 = (bf16[448,128]{1,0:T(8,128)(2,1)S(1)}, bf16[448,128]{1,0:T(8,128)(2,1)S(1)}, u32[]{:S(2)}, u32[]{:S(2)}) collective-permute-start(bf16[448,128]{1,0:T(8,128)(2,1)S(1)} %get-tuple-element.95), channel_id=1, source_target_pairs={{0,4},{1,5},{2,6},{3,7},{4,0},{5,1},{6,2},{7,3},{8,12},{9,13},{10,... | collective-permute-start | bytes 344072 | tf_op jit(solution)/shard_map/out_d1/ppermute | solution.py:359
  66.1 11.5 %collective-permute-start.25 = (bf16[576,128]{1,0:T(8,128)(2,1)S(1)}, bf16[576,128]{1,0:T(8,128)(2,1)S(1)}, u32[]{:S(2)}, u32[]{:S(2)}) collective-permute-start(bf16[576,128]{1,0:T(8,128)(2,1)S(1)} %join_f.1.refs_5_), channel_id=1, source_target_pairs={{0,8},{1,9},{2,10},{3,11},{4,12},{5,13},{6,14},{7,15},{8,0},{9,1},... | collective-permute-start | bytes 442376 | tf_op jit(solution)/shard_map/out_f2/ppermute | solution.py:359
  66.2 7.4 %collective-permute-start.27 = (bf16[1,112,448]{2,1,0:T(8,128)(2,1)S(1)}, bf16[1,112,448]{2,1,0:T(8,128)(2,1)S(1)}, u32[]{:S(2)}, u32[]{:S(2)}) collective-permute-start(bf16[1,112,448]{2,1,0:T(8,128)(2,1)S(1)} %get-tuple-element.94.refs_0_), channel_id=1, source_target_pairs={{0,2},{1,3},{2,0},{3,1},{4,6},{5,7},{6,4},{7,5},{8,10},{9,11},{10,... | collective-permute-start | bytes 301064 | tf_op jit(solution)/shard_map/sum_w1/ppermute | solution.py:359
  67.8 9.8 %collective-permute-start.22 = (bf16[448,128]{1,0:T(8,128)(2,1)S(1)}, bf16[448,128]{1,0:T(8,128)(2,1)S(1)}, u32[]{:S(2)}, u32[]{:S(2)}) collective-permute-start(bf16[448,128]{1,0:T(8,128)(2,1)S(1)} %get-tuple-element.89), channel_id=1, source_target_pairs={{0,4},{1,5},{2,6},{3,7},{4,0},{5,1},{6,2},{7,3},{8,12},{9,13},{10,... | collective-permute-start | bytes 344072 | tf_op jit(solution)/shard_map/out_f1/ppermute | solution.py:359
  69.6 8.0 %collective-permute-start.26 = (bf16[448,128]{1,0:T(8,128)(2,1)S(1)}, bf16[448,128]{1,0:T(8,128)(2,1)S(1)}, u32[]{:S(2)}, u32[]{:S(2)}) collective-permute-start(bf16[448,128]{1,0:T(8,128)(2,1)S(1)} %get-tuple-element.93), channel_id=1, source_target_pairs={{0,12},{1,13},{2,14},{3,15},{4,8},{5,9},{6,10},{7,11},{8,4},{9,5},... | collective-permute-start | bytes 344072 | tf_op jit(solution)/shard_map/out_f3/ppermute | solution.py:359
  (6 other events, 18.8 us)

commit v5 on v4

--- a/solution.py
+++ b/solution.py
@@ -392,7 +392,7 @@
         return call(mark_body, shape(8, LANES, dtype=F32), [], (), "mark", [u], declared=work)
 
     def cross(u, flip, name):
-        if name in ("fn_level1", "ff_level1", "s_level1", "d_far_level1", "d_near_level1"):
+        if name in ("fn_level1", "ff_level1", "s_level1", "d_far_level1", "d_near_level1", "sum_w0"):
             return send(u, 0, flip, name), u
         mark = call(mark_body, shape(8, LANES, dtype=F32), [], (), "mark", [u], declared=11500 * u.size * 2)
         return send(u, 0, flip, name), mark
@@ -420,21 +420,25 @@
     def spread(pieces, shift, ks, name):
         return {k: send(pieces[k], shift, k * low, f"{name}{k}") for k in ks}
 
-    held = [prev_grad[0], prev_out[0], coeffs[0], weights.T, seq_mix[0]]
-    *sp, upstream, incoming, factors, w_t, blocks = run(
-        functools.partial(open_body, nb),
-        [shape(bw, rows)] * nb + [shape(*a.shape, dtype=a.dtype) for a in held],
-        [at],
-        [
-            pltpu.VMEM((rows, width), BF16),
-            pltpu.VMEM((width, rows), BF16),
-            pltpu.SemaphoreType.DMA((1 + len(held),)),
-        ],
-        "pack_s",
-        in_hbm=[saved_in[0], *held],
-    )
+    def fetch(x, held, name):
+        return run(
+            functools.partial(open_body, nb),
+            [shape(bw, rows)] * nb + [shape(*a.shape, dtype=a.dtype) for a in held],
+            [at],
+            [
+                pltpu.VMEM((rows, width), BF16),
+                pltpu.VMEM((width, rows), BF16),
+                pltpu.SemaphoreType.DMA((1 + len(held),)),
+            ],
+            name,
+            in_hbm=[x, *held],
+        )
+
+    sp = fetch(saved_in[0], [], "pack_s")
     sr = {0: sp[0], **spread(sp, 0, range(1, nb), "in_s")}
-    up = pack(upstream, "pack_u")
+    *up, incoming, factors, w_t, blocks = fetch(
+        prev_grad[0], [prev_out[0], coeffs[0], weights.T, seq_mix[0]], "pack_u"
+    )
     ur = spread(up, -1, [*reversed(range(half)), *far[:-1]], "in_u")
     coef, w_own, w_own_t = run(
         functools.partial(prep_body, nb, n_low),
@@ -449,7 +453,7 @@
     s_all = more_steps(s_open, fwd_low, "s", [ur[k] for k in range(half)])
     fr = spread(fp, 1, reversed(range(half)), "in_f")
     ur[nb - 1] = spread({nb - 1: release(up[nb - 1 :], "release_u", [ur[half]])[0]}, -1, [nb - 1], "in_u")[nb - 1]
-    f_far = release(fp[half:], "release_f", [ur[half]])
+    f_far = release(fp[half:], "release_f", [ur[nb - 1]])
     fr.update(spread(dict(zip(far, f_far)), 1, far, "in_f"))
     near_open = open_step(stack([fr[k] for k in range(half)], "stack_fn"), "fn")
     fn = more_steps(near_open, fwd_low, "fn")

time: 79.3 us -> 79.1 us (level)
  waiting for transfers between devices: 24.1 us -> 18.8 us
  starting transfers between devices: 38.3 us -> 42.5 us
  Pallas kernels: 15.7 us -> 16.5 us
    ppermute x30, waiting for transfers between devices: 24.1 us -> 18.8 us  [send_(): return lax.ppermute(x, ('section', 'seq'), pairs)]
    ppermute x30, starting transfers between devices: 38.3 us -> 42.5 us  [send_(): return lax.ppermute(x, ('section', 'seq'), pairs)]
    pallas_call x34 -> x33, Pallas kernels: 15.7 us -> 16.5 us  [call(): pl.pallas_call(kernel, out_shape=shapes, in_specs=specs, out_specs=jax.tr...]
  transfers between devices with their start and end apart: 30 -> 30, of which waited for: 11 -> 11; matrix products, arithmetic and copies ran while one was open for 0% -> 0% of each run, Pallas kernels for 14% -> 17%
where the time goes in v5:
time: 79.1 us; the launch traced here: 78.9 us
  starting transfers between devices  42.5 us (54%)
  waiting for transfers between devices  18.8 us (24%)
  Pallas kernels  16.5 us (21%)
  between operations  0.94 us (1%)
    ppermute x30, starting transfers between devices, send_(): return lax.ppermute(x, ('section', 'seq'), pairs)  42.5 us
    ppermute x30, waiting for transfers between devices, send_(): return lax.ppermute(x, ('section', 'seq'), pairs)  18.8 us
    pallas_call x33, Pallas kernels, call(): pl.pallas_call(kernel, out_shape=shapes, in_specs=specs, out_specs=jax.tr...  16.5 us
  transfers between devices with their start and end apart: 30, of which 11 were waited for; matrix products, arithmetic and copies ran while one was open for 0% of the time, Pallas kernels for 17%

profile of v5, /device:TPU:0, one launch (start us, length us, event | category | flops | bytes accessed | tf_op | source)
XLA Modules:
  0.0 78.9 jit_solution(4417685155058998621)
XLA Ops:
  0.7 1.8 %pack_s.1 = (bf16[448,128]{1,0:T(8,128)(2,1)S(1)}, bf16[448,128]{1,0:T(8,128)(2,1)S(1)}, bf16[448,128]{1,0:T(8,128)(2,1)S(1)}, bf16[448,128]{1,0:T(8,128)(2,1)S(1)}) custom-call(s32[5]{0:T(128)S(1)} %stack.23.refs_0_, bf16[128,1792]{1,0:T(8,128)(2,1)} %bitcast.21), custom_call_target="tpu_custom_call" | custom-call | flops 200000000 | tf_op jit(solution)/shard_map/pack_s/pallas_call | solution.py:50
  2.5 3.1 %collective-permute-start = (bf16[448,128]{1,0:T(8,128)(2,1)S(1)}, bf16[448,128]{1,0:T(8,128)(2,1)S(1)}, u32[]{:S(2)}, u32[]{:S(2)}) collective-permute-start(bf16[448,128]{1,0:T(8,128)(2,1)S(1)} %get-tuple-element.56), channel_id=1, source_target_pairs={{0,4},{1,5},{2,6},{3,7},{4,0},{5,1},{6,2},{7,3},{8,12},{9,13},{10,... | collective-permute-start | bytes 344072 | tf_op jit(solution)/shard_map/in_s1/ppermute | solution.py:359
  5.6 2.6 %collective-permute-start.1 = (bf16[448,128]{1,0:T(8,128)(2,1)S(1)}, bf16[448,128]{1,0:T(8,128)(2,1)S(1)}, u32[]{:S(2)}, u32[]{:S(2)}) collective-permute-start(bf16[448,128]{1,0:T(8,128)(2,1)S(1)} %get-tuple-element.61), channel_id=1, source_target_pairs={{0,8},{1,9},{2,10},{3,11},{4,12},{5,13},{6,14},{7,15},{8,0},{9,1},... | collective-permute-start | bytes 344072 | tf_op jit(solution)/shard_map/in_s2/ppermute | solution.py:359
  8.2 2.3 %pack_u.1 = (bf16[448,128]{1,0:T(8,128)(2,1)S(1)}, bf16[448,128]{1,0:T(8,128)(2,1)S(1)}, bf16[448,128]{1,0:T(8,128)(2,1)S(1)}, bf16[448,128]{1,0:T(8,128)(2,1)S(...) custom-call(s32[5]{0:T(128)S(1)} %stack.23.refs_0_, ...), custom_call_target="tpu_custom_call" | custom-call | flops 200000000 | tf_op jit(solution)/shard_map/pack_u/pallas_call | solution.py:50
  10.5 1.8 %collective-permute-start.6 = (bf16[448,128]{1,0:T(8,128)(2,1)S(1)}, bf16[448,128]{1,0:T(8,128)(2,1)S(1)}, u32[]{:S(2)}, u32[]{:S(2)}) collective-permute-start(bf16[448,128]{1,0:T(8,128)(2,1)S(1)} %get-tuple-element.55.refs_3_), channel_id=1, source_target_pairs={{0,16},{1,17},{2,18},{3,19},{4,20},{5,21},{6,22},{7,23},{8,24},{9,... | collective-permute-start | bytes 344072 | tf_op jit(solution)/shard_map/in_u0/ppermute | solution.py:359
  13.0 4.4 %collective-permute-start.8 = (bf16[448,128]{1,0:T(8,128)(2,1)S(1)}, bf16[448,128]{1,0:T(8,128)(2,1)S(1)}, u32[]{:S(2)}, u32[]{:S(2)}) collective-permute-start(bf16[448,128]{1,0:T(8,128)(2,1)S(1)} %get-tuple-element.69), channel_id=1, source_target_pairs={{0,24},{1,25},{2,26},{3,27},{4,28},{5,29},{6,30},{7,31},{8,16},{9,... | collective-permute-start | bytes 344072 | tf_op jit(solution)/shard_map/in_u2/ppermute | solution.py:359
  20.5 1.6 %collective-permute-start.14 = (bf16[4,448,128]{2,1,0:T(8,128)(2,1)S(1)}, bf16[4,448,128]{2,1,0:T(8,128)(2,1)S(1)}, u32[]{:S(2)}, u32[]{:S(2)}) collective-permute-start(bf16[4,448,128]{2,1,0:T(8,128)(2,1)S(1)} %mix_s.1.refs_1_.refs_4_.refs_15_), channel_id=1, source_target_pairs={{0,2},{1,3},{2,0},{3,1},{4,6},{5,7},{6,4},{7,5},{8,10},{9,11},{10,... | collective-permute-start | bytes 1376264 | tf_op jit(solution)/shard_map/s_level1/ppermute | solution.py:359
  22.1 2.3 %collective-permute-done.8.refs_2_.refs_12_ = bf16[448,128]{1,0:T(8,128)(2,1)S(1)} collective-permute-done((bf16[448,128]{1,0:T(8,128)(2,1)S(1)}, bf16[448,128]{1,0:T(8,128)(2,1)S(1)}, u32[]{:S(2)}, u32[]{:S(2)}) %collective-permute-start.8) | collective-permute-done | bytes 114720 | tf_op jit(solution)/shard_map/in_u2/ppermute | solution.py:359
  24.4 2.5 %collective-permute-start.9 = (bf16[448,128]{1,0:T(8,128)(2,1)S(1)}, bf16[448,128]{1,0:T(8,128)(2,1)S(1)}, u32[]{:S(2)}, u32[]{:S(2)}) collective-permute-start(bf16[448,128]{1,0:T(8,128)(2,1)S(1)} %release_u.1.refs_2_), channel_id=1, source_target_pairs={{0,28},{1,29},{2,30},{3,31},{4,24},{5,25},{6,26},{7,27},{8,20},{9,... | collective-permute-start | bytes 344072 | tf_op jit(solution)/shard_map/in_u3/ppermute | solution.py:359
  28.4 2.2 %collective-permute-start.4 = (bf16[448,128]{1,0:T(8,128)(2,1)S(1)}, bf16[448,128]{1,0:T(8,128)(2,1)S(1)}, u32[]{:S(2)}, u32[]{:S(2)}) collective-permute-start(bf16[448,128]{1,0:T(8,128)(2,1)S(1)} %get-tuple-element.64), channel_id=1, source_target_pairs={{0,20},{1,21},{2,22},{3,23},{4,16},{5,17},{6,18},{7,19},{8,28},{9,... | collective-permute-start | bytes 344072 | tf_op jit(solution)/shard_map/in_f1/ppermute | solution.py:359
  30.6 1.6 %collective-permute-done.9.refs_3_.refs_13_ = bf16[448,128]{1,0:T(8,128)(2,1)S(1)} collective-permute-done((bf16[448,128]{1,0:T(8,128)(2,1)S(1)}, bf16[448,128]{1,0:T(8,128)(2,1)S(1)}, u32[]{:S(2)}, u32[]{:S(2)}) %collective-permute-start.9) | collective-permute-done | bytes 114720 | tf_op jit(solution)/shard_map/in_u3/ppermute | solution.py:359
  32.2 5.4 %collective-permute-start.12 = (bf16[448,128]{1,0:T(8,128)(2,1)S(1)}, bf16[448,128]{1,0:T(8,128)(2,1)S(1)}, u32[]{:S(2)}, u32[]{:S(2)}) collective-permute-start(bf16[448,128]{1,0:T(8,128)(2,1)S(1)} %get-tuple-element.70.refs_2_), channel_id=1, source_target_pairs={{0,24},{1,25},{2,26},{3,27},{4,28},{5,29},{6,30},{7,31},{8,16},{9,... | collective-permute-start | bytes 344072 | tf_op jit(solution)/shard_map/in_f2/ppermute | solution.py:359
  39.7 2.1 %layer_b.1 = (bf16[2,448,128]{2,1,0:T(8,128)(2,1)S(1)}, bf16[2,448,128]{2,1,0:T(8,128)(2,1)S(1)}, bf16[4,448,128]{2,1,0:T(8,128)(2,1)S(1)}, bf16[448,512]{1,0:T(...) custom-call(f32[448,24]{1,0:T(8,128)S(1)} %get-tuple-element.57.refs_4_.refs_0_, ...), custom_call_target="tpu_custom_call" | custom-call | flops 200000000 | tf_op jit(solution)/shard_map/layer_b/pallas_call | solution.py:50
  44.7 1.9 %collective-permute-start.21 = (bf16[2,448,128]{2,1,0:T(8,128)(2,1)S(1)}, bf16[2,448,128]{2,1,0:T(8,128)(2,1)S(1)}, u32[]{:S(2)}, u32[]{:S(2)}) collective-permute-start(bf16[2,448,128]{2,1,0:T(8,128)(2,1)S(1)} %mix_d_far.1.refs_3_.refs_1_.refs_5_), channel_id=1, source_target_pairs={{0,2},{1,3},{2,0},{3,1},{4,6},{5,7},{6,4},{7,5},{8,10},{9,11},{10,... | collective-permute-start | bytes 688136 | tf_op jit(solution)/shard_map/d_far_level1/ppermute | solution.py:359
  48.9 1.9 %collective-permute-start.18 = (bf16[2,448,128]{2,1,0:T(8,128)(2,1)S(1)}, bf16[2,448,128]{2,1,0:T(8,128)(2,1)S(1)}, u32[]{:S(2)}, u32[]{:S(2)}) collective-permute-start(bf16[2,448,128]{2,1,0:T(8,128)(2,1)S(1)} %mix_ff.1.refs_4_.refs_5_.refs_13_), channel_id=1, source_target_pairs={{0,2},{1,3},{2,0},{3,1},{4,6},{5,7},{6,4},{7,5},{8,10},{9,11},{10,... | collective-permute-start | bytes 688136 | tf_op jit(solution)/shard_map/ff_level1/ppermute | solution.py:359
  50.8 2.4 %collective-permute-done.21.refs_2_ = bf16[2,448,128]{2,1,0:T(8,128)(2,1)S(1)} collective-permute-done((bf16[2,448,128]{2,1,0:T(8,128)(2,1)S(1)}, bf16[2,448,128]{2,1,0:T(8,128)(2,1)S(1)}, u32[]{:S(2)}, u32[]{:S(2)}) %collective-permute-start.21) | collective-permute-done | bytes 229408 | tf_op jit(solution)/shard_map/d_far_level1/ppermute | solution.py:359
  53.5 2.8 %collective-permute-start.24 = (bf16[448,128]{1,0:T(8,128)(2,1)S(1)}, bf16[448,128]{1,0:T(8,128)(2,1)S(1)}, u32[]{:S(2)}, u32[]{:S(2)}) collective-permute-start(bf16[448,128]{1,0:T(8,128)(2,1)S(1)} %get-tuple-element.90), channel_id=1, source_target_pairs={{0,12},{1,13},{2,14},{3,15},{4,8},{5,9},{6,10},{7,11},{8,4},{9,5},... | collective-permute-start | bytes 344072 | tf_op jit(solution)/shard_map/out_d3/ppermute | solution.py:359
  56.8 2.0 %collective-permute-done.19.refs_2_ = bf16[1024,128]{1,0:T(8,128)(2,1)S(1)} collective-permute-done((bf16[1024,128]{1,0:T(8,128)(2,1)S(1)}, bf16[1024,128]{1,0:T(8,128)(2,1)S(1)}, u32[]{:S(2)}, u32[]{:S(2)}) %collective-permute-start.19) | collective-permute-done | bytes 262176 | tf_op jit(solution)/shard_map/d_near_level1/ppermute | solution.py:359
  61.2 2.1 %collective-permute-done.18.refs_6_ = bf16[2,448,128]{2,1,0:T(8,128)(2,1)S(1)} collective-permute-done((bf16[2,448,128]{2,1,0:T(8,128)(2,1)S(1)}, bf16[2,448,128]{2,1,0:T(8,128)(2,1)S(1)}, u32[]{:S(2)}, u32[]{:S(2)}) %collective-permute-start.18) | collective-permute-done | bytes 229408 | tf_op jit(solution)/shard_map/ff_level1/ppermute | solution.py:359
  64.8 2.3 %collective-permute-start.25 = (bf16[576,128]{1,0:T(8,128)(2,1)S(1)}, bf16[576,128]{1,0:T(8,128)(2,1)S(1)}, u32[]{:S(2)}, u32[]{:S(2)}) collective-permute-start(bf16[576,128]{1,0:T(8,128)(2,1)S(1)} %join_f.1.refs_5_), channel_id=1, source_target_pairs={{0,8},{1,9},{2,10},{3,11},{4,12},{5,13},{6,14},{7,15},{8,0},{9,1},... | collective-permute-start | bytes 442376 | tf_op jit(solution)/shard_map/out_f2/ppermute | solution.py:359
  68.8 2.2 %collective-permute-start.26 = (bf16[448,128]{1,0:T(8,128)(2,1)S(1)}, bf16[448,128]{1,0:T(8,128)(2,1)S(1)}, u32[]{:S(2)}, u32[]{:S(2)}) collective-permute-start(bf16[448,128]{1,0:T(8,128)(2,1)S(1)} %get-tuple-element.91), channel_id=1, source_target_pairs={{0,12},{1,13},{2,14},{3,15},{4,8},{5,9},{6,10},{7,11},{8,4},{9,5},... | collective-permute-start | bytes 344072 | tf_op jit(solution)/shard_map/out_f3/ppermute | solution.py:359
  71.0 1.5 %unpack_d.1 = (f32[8,128]{1,0:T(8,128)S(1)}, bf16[128,1792]{1,0:T(8,128)(2,1)}) custom-call(s32[5]{0:T(128)S(1)} %stack.23.refs_0_, bf16[448,128]{1,0:T(8,128)(2,1)S(1)} %get-tuple-element.85.refs_11_.refs_1_, bf16[448,128]{1,0:T(8,128)(2,1)S(1)} %collective-permute-done.28.refs_2_, bf16[448,128]{1,0:T(8,128)(2,1)S(1)} %collective-permute-done.29.refs_3_, ...), custom_call_target="tpu_custom_call" | custom-call | flops 200000000 | tf_op jit(solution)/shard_map/unpack_d/pallas_call | solution.py:50
  73.2 4.1 %collective-permute-done.22.refs_2_ = bf16[448,128]{1,0:T(8,128)(2,1)S(1)} collective-permute-done((bf16[448,128]{1,0:T(8,128)(2,1)S(1)}, bf16[448,128]{1,0:T(8,128)(2,1)S(1)}, u32[]{:S(2)}, u32[]{:S(2)}) %collective-permute-start.22) | collective-permute-done | bytes 114720 | tf_op jit(solution)/shard_map/out_f1/ppermute | solution.py:359
  77.3 1.5 %unpack_f.1 = (f32[8,128]{1,0:T(8,128)}, bf16[128,1792]{1,0:T(8,128)(2,1)}, f32[128,128]{1,0:T(8,128)}) custom-call(s32[5]{0:T(128)S(1)} %stack.23.refs_0_, bf16[448,128]{1,0:T(8,128)(2,1)S(1)} %get-tuple-element.86.refs_3_.refs_1_, bf16[448,128]{1,0:T(8,128)(2,1)S(1)} %collective-permute-done.22.refs_2_, ...), custom_call_target="tpu_custom_call" | custom-call | flops 200000000 | tf_op jit(solution)/shard_map/unpack_f/pallas_call | solution.py:50
  (70 shorter events, 19.5 us)
Async XLA Ops:
  2.5 10.4 %collective-permute-start = (bf16[448,128]{1,0:T(8,128)(2,1)S(1)}, bf16[448,128]{1,0:T(8,128)(2,1)S(1)}, u32[]{:S(2)}, u32[]{:S(2)}) collective-permute-start(bf16[448,128]{1,0:T(8,128)(2,1)S(1)} %get-tuple-element.56), channel_id=1, source_target_pairs={{0,4},{1,5},{2,6},{3,7},{4,0},{5,1},{6,2},{7,3},{8,12},{9,13},{10,... | collective-permute-start | bytes 344072 | tf_op jit(solution)/shard_map/in_s1/ppermute | solution.py:359
  5.6 12.7 %collective-permute-start.1 = (bf16[448,128]{1,0:T(8,128)(2,1)S(1)}, bf16[448,128]{1,0:T(8,128)(2,1)S(1)}, u32[]{:S(2)}, u32[]{:S(2)}) collective-permute-start(bf16[448,128]{1,0:T(8,128)(2,1)S(1)} %get-tuple-element.61), channel_id=1, source_target_pairs={{0,8},{1,9},{2,10},{3,11},{4,12},{5,13},{6,14},{7,15},{8,0},{9,1},... | collective-permute-start | bytes 344072 | tf_op jit(solution)/shard_map/in_s2/ppermute | solution.py:359
  8.2 10.1 %collective-permute-start.2 = (bf16[448,128]{1,0:T(8,128)(2,1)S(1)}, bf16[448,128]{1,0:T(8,128)(2,1)S(1)}, u32[]{:S(2)}, u32[]{:S(2)}) collective-permute-start(bf16[448,128]{1,0:T(8,128)(2,1)S(1)} %get-tuple-element.62), channel_id=1, source_target_pairs={{0,12},{1,13},{2,14},{3,15},{4,8},{5,9},{6,10},{7,11},{8,4},{9,5},... | collective-permute-start | bytes 344072 | tf_op jit(solution)/shard_map/in_s3/ppermute | solution.py:359
  10.5 8.7 %collective-permute-start.6 = (bf16[448,128]{1,0:T(8,128)(2,1)S(1)}, bf16[448,128]{1,0:T(8,128)(2,1)S(1)}, u32[]{:S(2)}, u32[]{:S(2)}) collective-permute-start(bf16[448,128]{1,0:T(8,128)(2,1)S(1)} %get-tuple-element.55.refs_3_), channel_id=1, source_target_pairs={{0,16},{1,17},{2,18},{3,19},{4,20},{5,21},{6,22},{7,23},{8,24},{9,... | collective-permute-start | bytes 344072 | tf_op jit(solution)/shard_map/in_u0/ppermute | solution.py:359
  12.3 7.7 %collective-permute-start.7 = (bf16[448,128]{1,0:T(8,128)(2,1)S(1)}, bf16[448,128]{1,0:T(8,128)(2,1)S(1)}, u32[]{:S(2)}, u32[]{:S(2)}) collective-permute-start(bf16[448,128]{1,0:T(8,128)(2,1)S(1)} %get-tuple-element.68), channel_id=1, source_target_pairs={{0,20},{1,21},{2,22},{3,23},{4,16},{5,17},{6,18},{7,19},{8,28},{9,... | collective-permute-start | bytes 344072 | tf_op jit(solution)/shard_map/in_u1/ppermute | solution.py:359
  13.0 11.4 %collective-permute-start.8 = (bf16[448,128]{1,0:T(8,128)(2,1)S(1)}, bf16[448,128]{1,0:T(8,128)(2,1)S(1)}, u32[]{:S(2)}, u32[]{:S(2)}) collective-permute-start(bf16[448,128]{1,0:T(8,128)(2,1)S(1)} %get-tuple-element.69), channel_id=1, source_target_pairs={{0,24},{1,25},{2,26},{3,27},{4,28},{5,29},{6,30},{7,31},{8,16},{9,... | collective-permute-start | bytes 344072 | tf_op jit(solution)/shard_map/in_u2/ppermute | solution.py:359
  20.5 19.2 %collective-permute-start.14 = (bf16[4,448,128]{2,1,0:T(8,128)(2,1)S(1)}, bf16[4,448,128]{2,1,0:T(8,128)(2,1)S(1)}, u32[]{:S(2)}, u32[]{:S(2)}) collective-permute-start(bf16[4,448,128]{2,1,0:T(8,128)(2,1)S(1)} %mix_s.1.refs_1_.refs_4_.refs_15_), channel_id=1, source_target_pairs={{0,2},{1,3},{2,0},{3,1},{4,6},{5,7},{6,4},{7,5},{8,10},{9,11},{10,... | collective-permute-start | bytes 1376264 | tf_op jit(solution)/shard_map/s_level1/ppermute | solution.py:359
  24.4 7.8 %collective-permute-start.9 = (bf16[448,128]{1,0:T(8,128)(2,1)S(1)}, bf16[448,128]{1,0:T(8,128)(2,1)S(1)}, u32[]{:S(2)}, u32[]{:S(2)}) collective-permute-start(bf16[448,128]{1,0:T(8,128)(2,1)S(1)} %release_u.1.refs_2_), channel_id=1, source_target_pairs={{0,28},{1,29},{2,30},{3,31},{4,24},{5,25},{6,26},{7,27},{8,20},{9,... | collective-permute-start | bytes 344072 | tf_op jit(solution)/shard_map/in_u3/ppermute | solution.py:359
  26.9 10.8 %collective-permute-start.3 = (bf16[448,128]{1,0:T(8,128)(2,1)S(1)}, bf16[448,128]{1,0:T(8,128)(2,1)S(1)}, u32[]{:S(2)}, u32[]{:S(2)}) collective-permute-start(bf16[448,128]{1,0:T(8,128)(2,1)S(1)} %get-tuple-element.63.refs_3_), channel_id=1, source_target_pairs={{0,16},{1,17},{2,18},{3,19},{4,20},{5,21},{6,22},{7,23},{8,24},{9,... | collective-permute-start | bytes 344072 | tf_op jit(solution)/shard_map/in_f0/ppermute | solution.py:359
  28.4 9.3 %collective-permute-start.4 = (bf16[448,128]{1,0:T(8,128)(2,1)S(1)}, bf16[448,128]{1,0:T(8,128)(2,1)S(1)}, u32[]{:S(2)}, u32[]{:S(2)}) collective-permute-start(bf16[448,128]{1,0:T(8,128)(2,1)S(1)} %get-tuple-element.64), channel_id=1, source_target_pairs={{0,20},{1,21},{2,22},{3,23},{4,16},{5,17},{6,18},{7,19},{8,28},{9,... | collective-permute-start | bytes 344072 | tf_op jit(solution)/shard_map/in_f1/ppermute | solution.py:359
  32.2 14.6 %collective-permute-start.12 = (bf16[448,128]{1,0:T(8,128)(2,1)S(1)}, bf16[448,128]{1,0:T(8,128)(2,1)S(1)}, u32[]{:S(2)}, u32[]{:S(2)}) collective-permute-start(bf16[448,128]{1,0:T(8,128)(2,1)S(1)} %get-tuple-element.70.refs_2_), channel_id=1, source_target_pairs={{0,24},{1,25},{2,26},{3,27},{4,28},{5,29},{6,30},{7,31},{8,16},{9,... | collective-permute-start | bytes 344072 | tf_op jit(solution)/shard_map/in_f2/ppermute | solution.py:359
  37.8 9.4 %collective-permute-start.13 = (bf16[448,128]{1,0:T(8,128)(2,1)S(1)}, bf16[448,128]{1,0:T(8,128)(2,1)S(1)}, u32[]{:S(2)}, u32[]{:S(2)}) collective-permute-start(bf16[448,128]{1,0:T(8,128)(2,1)S(1)} %get-tuple-element.71), channel_id=1, source_target_pairs={{0,28},{1,29},{2,30},{3,31},{4,24},{5,25},{6,26},{7,27},{8,20},{9,... | collective-permute-start | bytes 344072 | tf_op jit(solution)/shard_map/in_f3/ppermute | solution.py:359
  39.5 7.8 %collective-permute-start.11 = (bf16[2,448,128]{2,1,0:T(8,128)(2,1)S(1)}, bf16[2,448,128]{2,1,0:T(8,128)(2,1)S(1)}, u32[]{:S(2)}, u32[]{:S(2)}) collective-permute-start(bf16[2,448,128]{2,1,0:T(8,128)(2,1)S(1)} %mix_fn.1.refs_14_.refs_3_.refs_12_), channel_id=1, source_target_pairs={{0,2},{1,3},{2,0},{3,1},{4,6},{5,7},{6,4},{7,5},{8,10},{9,11},{10,... | collective-permute-start | bytes 688136 | tf_op jit(solution)/shard_map/fn_level1/ppermute | solution.py:359
  44.4 11.9 %collective-permute-start.20 = (bf16[2,112,448]{2,1,0:T(8,128)(2,1)S(1)}, bf16[2,112,448]{2,1,0:T(8,128)(2,1)S(1)}, u32[]{:S(2)}, u32[]{:S(2)}) collective-permute-start(bf16[2,112,448]{2,1,0:T(8,128)(2,1)S(1)} %get-tuple-element.82.refs_4_), channel_id=1, source_target_pairs={{0,1},{1,0},{2,3},{3,2},{4,5},{5,4},{6,7},{7,6},{8,9},{9,8},{10,11... | collective-permute-start | bytes 602120 | tf_op jit(solution)/shard_map/sum_w0/ppermute | solution.py:359
  44.7 8.5 %collective-permute-start.21 = (bf16[2,448,128]{2,1,0:T(8,128)(2,1)S(1)}, bf16[2,448,128]{2,1,0:T(8,128)(2,1)S(1)}, u32[]{:S(2)}, u32[]{:S(2)}) collective-permute-start(bf16[2,448,128]{2,1,0:T(8,128)(2,1)S(1)} %mix_d_far.1.refs_3_.refs_1_.refs_5_), channel_id=1, source_target_pairs={{0,2},{1,3},{2,0},{3,1},{4,6},{5,7},{6,4},{7,5},{8,10},{9,11},{10,... | collective-permute-start | bytes 688136 | tf_op jit(solution)/shard_map/d_far_level1/ppermute | solution.py:359
  46.9 12.0 %collective-permute-start.19 = (bf16[1024,128]{1,0:T(8,128)(2,1)S(1)}, bf16[1024,128]{1,0:T(8,128)(2,1)S(1)}, u32[]{:S(2)}, u32[]{:S(2)}) collective-permute-start(bf16[1024,128]{1,0:T(8,128)(2,1)S(1)} %mix_d_near.1.refs_2_.refs_1_.refs_5_), channel_id=1, source_target_pairs={{0,2},{1,3},{2,0},{3,1},{4,6},{5,7},{6,4},{7,5},{8,10},{9,11},{10,... | collective-permute-start | bytes 786440 | tf_op jit(solution)/shard_map/d_near_level1/ppermute | solution.py:359
  48.9 14.4 %collective-permute-start.18 = (bf16[2,448,128]{2,1,0:T(8,128)(2,1)S(1)}, bf16[2,448,128]{2,1,0:T(8,128)(2,1)S(1)}, u32[]{:S(2)}, u32[]{:S(2)}) collective-permute-start(bf16[2,448,128]{2,1,0:T(8,128)(2,1)S(1)} %mix_ff.1.refs_4_.refs_5_.refs_13_), channel_id=1, source_target_pairs={{0,2},{1,3},{2,0},{3,1},{4,6},{5,7},{6,4},{7,5},{8,10},{9,11},{10,... | collective-permute-start | bytes 688136 | tf_op jit(solution)/shard_map/ff_level1/ppermute | solution.py:359
  53.5 11.3 %collective-permute-start.24 = (bf16[448,128]{1,0:T(8,128)(2,1)S(1)}, bf16[448,128]{1,0:T(8,128)(2,1)S(1)}, u32[]{:S(2)}, u32[]{:S(2)}) collective-permute-start(bf16[448,128]{1,0:T(8,128)(2,1)S(1)} %get-tuple-element.90), channel_id=1, source_target_pairs={{0,12},{1,13},{2,14},{3,15},{4,8},{5,9},{6,10},{7,11},{8,4},{9,5},... | collective-permute-start | bytes 344072 | tf_op jit(solution)/shard_map/out_d3/ppermute | solution.py:359
  56.2 12.6 %collective-permute-start.29 = (bf16[448,128]{1,0:T(8,128)(2,1)S(1)}, bf16[448,128]{1,0:T(8,128)(2,1)S(1)}, u32[]{:S(2)}, u32[]{:S(2)}) collective-permute-start(bf16[448,128]{1,0:T(8,128)(2,1)S(1)} %get-tuple-element.83.refs_3_), channel_id=1, source_target_pairs={{0,8},{1,9},{2,10},{3,11},{4,12},{5,13},{6,14},{7,15},{8,0},{9,1},... | collective-permute-start | bytes 344072 | tf_op jit(solution)/shard_map/out_d2/ppermute | solution.py:359
  59.1 5.7 %collective-permute-start.23 = (bf16[128,128]{1,0:T(8,128)(2,1)S(1)}, bf16[128,128]{1,0:T(8,128)(2,1)S(1)}, u32[]{:S(2)}, u32[]{:S(2)}) collective-permute-start(bf16[128,128]{1,0:T(8,128)(2,1)S(1)} %get-tuple-element.89.refs_0_.refs_1_), channel_id=1, source_target_pairs={{0,4},{1,5},{2,6},{3,7},{4,0},{5,1},{6,2},{7,3},{8,12},{9,13},{10,... | collective-permute-start | bytes 98312 | tf_op jit(solution)/shard_map/sum_b0/ppermute | solution.py:359
  60.2 10.8 %collective-permute-start.28 = (bf16[448,128]{1,0:T(8,128)(2,1)S(1)}, bf16[448,128]{1,0:T(8,128)(2,1)S(1)}, u32[]{:S(2)}, u32[]{:S(2)}) collective-permute-start(bf16[448,128]{1,0:T(8,128)(2,1)S(1)} %get-tuple-element.93), channel_id=1, source_target_pairs={{0,4},{1,5},{2,6},{3,7},{4,0},{5,1},{6,2},{7,3},{8,12},{9,13},{10,... | collective-permute-start | bytes 344072 | tf_op jit(solution)/shard_map/out_d1/ppermute | solution.py:359
  64.8 12.5 %collective-permute-start.25 = (bf16[576,128]{1,0:T(8,128)(2,1)S(1)}, bf16[576,128]{1,0:T(8,128)(2,1)S(1)}, u32[]{:S(2)}, u32[]{:S(2)}) collective-permute-start(bf16[576,128]{1,0:T(8,128)(2,1)S(1)} %join_f.1.refs_5_), channel_id=1, source_target_pairs={{0,8},{1,9},{2,10},{3,11},{4,12},{5,13},{6,14},{7,15},{8,0},{9,1},... | collective-permute-start | bytes 442376 | tf_op jit(solution)/shard_map/out_f2/ppermute | solution.py:359
  67.7 9.7 %collective-permute-start.22 = (bf16[448,128]{1,0:T(8,128)(2,1)S(1)}, bf16[448,128]{1,0:T(8,128)(2,1)S(1)}, u32[]{:S(2)}, u32[]{:S(2)}) collective-permute-start(bf16[448,128]{1,0:T(8,128)(2,1)S(1)} %get-tuple-element.87), channel_id=1, source_target_pairs={{0,4},{1,5},{2,6},{3,7},{4,0},{5,1},{6,2},{7,3},{8,12},{9,13},{10,... | collective-permute-start | bytes 344072 | tf_op jit(solution)/shard_map/out_f1/ppermute | solution.py:359
  68.8 8.5 %collective-permute-start.26 = (bf16[448,128]{1,0:T(8,128)(2,1)S(1)}, bf16[448,128]{1,0:T(8,128)(2,1)S(1)}, u32[]{:S(2)}, u32[]{:S(2)}) collective-permute-start(bf16[448,128]{1,0:T(8,128)(2,1)S(1)} %get-tuple-element.91), channel_id=1, source_target_pairs={{0,12},{1,13},{2,14},{3,15},{4,8},{5,9},{6,10},{7,11},{8,4},{9,5},... | collective-permute-start | bytes 344072 | tf_op jit(solution)/shard_map/out_f3/ppermute | solution.py:359
  (6 other events, 14.5 us)
